TPU v7x, 128 devices: a whole 4x4x4 slice. The times are simulated.
128 devices in a mesh: gx: 16 (over z, y_lo, core), gy: 8 (over y_hi, x).
Axes of the slice: x: 4, y: 4 (y_hi: 2, y_lo: 2; y = y_hi * 2 + y_lo), z: 4, core: 2. Of those that a mesh axis runs over, the one named last changes fastest.
Arguments:
- observed: float32 [16, 32768], P(None, ('gx', 'gy')), may hold values from -24 to 24
- synthetic: float32 [32, 32768], P(None, ('gx', 'gy')), may hold values from -24 to 24
- match_filter: float32 [16, 17], replicated, may hold values from -1.8 to 1.8
- trace_shot: int32 [32768], P(('gx', 'gy')), may hold values from 0 to 15
- trace_owner: int32 [32768, 1], P(('gx', 'gy')), may hold values from 0 to 127; in each aligned block of 256 rows (0 to 255, 256 to 511, ...) at most 4 rows name the same one
- trace_cell: int32 [32768], P(('gx', 'gy')), may hold values from 0 to 262143
- courant: float32 [512, 256, 256], P('gx', 'gy'), may hold values from 0.05 to 0.18
- adjoint_now: float32 [512, 256, 256], P('gx', 'gy'), may hold values from -6 to 6
- adjoint_prev: float32 [512, 256, 256], P('gx', 'gy'), may hold values from -6 to 6
- forward_field: bfloat16 [16, 512, 256, 256], P(None, 'gx', 'gy'), may hold values from -6 to 6
- image_start: float32 [512, 256, 256], P('gx', 'gy'), may hold values from -6 to 6
Outputs:
- adjoint_field: float32 [512, 256, 256], P('gx', 'gy')
- adjoint_before: float32 [512, 256, 256], P('gx', 'gy')
- gradient_image: float32 [512, 256, 256], P('gx', 'gy')
Inputs may be any that keep to these rules, and one draw needn't show every extreme that they name: `trace_owner`: among the rows of one device, no owner appears more than 4 times. `trace_cell`: local cell number (a * 32 + b) * 256 + z of the receiver inside its owner's block.
All inputs are finite; a program needn't handle non-finite values.
Results may differ from a plain program's by a relative error of at most 0.0003.
Values sent between devices are 32-bit elements; how exact they have to be, the bound alone decides.
A program may use at most 128 MiB of HBM per device.

v0:
```python
import jax
import jax.numpy as jnp
from jax import lax
from jax.sharding import PartitionSpec as P

STEPS = 16
SHOTS = 16
TAPS = 17


stencil_weights = (-205.0 / 72.0, 8.0 / 5.0, -1.0 / 5.0, 8.0 / 315.0, -1.0 / 560.0)


def extended(value, sides, width):
    for axis, dim in sides:
        peers, length = (lax.axis_size(axis), value.shape[dim])
        up = [(i, (i + 1) % peers) for i in range(peers - 1)]
        down = [(j, i) for i, j in up]
        last = lax.slice_in_dim(value, length - width, length, axis=dim)
        first = lax.slice_in_dim(value, 0, width, axis=dim)
        before = lax.ppermute(last, axis, up)
        after = lax.ppermute(first, axis, down)
        value = jnp.concatenate([before, value, after], axis=dim)
    return value


def laplace(padded):
    width_x = padded.shape[0] - 8
    width_y = padded.shape[1] - 8
    center = padded[4 : 4 + width_x, 4 : 4 + width_y]
    column = center.shape[2]
    z_padded = jnp.pad(center, ((0, 0), (0, 0), (4, 4)))
    summed = 3.0 * stencil_weights[0] * center
    for offset in range(1, 5):
        along_x = (
            padded[4 + offset : 4 + offset + width_x, 4 : 4 + width_y]
            + padded[4 - offset : 4 - offset + width_x, 4 : 4 + width_y]
        )
        along_y = (
            padded[4 : 4 + width_x, 4 + offset : 4 + offset + width_y]
            + padded[4 : 4 + width_x, 4 - offset : 4 - offset + width_y]
        )
        along_z = (
            z_padded[:, :, 4 + offset : 4 + offset + column]
            + z_padded[:, :, 4 - offset : 4 - offset + column]
        )
        summed = summed + stencil_weights[offset] * (along_x + along_y + along_z)
    return summed


def per_device(
    observed,
    synthetic,
    match_filter,
    trace_shot,
    trace_owner,
    trace_cell,
    courant,
    adjoint_now,
    adjoint_prev,
    forward_field,
    image_start,
):
    trace_rows = observed.shape[1]
    grid_x = lax.axis_size("gx")
    grid_y = lax.axis_size("gy")
    devices = grid_x * grid_y
    capacity = max(2, 2 * trace_rows // devices)
    slot_count = devices * capacity
    shot_match = (trace_shot[:, None] == jnp.arange(SHOTS, dtype=jnp.int32)[None, :]).astype(
        jnp.float32
    )
    filters = jnp.dot(match_filter.T, shot_match.T, precision=lax.Precision.HIGHEST)
    residual = -observed
    for lag_index in range(TAPS):
        residual = (
            residual
            + filters[lag_index][None, :] * synthetic[STEPS - lag_index : 2 * STEPS - lag_index]
        )
    owners = trace_owner[:, 0]
    same_owner = owners[:, None] == owners[None, :]
    row_ids = jnp.arange(trace_rows, dtype=jnp.int32)
    earlier = row_ids[None, :] < row_ids[:, None]
    ranks = jnp.sum((same_owner & earlier).astype(jnp.int32), axis=1)
    slot_index = owners * capacity + ranks
    slot_table = (slot_index[:, None] == jnp.arange(slot_count, dtype=jnp.int32)[None, :]).astype(
        jnp.float32
    )
    payload = jnp.concatenate([residual, trace_cell.astype(jnp.float32)[None, :]], axis=0)
    parcel = jnp.dot(payload, slot_table, precision=lax.Precision.HIGHEST)
    received = lax.all_to_all(parcel, ("gx", "gy"), split_axis=1, concat_axis=1, tiled=True)
    got_values = received[:STEPS]
    got_cells = received[STEPS].astype(jnp.int32)
    own_weights = courant.reshape(-1)[got_cells]

    def inject_own(field, position):
        values_row = lax.dynamic_index_in_dim(got_values, STEPS - 1 - position, 0, keepdims=False)
        return field.reshape(-1).at[got_cells].add(own_weights * values_row).reshape(field.shape)

    def snapshot(position):
        return lax.dynamic_index_in_dim(forward_field, position, 0, keepdims=False).astype(
            jnp.float32
        )

    def advance(position, carry):
        current, before, imaging = carry
        padded = extended(current, (("gx", 0), ("gy", 1)), 4)
        following = 2.0 * current - before + courant * laplace(padded)
        following = inject_own(following, position)
        imaging = imaging + snapshot(position) * following
        return (following, current, imaging)

    current, before, imaging = lax.fori_loop(
        0, STEPS, advance, (adjoint_now, adjoint_prev, image_start)
    )
    return (current, before, imaging)


def solution(mesh):
    return jax.shard_map(
        per_device,
        mesh=mesh,
        in_specs=(
            P(None, ("gx", "gy")),
            P(None, ("gx", "gy")),
            P(),
            P(("gx", "gy")),
            P(("gx", "gy"), None),
            P(("gx", "gy")),
            P("gx", "gy", None),
            P("gx", "gy", None),
            P("gx", "gy", None),
            P(None, "gx", "gy", None),
            P("gx", "gy", None),
        ),
        out_specs=(P("gx", "gy", None), P("gx", "gy", None), P("gx", "gy", None)),
        check_vma=False,
    )
```

profile of v0, /device:TPU:38, one launch (start us, length us, event | category | flops | bytes accessed | tf_op | source)
XLA Modules:
  0.0 593.1 jit_solution(6530571552086648441)
XLA Ops:
  4.9 10.2 %all-to-all-start = ((f32[17,128,4]{0,2,1:T(4,128)}), f32[17,128,4]{0,2,1:T(4,128)S(1)}, u32[]{:S(2)}, u32[]{:S(2)}) async-start(f32[17,128,4]{0,2,1:T(4,128)} %bitcast.26), calls=%async_computation | async-start | bytes 524288 | tf_op jit(solution)/shard_map/all_to_all | solution.py:91
  16.6 7.0 %all-to-all-done = f32[17,128,4]{0,2,1:T(4,128)S(1)} async-done(((f32[17,128,4]{0,2,1:T(4,128)}), f32[17,128,4]{0,2,1:T(4,128)S(1)}, u32[]{:S(2)}, u32[]{:S(2)}) %all-to-all-start) | async-done | bytes 34848 | tf_op jit(solution)/shard_map/all_to_all | solution.py:91
  27.0 7.6 %gather_fusion = f32[512]{0:T(512)} fusion(f32[262144]{0:T(1024)} %bitcast.53, s32[1024]{0:T(1024)S(1)} %pad_clamp_fusion), kind=kCustom, calls=%fused_computation | custom fusion | bytes 6144 | tf_op jit(solution)/shard_map/gather | solution.py:94
  34.6 557.1 %while.19 = (s32[]{:T(128)}, f32[32,32,256]{2,1,0:T(8,128)S(1)}, f32[32,32,256]{2,1,0:T(8,128)S(1)}, f32[32,32,256]{2,1,0:T(8,128)}, f32[32,32,256]{2,1,0:T(8,12...) while((s32[]{:T(128)}, f32[32,32,256]{2,1,0:T(8,128)S(1)}, ...), condition=%wide.region_3.4_spmd, body=%wide.region_1.3_spmd.sunk | while | flops 11536902 | bytes 36919668 | solution.py:113
  35.3 12.0 %collective-permute-start = (f32[4,32,256]{2,1,0:T(8,128)}, f32[4,32,256]{2,1,0:T(8,128)S(1)}, u32[]{:S(2)}, u32[]{:S(2)}) collective-permute-start(f32[4,32,256]{2,1,0:T(8,128)} %get-tuple-element.359), channel_id=1, source_target_pairs={{0,8},{8,16},{16,24},{24,32},{32,40},{40,48},{48,56},{56,64},{64,7... | collective-permute-start | bytes 393224 | tf_op jit(solution)/shard_map/while/body/eval_jaxpr/ppermute | solution.py:21
  59.9 6.3 %collective-permute-done.3 = f32[40,4,256]{2,1,0:T(4,128)S(1)} collective-permute-done((f32[40,4,256]{2,1,0:T(4,128)S(1)}, f32[40,4,256]{2,1,0:T(4,128)S(1)}, u32[]{:S(2)}, u32[]{:S(2)}) %collective-permute-start.3) | collective-permute-done | bytes 163872 | tf_op jit(solution)/shard_map/while/body/eval_jaxpr/ppermute | solution.py:22
  80.9 4.2 collective-permute-start.1
  89.6 3.9 collective-permute-start.3
  94.8 5.5 collective-permute-done.3
  123.8 3.9 collective-permute-start.3
  129.1 5.5 collective-permute-done.3
  158.1 3.9 collective-permute-start.3
  163.4 5.5 collective-permute-done.3
  192.3 3.9 collective-permute-start.3
  197.6 5.5 collective-permute-done.3
  215.6 3.8 collective-permute-start
  226.6 3.9 collective-permute-start.3
  231.9 5.5 collective-permute-done.3
  249.9 3.9 collective-permute-start
  260.8 3.9 collective-permute-start.3
  266.1 5.5 collective-permute-done.3
  284.1 4.0 collective-permute-start
  295.1 3.9 collective-permute-start.3
  300.4 5.5 collective-permute-done.3
  318.4 4.1 collective-permute-start
  329.4 3.9 collective-permute-start.3
  334.6 5.5 collective-permute-done.3
  352.6 4.2 collective-permute-start
  363.6 3.9 collective-permute-start.3
  368.9 5.5 collective-permute-done.3
  386.9 4.3 collective-permute-start
  397.9 3.9 collective-permute-start.3
  403.2 5.5 collective-permute-done.3
  421.1 4.4 collective-permute-start
  432.1 3.9 collective-permute-start.3
  437.4 5.5 collective-permute-done.3
  455.4 4.5 collective-permute-start
  466.4 3.9 collective-permute-start.3
  471.7 5.5 collective-permute-done.3
  489.7 4.5 collective-permute-start
  500.7 3.9 collective-permute-start.3
  505.9 5.6 collective-permute-done.3
  523.9 4.5 collective-permute-start
  534.9 3.9 collective-permute-start.3
  540.2 5.5 collective-permute-done.3
  558.2 4.5 collective-permute-start
  569.2 3.9 collective-permute-start.3
  574.5 5.5 collective-permute-done.3
  (379 shorter events, 354.7 us)
Async XLA Ops:
  4.9 18.7 %all-to-all-start = ((f32[17,128,4]{0,2,1:T(4,128)}), f32[17,128,4]{0,2,1:T(4,128)S(1)}, u32[]{:S(2)}, u32[]{:S(2)}) async-start(f32[17,128,4]{0,2,1:T(4,128)} %bitcast.26), calls=%async_computation | async-start | bytes 524288 | tf_op jit(solution)/shard_map/all_to_all | solution.py:91
  35.3 15.3 %collective-permute-start = (f32[4,32,256]{2,1,0:T(8,128)}, f32[4,32,256]{2,1,0:T(8,128)S(1)}, u32[]{:S(2)}, u32[]{:S(2)}) collective-permute-start(f32[4,32,256]{2,1,0:T(8,128)} %get-tuple-element.359), channel_id=1, source_target_pairs={{0,8},{8,16},{16,24},{24,32},{32,40},{40,48},{48,56},{56,64},{64,7... | collective-permute-start | bytes 393224 | tf_op jit(solution)/shard_map/while/body/eval_jaxpr/ppermute | solution.py:21
  51.8 8.1 %collective-permute-start.2 = (f32[40,4,256]{2,1,0:T(4,128)S(1)}, f32[40,4,256]{2,1,0:T(4,128)S(1)}, u32[]{:S(2)}, u32[]{:S(2)}) collective-permute-start(f32[40,4,256]{2,1,0:T(4,128)S(1)} %get-tuple-element.366), channel_id=1, source_target_pairs={{0,1},{1,2},{2,3},{3,4},{4,5},{5,6},{6,7},{8,9},{9,10},{10,11},{11... | collective-permute-start | bytes 491528 | tf_op jit(solution)/shard_map/while/body/eval_jaxpr/ppermute | solution.py:21
  54.1 12.0 %collective-permute-start.3 = (f32[40,4,256]{2,1,0:T(4,128)S(1)}, f32[40,4,256]{2,1,0:T(4,128)S(1)}, u32[]{:S(2)}, u32[]{:S(2)}) collective-permute-start(f32[40,4,256]{2,1,0:T(4,128)S(1)} %get-tuple-element.367), channel_id=1, source_target_pairs={{1,0},{2,1},{3,2},{4,3},{5,4},{6,5},{7,6},{9,8},{10,9},{11,10},{12... | collective-permute-start | bytes 491528 | tf_op jit(solution)/shard_map/while/body/eval_jaxpr/ppermute | solution.py:22
  78.6 7.9 %collective-permute-start = (f32[4,32,256]{2,1,0:T(8,128)}, f32[4,32,256]{2,1,0:T(8,128)S(1)}, u32[]{:S(2)}, u32[]{:S(2)}) collective-permute-start(f32[4,32,256]{2,1,0:T(8,128)} %get-tuple-element.359), channel_id=1, source_target_pairs={{0,8},{8,16},{16,24},{24,32},{32,40},{40,48},{48,56},{56,64},{64,7... | collective-permute-start | bytes 393224 | tf_op jit(solution)/shard_map/while/body/eval_jaxpr/ppermute | solution.py:21
  87.6 7.2 %collective-permute-start.2 = (f32[40,4,256]{2,1,0:T(4,128)S(1)}, f32[40,4,256]{2,1,0:T(4,128)S(1)}, u32[]{:S(2)}, u32[]{:S(2)}) collective-permute-start(f32[40,4,256]{2,1,0:T(4,128)S(1)} %get-tuple-element.366), channel_id=1, source_target_pairs={{0,1},{1,2},{2,3},{3,4},{4,5},{5,6},{6,7},{8,9},{9,10},{10,11},{11... | collective-permute-start | bytes 491528 | tf_op jit(solution)/shard_map/while/body/eval_jaxpr/ppermute | solution.py:21
  89.6 10.8 %collective-permute-start.3 = (f32[40,4,256]{2,1,0:T(4,128)S(1)}, f32[40,4,256]{2,1,0:T(4,128)S(1)}, u32[]{:S(2)}, u32[]{:S(2)}) collective-permute-start(f32[40,4,256]{2,1,0:T(4,128)S(1)} %get-tuple-element.367), channel_id=1, source_target_pairs={{1,0},{2,1},{3,2},{4,3},{5,4},{6,5},{7,6},{9,8},{10,9},{11,10},{12... | collective-permute-start | bytes 491528 | tf_op jit(solution)/shard_map/while/body/eval_jaxpr/ppermute | solution.py:22
  112.8 7.9 %collective-permute-start = (f32[4,32,256]{2,1,0:T(8,128)}, f32[4,32,256]{2,1,0:T(8,128)S(1)}, u32[]{:S(2)}, u32[]{:S(2)}) collective-permute-start(f32[4,32,256]{2,1,0:T(8,128)} %get-tuple-element.359), channel_id=1, source_target_pairs={{0,8},{8,16},{16,24},{24,32},{32,40},{40,48},{48,56},{56,64},{64,7... | collective-permute-start | bytes 393224 | tf_op jit(solution)/shard_map/while/body/eval_jaxpr/ppermute | solution.py:21
  121.9 7.2 %collective-permute-start.2 = (f32[40,4,256]{2,1,0:T(4,128)S(1)}, f32[40,4,256]{2,1,0:T(4,128)S(1)}, u32[]{:S(2)}, u32[]{:S(2)}) collective-permute-start(f32[40,4,256]{2,1,0:T(4,128)S(1)} %get-tuple-element.366), channel_id=1, source_target_pairs={{0,1},{1,2},{2,3},{3,4},{4,5},{5,6},{6,7},{8,9},{9,10},{10,11},{11... | collective-permute-start | bytes 491528 | tf_op jit(solution)/shard_map/while/body/eval_jaxpr/ppermute | solution.py:21
  123.8 10.8 %collective-permute-start.3 = (f32[40,4,256]{2,1,0:T(4,128)S(1)}, f32[40,4,256]{2,1,0:T(4,128)S(1)}, u32[]{:S(2)}, u32[]{:S(2)}) collective-permute-start(f32[40,4,256]{2,1,0:T(4,128)S(1)} %get-tuple-element.367), channel_id=1, source_target_pairs={{1,0},{2,1},{3,2},{4,3},{5,4},{6,5},{7,6},{9,8},{10,9},{11,10},{12... | collective-permute-start | bytes 491528 | tf_op jit(solution)/shard_map/while/body/eval_jaxpr/ppermute | solution.py:22
  147.1 7.9 %collective-permute-start = (f32[4,32,256]{2,1,0:T(8,128)}, f32[4,32,256]{2,1,0:T(8,128)S(1)}, u32[]{:S(2)}, u32[]{:S(2)}) collective-permute-start(f32[4,32,256]{2,1,0:T(8,128)} %get-tuple-element.359), channel_id=1, source_target_pairs={{0,8},{8,16},{16,24},{24,32},{32,40},{40,48},{48,56},{56,64},{64,7... | collective-permute-start | bytes 393224 | tf_op jit(solution)/shard_map/while/body/eval_jaxpr/ppermute | solution.py:21
  156.1 7.2 %collective-permute-start.2 = (f32[40,4,256]{2,1,0:T(4,128)S(1)}, f32[40,4,256]{2,1,0:T(4,128)S(1)}, u32[]{:S(2)}, u32[]{:S(2)}) collective-permute-start(f32[40,4,256]{2,1,0:T(4,128)S(1)} %get-tuple-element.366), channel_id=1, source_target_pairs={{0,1},{1,2},{2,3},{3,4},{4,5},{5,6},{6,7},{8,9},{9,10},{10,11},{11... | collective-permute-start | bytes 491528 | tf_op jit(solution)/shard_map/while/body/eval_jaxpr/ppermute | solution.py:21
  158.1 10.8 %collective-permute-start.3 = (f32[40,4,256]{2,1,0:T(4,128)S(1)}, f32[40,4,256]{2,1,0:T(4,128)S(1)}, u32[]{:S(2)}, u32[]{:S(2)}) collective-permute-start(f32[40,4,256]{2,1,0:T(4,128)S(1)} %get-tuple-element.367), channel_id=1, source_target_pairs={{1,0},{2,1},{3,2},{4,3},{5,4},{6,5},{7,6},{9,8},{10,9},{11,10},{12... | collective-permute-start | bytes 491528 | tf_op jit(solution)/shard_map/while/body/eval_jaxpr/ppermute | solution.py:22
  181.3 7.9 %collective-permute-start = (f32[4,32,256]{2,1,0:T(8,128)}, f32[4,32,256]{2,1,0:T(8,128)S(1)}, u32[]{:S(2)}, u32[]{:S(2)}) collective-permute-start(f32[4,32,256]{2,1,0:T(8,128)} %get-tuple-element.359), channel_id=1, source_target_pairs={{0,8},{8,16},{16,24},{24,32},{32,40},{40,48},{48,56},{56,64},{64,7... | collective-permute-start | bytes 393224 | tf_op jit(solution)/shard_map/while/body/eval_jaxpr/ppermute | solution.py:21
  190.4 7.2 %collective-permute-start.2 = (f32[40,4,256]{2,1,0:T(4,128)S(1)}, f32[40,4,256]{2,1,0:T(4,128)S(1)}, u32[]{:S(2)}, u32[]{:S(2)}) collective-permute-start(f32[40,4,256]{2,1,0:T(4,128)S(1)} %get-tuple-element.366), channel_id=1, source_target_pairs={{0,1},{1,2},{2,3},{3,4},{4,5},{5,6},{6,7},{8,9},{9,10},{10,11},{11... | collective-permute-start | bytes 491528 | tf_op jit(solution)/shard_map/while/body/eval_jaxpr/ppermute | solution.py:21
  192.3 10.8 %collective-permute-start.3 = (f32[40,4,256]{2,1,0:T(4,128)S(1)}, f32[40,4,256]{2,1,0:T(4,128)S(1)}, u32[]{:S(2)}, u32[]{:S(2)}) collective-permute-start(f32[40,4,256]{2,1,0:T(4,128)S(1)} %get-tuple-element.367), channel_id=1, source_target_pairs={{1,0},{2,1},{3,2},{4,3},{5,4},{6,5},{7,6},{9,8},{10,9},{11,10},{12... | collective-permute-start | bytes 491528 | tf_op jit(solution)/shard_map/while/body/eval_jaxpr/ppermute | solution.py:22
  215.6 7.9 %collective-permute-start = (f32[4,32,256]{2,1,0:T(8,128)}, f32[4,32,256]{2,1,0:T(8,128)S(1)}, u32[]{:S(2)}, u32[]{:S(2)}) collective-permute-start(f32[4,32,256]{2,1,0:T(8,128)} %get-tuple-element.359), channel_id=1, source_target_pairs={{0,8},{8,16},{16,24},{24,32},{32,40},{40,48},{48,56},{56,64},{64,7... | collective-permute-start | bytes 393224 | tf_op jit(solution)/shard_map/while/body/eval_jaxpr/ppermute | solution.py:21
  224.7 7.2 %collective-permute-start.2 = (f32[40,4,256]{2,1,0:T(4,128)S(1)}, f32[40,4,256]{2,1,0:T(4,128)S(1)}, u32[]{:S(2)}, u32[]{:S(2)}) collective-permute-start(f32[40,4,256]{2,1,0:T(4,128)S(1)} %get-tuple-element.366), channel_id=1, source_target_pairs={{0,1},{1,2},{2,3},{3,4},{4,5},{5,6},{6,7},{8,9},{9,10},{10,11},{11... | collective-permute-start | bytes 491528 | tf_op jit(solution)/shard_map/while/body/eval_jaxpr/ppermute | solution.py:21
  226.6 10.8 %collective-permute-start.3 = (f32[40,4,256]{2,1,0:T(4,128)S(1)}, f32[40,4,256]{2,1,0:T(4,128)S(1)}, u32[]{:S(2)}, u32[]{:S(2)}) collective-permute-start(f32[40,4,256]{2,1,0:T(4,128)S(1)} %get-tuple-element.367), channel_id=1, source_target_pairs={{1,0},{2,1},{3,2},{4,3},{5,4},{6,5},{7,6},{9,8},{10,9},{11,10},{12... | collective-permute-start | bytes 491528 | tf_op jit(solution)/shard_map/while/body/eval_jaxpr/ppermute | solution.py:22
  249.9 7.9 %collective-permute-start = (f32[4,32,256]{2,1,0:T(8,128)}, f32[4,32,256]{2,1,0:T(8,128)S(1)}, u32[]{:S(2)}, u32[]{:S(2)}) collective-permute-start(f32[4,32,256]{2,1,0:T(8,128)} %get-tuple-element.359), channel_id=1, source_target_pairs={{0,8},{8,16},{16,24},{24,32},{32,40},{40,48},{48,56},{56,64},{64,7... | collective-permute-start | bytes 393224 | tf_op jit(solution)/shard_map/while/body/eval_jaxpr/ppermute | solution.py:21
  258.9 7.2 %collective-permute-start.2 = (f32[40,4,256]{2,1,0:T(4,128)S(1)}, f32[40,4,256]{2,1,0:T(4,128)S(1)}, u32[]{:S(2)}, u32[]{:S(2)}) collective-permute-start(f32[40,4,256]{2,1,0:T(4,128)S(1)} %get-tuple-element.366), channel_id=1, source_target_pairs={{0,1},{1,2},{2,3},{3,4},{4,5},{5,6},{6,7},{8,9},{9,10},{10,11},{11... | collective-permute-start | bytes 491528 | tf_op jit(solution)/shard_map/while/body/eval_jaxpr/ppermute | solution.py:21
  260.8 10.8 %collective-permute-start.3 = (f32[40,4,256]{2,1,0:T(4,128)S(1)}, f32[40,4,256]{2,1,0:T(4,128)S(1)}, u32[]{:S(2)}, u32[]{:S(2)}) collective-permute-start(f32[40,4,256]{2,1,0:T(4,128)S(1)} %get-tuple-element.367), channel_id=1, source_target_pairs={{1,0},{2,1},{3,2},{4,3},{5,4},{6,5},{7,6},{9,8},{10,9},{11,10},{12... | collective-permute-start | bytes 491528 | tf_op jit(solution)/shard_map/while/body/eval_jaxpr/ppermute | solution.py:22
  284.1 7.9 %collective-permute-start = (f32[4,32,256]{2,1,0:T(8,128)}, f32[4,32,256]{2,1,0:T(8,128)S(1)}, u32[]{:S(2)}, u32[]{:S(2)}) collective-permute-start(f32[4,32,256]{2,1,0:T(8,128)} %get-tuple-element.359), channel_id=1, source_target_pairs={{0,8},{8,16},{16,24},{24,32},{32,40},{40,48},{48,56},{56,64},{64,7... | collective-permute-start | bytes 393224 | tf_op jit(solution)/shard_map/while/body/eval_jaxpr/ppermute | solution.py:21
  293.2 7.2 %collective-permute-start.2 = (f32[40,4,256]{2,1,0:T(4,128)S(1)}, f32[40,4,256]{2,1,0:T(4,128)S(1)}, u32[]{:S(2)}, u32[]{:S(2)}) collective-permute-start(f32[40,4,256]{2,1,0:T(4,128)S(1)} %get-tuple-element.366), channel_id=1, source_target_pairs={{0,1},{1,2},{2,3},{3,4},{4,5},{5,6},{6,7},{8,9},{9,10},{10,11},{11... | collective-permute-start | bytes 491528 | tf_op jit(solution)/shard_map/while/body/eval_jaxpr/ppermute | solution.py:21
  295.1 10.8 %collective-permute-start.3 = (f32[40,4,256]{2,1,0:T(4,128)S(1)}, f32[40,4,256]{2,1,0:T(4,128)S(1)}, u32[]{:S(2)}, u32[]{:S(2)}) collective-permute-start(f32[40,4,256]{2,1,0:T(4,128)S(1)} %get-tuple-element.367), channel_id=1, source_target_pairs={{1,0},{2,1},{3,2},{4,3},{5,4},{6,5},{7,6},{9,8},{10,9},{11,10},{12... | collective-permute-start | bytes 491528 | tf_op jit(solution)/shard_map/while/body/eval_jaxpr/ppermute | solution.py:22
  318.4 7.9 %collective-permute-start = (f32[4,32,256]{2,1,0:T(8,128)}, f32[4,32,256]{2,1,0:T(8,128)S(1)}, u32[]{:S(2)}, u32[]{:S(2)}) collective-permute-start(f32[4,32,256]{2,1,0:T(8,128)} %get-tuple-element.359), channel_id=1, source_target_pairs={{0,8},{8,16},{16,24},{24,32},{32,40},{40,48},{48,56},{56,64},{64,7... | collective-permute-start | bytes 393224 | tf_op jit(solution)/shard_map/while/body/eval_jaxpr/ppermute | solution.py:21
  327.4 7.2 %collective-permute-start.2 = (f32[40,4,256]{2,1,0:T(4,128)S(1)}, f32[40,4,256]{2,1,0:T(4,128)S(1)}, u32[]{:S(2)}, u32[]{:S(2)}) collective-permute-start(f32[40,4,256]{2,1,0:T(4,128)S(1)} %get-tuple-element.366), channel_id=1, source_target_pairs={{0,1},{1,2},{2,3},{3,4},{4,5},{5,6},{6,7},{8,9},{9,10},{10,11},{11... | collective-permute-start | bytes 491528 | tf_op jit(solution)/shard_map/while/body/eval_jaxpr/ppermute | solution.py:21
  329.4 10.8 %collective-permute-start.3 = (f32[40,4,256]{2,1,0:T(4,128)S(1)}, f32[40,4,256]{2,1,0:T(4,128)S(1)}, u32[]{:S(2)}, u32[]{:S(2)}) collective-permute-start(f32[40,4,256]{2,1,0:T(4,128)S(1)} %get-tuple-element.367), channel_id=1, source_target_pairs={{1,0},{2,1},{3,2},{4,3},{5,4},{6,5},{7,6},{9,8},{10,9},{11,10},{12... | collective-permute-start | bytes 491528 | tf_op jit(solution)/shard_map/while/body/eval_jaxpr/ppermute | solution.py:22
  352.6 7.9 %collective-permute-start = (f32[4,32,256]{2,1,0:T(8,128)}, f32[4,32,256]{2,1,0:T(8,128)S(1)}, u32[]{:S(2)}, u32[]{:S(2)}) collective-permute-start(f32[4,32,256]{2,1,0:T(8,128)} %get-tuple-element.359), channel_id=1, source_target_pairs={{0,8},{8,16},{16,24},{24,32},{32,40},{40,48},{48,56},{56,64},{64,7... | collective-permute-start | bytes 393224 | tf_op jit(solution)/shard_map/while/body/eval_jaxpr/ppermute | solution.py:21
  361.7 7.2 %collective-permute-start.2 = (f32[40,4,256]{2,1,0:T(4,128)S(1)}, f32[40,4,256]{2,1,0:T(4,128)S(1)}, u32[]{:S(2)}, u32[]{:S(2)}) collective-permute-start(f32[40,4,256]{2,1,0:T(4,128)S(1)} %get-tuple-element.366), channel_id=1, source_target_pairs={{0,1},{1,2},{2,3},{3,4},{4,5},{5,6},{6,7},{8,9},{9,10},{10,11},{11... | collective-permute-start | bytes 491528 | tf_op jit(solution)/shard_map/while/body/eval_jaxpr/ppermute | solution.py:21
  363.6 10.8 %collective-permute-start.3 = (f32[40,4,256]{2,1,0:T(4,128)S(1)}, f32[40,4,256]{2,1,0:T(4,128)S(1)}, u32[]{:S(2)}, u32[]{:S(2)}) collective-permute-start(f32[40,4,256]{2,1,0:T(4,128)S(1)} %get-tuple-element.367), channel_id=1, source_target_pairs={{1,0},{2,1},{3,2},{4,3},{5,4},{6,5},{7,6},{9,8},{10,9},{11,10},{12... | collective-permute-start | bytes 491528 | tf_op jit(solution)/shard_map/while/body/eval_jaxpr/ppermute | solution.py:22
  386.9 7.9 %collective-permute-start = (f32[4,32,256]{2,1,0:T(8,128)}, f32[4,32,256]{2,1,0:T(8,128)S(1)}, u32[]{:S(2)}, u32[]{:S(2)}) collective-permute-start(f32[4,32,256]{2,1,0:T(8,128)} %get-tuple-element.359), channel_id=1, source_target_pairs={{0,8},{8,16},{16,24},{24,32},{32,40},{40,48},{48,56},{56,64},{64,7... | collective-permute-start | bytes 393224 | tf_op jit(solution)/shard_map/while/body/eval_jaxpr/ppermute | solution.py:21
  395.9 7.2 %collective-permute-start.2 = (f32[40,4,256]{2,1,0:T(4,128)S(1)}, f32[40,4,256]{2,1,0:T(4,128)S(1)}, u32[]{:S(2)}, u32[]{:S(2)}) collective-permute-start(f32[40,4,256]{2,1,0:T(4,128)S(1)} %get-tuple-element.366), channel_id=1, source_target_pairs={{0,1},{1,2},{2,3},{3,4},{4,5},{5,6},{6,7},{8,9},{9,10},{10,11},{11... | collective-permute-start | bytes 491528 | tf_op jit(solution)/shard_map/while/body/eval_jaxpr/ppermute | solution.py:21
  397.9 10.8 %collective-permute-start.3 = (f32[40,4,256]{2,1,0:T(4,128)S(1)}, f32[40,4,256]{2,1,0:T(4,128)S(1)}, u32[]{:S(2)}, u32[]{:S(2)}) collective-permute-start(f32[40,4,256]{2,1,0:T(4,128)S(1)} %get-tuple-element.367), channel_id=1, source_target_pairs={{1,0},{2,1},{3,2},{4,3},{5,4},{6,5},{7,6},{9,8},{10,9},{11,10},{12... | collective-permute-start | bytes 491528 | tf_op jit(solution)/shard_map/while/body/eval_jaxpr/ppermute | solution.py:22
  421.1 7.9 %collective-permute-start = (f32[4,32,256]{2,1,0:T(8,128)}, f32[4,32,256]{2,1,0:T(8,128)S(1)}, u32[]{:S(2)}, u32[]{:S(2)}) collective-permute-start(f32[4,32,256]{2,1,0:T(8,128)} %get-tuple-element.359), channel_id=1, source_target_pairs={{0,8},{8,16},{16,24},{24,32},{32,40},{40,48},{48,56},{56,64},{64,7... | collective-permute-start | bytes 393224 | tf_op jit(solution)/shard_map/while/body/eval_jaxpr/ppermute | solution.py:21
  430.2 7.2 %collective-permute-start.2 = (f32[40,4,256]{2,1,0:T(4,128)S(1)}, f32[40,4,256]{2,1,0:T(4,128)S(1)}, u32[]{:S(2)}, u32[]{:S(2)}) collective-permute-start(f32[40,4,256]{2,1,0:T(4,128)S(1)} %get-tuple-element.366), channel_id=1, source_target_pairs={{0,1},{1,2},{2,3},{3,4},{4,5},{5,6},{6,7},{8,9},{9,10},{10,11},{11... | collective-permute-start | bytes 491528 | tf_op jit(solution)/shard_map/while/body/eval_jaxpr/ppermute | solution.py:21
  432.1 10.8 %collective-permute-start.3 = (f32[40,4,256]{2,1,0:T(4,128)S(1)}, f32[40,4,256]{2,1,0:T(4,128)S(1)}, u32[]{:S(2)}, u32[]{:S(2)}) collective-permute-start(f32[40,4,256]{2,1,0:T(4,128)S(1)} %get-tuple-element.367), channel_id=1, source_target_pairs={{1,0},{2,1},{3,2},{4,3},{5,4},{6,5},{7,6},{9,8},{10,9},{11,10},{12... | collective-permute-start | bytes 491528 | tf_op jit(solution)/shard_map/while/body/eval_jaxpr/ppermute | solution.py:22
  455.4 7.9 %collective-permute-start = (f32[4,32,256]{2,1,0:T(8,128)}, f32[4,32,256]{2,1,0:T(8,128)S(1)}, u32[]{:S(2)}, u32[]{:S(2)}) collective-permute-start(f32[4,32,256]{2,1,0:T(8,128)} %get-tuple-element.359), channel_id=1, source_target_pairs={{0,8},{8,16},{16,24},{24,32},{32,40},{40,48},{48,56},{56,64},{64,7... | collective-permute-start | bytes 393224 | tf_op jit(solution)/shard_map/while/body/eval_jaxpr/ppermute | solution.py:21
  466.4 10.8 %collective-permute-start.3 = (f32[40,4,256]{2,1,0:T(4,128)S(1)}, f32[40,4,256]{2,1,0:T(4,128)S(1)}, u32[]{:S(2)}, u32[]{:S(2)}) collective-permute-start(f32[40,4,256]{2,1,0:T(4,128)S(1)} %get-tuple-element.367), channel_id=1, source_target_pairs={{1,0},{2,1},{3,2},{4,3},{5,4},{6,5},{7,6},{9,8},{10,9},{11,10},{12... | collective-permute-start | bytes 491528 | tf_op jit(solution)/shard_map/while/body/eval_jaxpr/ppermute | solution.py:22
  489.7 7.9 %collective-permute-start = (f32[4,32,256]{2,1,0:T(8,128)}, f32[4,32,256]{2,1,0:T(8,128)S(1)}, u32[]{:S(2)}, u32[]{:S(2)}) collective-permute-start(f32[4,32,256]{2,1,0:T(8,128)} %get-tuple-element.359), channel_id=1, source_target_pairs={{0,8},{8,16},{16,24},{24,32},{32,40},{40,48},{48,56},{56,64},{64,7... | collective-permute-start | bytes 393224 | tf_op jit(solution)/shard_map/while/body/eval_jaxpr/ppermute | solution.py:21
  498.7 7.2 %collective-permute-start.2 = (f32[40,4,256]{2,1,0:T(4,128)S(1)}, f32[40,4,256]{2,1,0:T(4,128)S(1)}, u32[]{:S(2)}, u32[]{:S(2)}) collective-permute-start(f32[40,4,256]{2,1,0:T(4,128)S(1)} %get-tuple-element.366), channel_id=1, source_target_pairs={{0,1},{1,2},{2,3},{3,4},{4,5},{5,6},{6,7},{8,9},{9,10},{10,11},{11... | collective-permute-start | bytes 491528 | tf_op jit(solution)/shard_map/while/body/eval_jaxpr/ppermute | solution.py:21
  500.7 10.8 %collective-permute-start.3 = (f32[40,4,256]{2,1,0:T(4,128)S(1)}, f32[40,4,256]{2,1,0:T(4,128)S(1)}, u32[]{:S(2)}, u32[]{:S(2)}) collective-permute-start(f32[40,4,256]{2,1,0:T(4,128)S(1)} %get-tuple-element.367), channel_id=1, source_target_pairs={{1,0},{2,1},{3,2},{4,3},{5,4},{6,5},{7,6},{9,8},{10,9},{11,10},{12... | collective-permute-start | bytes 491528 | tf_op jit(solution)/shard_map/while/body/eval_jaxpr/ppermute | solution.py:22
  523.9 7.9 %collective-permute-start = (f32[4,32,256]{2,1,0:T(8,128)}, f32[4,32,256]{2,1,0:T(8,128)S(1)}, u32[]{:S(2)}, u32[]{:S(2)}) collective-permute-start(f32[4,32,256]{2,1,0:T(8,128)} %get-tuple-element.359), channel_id=1, source_target_pairs={{0,8},{8,16},{16,24},{24,32},{32,40},{40,48},{48,56},{56,64},{64,7... | collective-permute-start | bytes 393224 | tf_op jit(solution)/shard_map/while/body/eval_jaxpr/ppermute | solution.py:21
  533.0 7.2 %collective-permute-start.2 = (f32[40,4,256]{2,1,0:T(4,128)S(1)}, f32[40,4,256]{2,1,0:T(4,128)S(1)}, u32[]{:S(2)}, u32[]{:S(2)}) collective-permute-start(f32[40,4,256]{2,1,0:T(4,128)S(1)} %get-tuple-element.366), channel_id=1, source_target_pairs={{0,1},{1,2},{2,3},{3,4},{4,5},{5,6},{6,7},{8,9},{9,10},{10,11},{11... | collective-permute-start | bytes 491528 | tf_op jit(solution)/shard_map/while/body/eval_jaxpr/ppermute | solution.py:21
  534.9 10.8 %collective-permute-start.3 = (f32[40,4,256]{2,1,0:T(4,128)S(1)}, f32[40,4,256]{2,1,0:T(4,128)S(1)}, u32[]{:S(2)}, u32[]{:S(2)}) collective-permute-start(f32[40,4,256]{2,1,0:T(4,128)S(1)} %get-tuple-element.367), channel_id=1, source_target_pairs={{1,0},{2,1},{3,2},{4,3},{5,4},{6,5},{7,6},{9,8},{10,9},{11,10},{12... | collective-permute-start | bytes 491528 | tf_op jit(solution)/shard_map/while/body/eval_jaxpr/ppermute | solution.py:22
  558.2 7.9 %collective-permute-start = (f32[4,32,256]{2,1,0:T(8,128)}, f32[4,32,256]{2,1,0:T(8,128)S(1)}, u32[]{:S(2)}, u32[]{:S(2)}) collective-permute-start(f32[4,32,256]{2,1,0:T(8,128)} %get-tuple-element.359), channel_id=1, source_target_pairs={{0,8},{8,16},{16,24},{24,32},{32,40},{40,48},{48,56},{56,64},{64,7... | collective-permute-start | bytes 393224 | tf_op jit(solution)/shard_map/while/body/eval_jaxpr/ppermute | solution.py:21
  567.2 7.2 %collective-permute-start.2 = (f32[40,4,256]{2,1,0:T(4,128)S(1)}, f32[40,4,256]{2,1,0:T(4,128)S(1)}, u32[]{:S(2)}, u32[]{:S(2)}) collective-permute-start(f32[40,4,256]{2,1,0:T(4,128)S(1)} %get-tuple-element.366), channel_id=1, source_target_pairs={{0,1},{1,2},{2,3},{3,4},{4,5},{5,6},{6,7},{8,9},{9,10},{10,11},{11... | collective-permute-start | bytes 491528 | tf_op jit(solution)/shard_map/while/body/eval_jaxpr/ppermute | solution.py:21
  569.2 10.8 %collective-permute-start.3 = (f32[40,4,256]{2,1,0:T(4,128)S(1)}, f32[40,4,256]{2,1,0:T(4,128)S(1)}, u32[]{:S(2)}, u32[]{:S(2)}) collective-permute-start(f32[40,4,256]{2,1,0:T(4,128)S(1)} %get-tuple-element.367), channel_id=1, source_target_pairs={{1,0},{2,1},{3,2},{4,3},{5,4},{6,5},{7,6},{9,8},{10,9},{11,10},{12... | collective-permute-start | bytes 491528 | tf_op jit(solution)/shard_map/while/body/eval_jaxpr/ppermute | solution.py:22
  (45 other events, 172.8 us)
where the time goes:
time: 602 us; the launch traced here: 593 us
  starting transfers between devices  214 us (36%)
  other arithmetic  172 us (29%)
  waiting for transfers between devices  129 us (21%)
  local copies, waits for them, and re-layouts  72.8 us (12%)
    ppermute x32, starting transfers between devices, extended(): before = lax.ppermute(last, axis, up)  103 us
    ppermute x32, starting transfers between devices, extended(): after = lax.ppermute(first, axis, down)  101 us
    ppermute x32, waiting for transfers between devices, extended(): after = lax.ppermute(first, axis, down)  99.9 us
    scatter-add x16, other arithmetic, inject_own(): field.reshape(-1).at[got_cells].add(own_weights * values_row)  59.8 us
    add x16, other arithmetic, advance(): following = 2.0 * current - before + courant * laplace(padded)  55.6 us
    add x16, other arithmetic, advance(): imaging = imaging + snapshot(position) * following  43.4 us
    while x96, local copies, waits for them, and re-layouts  30.8 us
    ppermute x32, waiting for transfers between devices, extended(): before = lax.ppermute(last, axis, up)  22.4 us
  transfers between devices with their start and end apart: 65, of which 49 were waited for; matrix products, arithmetic and copies ran while one was open for 5% of the time, Pallas kernels for 0%

commit v1 on v0

--- a/solution.py
+++ b/solution.py
@@ -6,39 +6,35 @@
 STEPS = 16
 SHOTS = 16
 TAPS = 17
+HALO = 4
 
 
 stencil_weights = (-205.0 / 72.0, 8.0 / 5.0, -1.0 / 5.0, 8.0 / 315.0, -1.0 / 560.0)
 
 
-def extended(value, sides, width):
-    for axis, dim in sides:
-        peers, length = (lax.axis_size(axis), value.shape[dim])
-        up = [(i, (i + 1) % peers) for i in range(peers - 1)]
-        down = [(j, i) for i, j in up]
-        last = lax.slice_in_dim(value, length - width, length, axis=dim)
-        first = lax.slice_in_dim(value, 0, width, axis=dim)
-        before = lax.ppermute(last, axis, up)
-        after = lax.ppermute(first, axis, down)
-        value = jnp.concatenate([before, value, after], axis=dim)
-    return value
+def faces(value, axis, dim):
+    peers, length = lax.axis_size(axis), value.shape[dim]
+    up = [(i, i + 1) for i in range(peers - 1)]
+    down = [(j, i) for i, j in up]
+    last = lax.slice_in_dim(value, length - HALO, length, axis=dim)
+    first = lax.slice_in_dim(value, 0, HALO, axis=dim)
+    return lax.ppermute(last, axis, up), lax.ppermute(first, axis, down)
 
 
-def laplace(padded):
-    width_x = padded.shape[0] - 8
-    width_y = padded.shape[1] - 8
-    center = padded[4 : 4 + width_x, 4 : 4 + width_y]
-    column = center.shape[2]
+def laplace(center, x_lo, x_hi, y_lo, y_hi):
+    width_x, width_y, column = center.shape
+    along_x_src = jnp.concatenate([x_lo, center, x_hi], axis=0)
+    along_y_src = jnp.concatenate([y_lo, center, y_hi], axis=1)
     z_padded = jnp.pad(center, ((0, 0), (0, 0), (4, 4)))
     summed = 3.0 * stencil_weights[0] * center
     for offset in range(1, 5):
         along_x = (
-            padded[4 + offset : 4 + offset + width_x, 4 : 4 + width_y]
-            + padded[4 - offset : 4 - offset + width_x, 4 : 4 + width_y]
+            along_x_src[4 + offset : 4 + offset + width_x]
+            + along_x_src[4 - offset : 4 - offset + width_x]
         )
         along_y = (
-            padded[4 : 4 + width_x, 4 + offset : 4 + offset + width_y]
-            + padded[4 : 4 + width_x, 4 - offset : 4 - offset + width_y]
+            along_y_src[:, 4 + offset : 4 + offset + width_y]
+            + along_y_src[:, 4 - offset : 4 - offset + width_y]
         )
         along_z = (
             z_padded[:, :, 4 + offset : 4 + offset + column]
@@ -89,25 +85,36 @@
     payload = jnp.concatenate([residual, trace_cell.astype(jnp.float32)[None, :]], axis=0)
     parcel = jnp.dot(payload, slot_table, precision=lax.Precision.HIGHEST)
     received = lax.all_to_all(parcel, ("gx", "gy"), split_axis=1, concat_axis=1, tiled=True)
-    got_values = received[:STEPS]
+    got_values = received[:STEPS][::-1]
     got_cells = received[STEPS].astype(jnp.int32)
-    own_weights = courant.reshape(-1)[got_cells]
-
-    def inject_own(field, position):
-        values_row = lax.dynamic_index_in_dim(got_values, STEPS - 1 - position, 0, keepdims=False)
-        return field.reshape(-1).at[got_cells].add(own_weights * values_row).reshape(field.shape)
-
-    def snapshot(position):
-        return lax.dynamic_index_in_dim(forward_field, position, 0, keepdims=False).astype(
-            jnp.float32
-        )
+    plane = courant.shape[0] * courant.shape[1]
+    column = courant.shape[2]
+    got_plane = got_cells // column
+    got_depth = got_cells % column
+    at_plane = (got_plane[None, :] == jnp.arange(plane, dtype=jnp.int32)[:, None]).astype(jnp.bfloat16)
+    at_plane = jnp.concatenate([at_plane] * 3, axis=1)
+    at_depth = got_depth[:, None] == jnp.arange(column, dtype=jnp.int32)[None, :]
+    at_depth = jnp.concatenate([at_depth] * 3, axis=0)
+    high = got_values.astype(jnp.bfloat16)
+    rest = got_values - high.astype(jnp.float32)
+    middle = rest.astype(jnp.bfloat16)
+    low = (rest - middle.astype(jnp.float32)).astype(jnp.bfloat16)
+    pieces = jnp.concatenate([high, middle, low], axis=1)
 
     def advance(position, carry):
         current, before, imaging = carry
-        padded = extended(current, (("gx", 0), ("gy", 1)), 4)
-        following = 2.0 * current - before + courant * laplace(padded)
-        following = inject_own(following, position)
-        imaging = imaging + snapshot(position) * following
+        x_lo, x_hi = faces(current, "gx", 0)
+        y_lo, y_hi = faces(current, "gy", 1)
+        piece = lax.dynamic_index_in_dim(pieces, position, 0, keepdims=False)
+        spread = jnp.where(at_depth, piece[:, None], jnp.zeros((), jnp.bfloat16))
+        source = jnp.dot(at_plane, spread, preferred_element_type=jnp.float32).reshape(
+            current.shape
+        )
+        following = 2.0 * current - before + courant * (
+            laplace(current, x_lo, x_hi, y_lo, y_hi) + source
+        )
+        snapshot = lax.dynamic_index_in_dim(forward_field, position, 0, keepdims=False)
+        imaging = imaging + snapshot.astype(jnp.float32) * following
         return (following, current, imaging)
 
     current, before, imaging = lax.fori_loop(

time: 602 us -> 532 us (0.88)
  waiting for transfers between devices: 129 us -> 8.7 us
  other arithmetic: 172 us -> 62.3 us
  matrix products: 1.65 us -> 68.6 us
  starting transfers between devices: 214 us -> 270 us
  local copies, waits for them, and re-layouts: 72.8 us -> 114 us
    ppermute x64, waiting for transfers between devices: 122 us -> 0.17 us  [faces(): return (lax.ppermute(last, axis, up), lax.ppermute(first, axis, down))]
    dot_general x0 -> x16, matrix products: none -> 67 us  [advance(): jnp.dot(at_plane, spread, preferred_element_type=jnp.float32)]
    scatter-add x16 -> x0, other arithmetic: 59.8 us -> none  [inject_own(): field.reshape(-1).at[got_cells].add(own_weights * values_row)]
    ppermute x64, starting transfers between devices: 204 us -> 259 us  [faces(): return (lax.ppermute(last, axis, up), lax.ppermute(first, axis, down))]
    add x32 -> x16, other arithmetic: 99 us -> 57.2 us  [advance(): imaging = imaging + snapshot.astype(jnp.float32) * following]
    while x97 -> x288, local copies, waits for them, and re-layouts: 31.5 us -> 59.2 us
    dot_general x0 -> x16, local copies, waits for them, and re-layouts: none -> 24.9 us  [advance(): jnp.dot(at_plane, spread, preferred_element_type=jnp.float32)]
    slice x32 -> x33, local copies, waits for them, and re-layouts: 11.7 us -> 24.2 us  [the longest x32 24.2 us: faces(): first = lax.slice_in_dim(value, 0, HALO, axis=dim)]
  transfers between devices with their start and end apart: 65 -> 65, of which waited for: 49 -> 1; matrix products, arithmetic and copies ran while one was open for 5% -> 24% of each run, Pallas kernels for 0% -> 0%
where the time goes in v1:
time: 532 us; the launch traced here: 527 us
  starting transfers between devices  270 us (51%)
  local copies, waits for them, and re-layouts  114 us (21%)
  matrix products  68.6 us (13%)
  other arithmetic  62.3 us (12%)
  waiting for transfers between devices  8.7 us (2%)
    ppermute x64, starting transfers between devices, faces(): return (lax.ppermute(last, axis, up), lax.ppermute(first, axis, down))  259 us
    dot_general x16, matrix products, advance(): jnp.dot(at_plane, spread, preferred_element_type=jnp.float32)  67 us
    while x288, local copies, waits for them, and re-layouts  59.2 us
    add x16, other arithmetic, advance(): imaging = imaging + snapshot.astype(jnp.float32) * following  57.2 us
    dot_general x16, local copies, waits for them, and re-layouts, advance(): jnp.dot(at_plane, spread, preferred_element_type=jnp.float32)  24.9 us
    slice x32, local copies, waits for them, and re-layouts, faces(): first = lax.slice_in_dim(value, 0, HALO, axis=dim)  24.2 us
  transfers between devices with their start and end apart: 65, of which 1 were waited for; matrix products, arithmetic and copies ran while one was open for 24% of the time, Pallas kernels for 0%

profile of v1, /device:TPU:38, one launch (start us, length us, event | category | flops | bytes accessed | tf_op | source)
XLA Modules:
  0.0 526.8 jit_solution(7075984810444517535)
XLA Ops:
  4.9 10.2 %all-to-all-start = ((f32[17,128,4]{0,2,1:T(4,128)}), f32[17,128,4]{0,2,1:T(4,128)S(1)}, u32[]{:S(2)}, u32[]{:S(2)}) async-start(f32[17,128,4]{0,2,1:T(4,128)} %bitcast.25), calls=%async_computation | async-start | bytes 524288 | tf_op jit(solution)/shard_map/all_to_all | solution.py:87
  15.1 8.5 %all-to-all-done = f32[17,128,4]{0,2,1:T(4,128)S(1)} async-done(((f32[17,128,4]{0,2,1:T(4,128)}), f32[17,128,4]{0,2,1:T(4,128)S(1)}, u32[]{:S(2)}, u32[]{:S(2)}) %all-to-all-start) | async-done | bytes 34848 | tf_op jit(solution)/shard_map/all_to_all | solution.py:87
  29.1 496.4 %while.19 = (s32[]{:T(128)}, f32[32,32,256]{2,1,0:T(8,128)S(1)}, f32[32,32,256]{2,1,0:T(8,128)S(1)}, f32[32,32,256]{2,1,0:T(8,128)}, bf16[16,1536]{1,0:T(8,128)(...) while((s32[]{:T(128)}, f32[32,32,256]{2,1,0:T(8,128)S(1)}, ...), condition=%wide.region_2.3_spmd, body=%wide.region_1.2_spmd.sunk | while | flops 816447488 | bytes 55715288 | solution.py:120
  39.0 7.9 %collective-permute-start = (f32[32,4,256]{2,1,0:T(4,128)}, f32[32,4,256]{2,1,0:T(4,128)S(1)}, u32[]{:S(2)}, u32[]{:S(2)}) collective-permute-start(f32[32,4,256]{2,1,0:T(4,128)} %get-tuple-element.362), channel_id=1, source_target_pairs={{0,1},{1,2},{2,3},{3,4},{4,5},{5,6},{6,7},{8,9},{9,10},{10,11},{11... | collective-permute-start | bytes 393224 | tf_op jit(solution)/shard_map/while/body/eval_jaxpr/ppermute | solution.py:21
  46.9 4.2 convolution_bitcast_fusion.3
  65.4 4.5 collective-permute-start.3
  70.0 7.9 %collective-permute-start = (f32[32,4,256]{2,1,0:T(4,128)}, f32[32,4,256]{2,1,0:T(4,128)S(1)}, u32[]{:S(2)}, u32[]{:S(2)}) collective-permute-start(f32[32,4,256]{2,1,0:T(4,128)} %get-tuple-element.362), channel_id=1, source_target_pairs={{0,1},{1,2},{2,3},{3,4},{4,5},{5,6},{6,7},{8,9},{9,10},{10,11},{11... | collective-permute-start | bytes 393224 | tf_op jit(solution)/shard_map/while/body/eval_jaxpr/ppermute | solution.py:21
  77.9 4.2 convolution_bitcast_fusion.3
  96.5 4.5 collective-permute-start.3
  101.0 7.9 %collective-permute-start = (f32[32,4,256]{2,1,0:T(4,128)}, f32[32,4,256]{2,1,0:T(4,128)S(1)}, u32[]{:S(2)}, u32[]{:S(2)}) collective-permute-start(f32[32,4,256]{2,1,0:T(4,128)} %get-tuple-element.362), channel_id=1, source_target_pairs={{0,1},{1,2},{2,3},{3,4},{4,5},{5,6},{6,7},{8,9},{9,10},{10,11},{11... | collective-permute-start | bytes 393224 | tf_op jit(solution)/shard_map/while/body/eval_jaxpr/ppermute | solution.py:21
  108.9 4.2 convolution_bitcast_fusion.3
  127.5 4.5 collective-permute-start.3
  132.0 7.9 %collective-permute-start = (f32[32,4,256]{2,1,0:T(4,128)}, f32[32,4,256]{2,1,0:T(4,128)S(1)}, u32[]{:S(2)}, u32[]{:S(2)}) collective-permute-start(f32[32,4,256]{2,1,0:T(4,128)} %get-tuple-element.362), channel_id=1, source_target_pairs={{0,1},{1,2},{2,3},{3,4},{4,5},{5,6},{6,7},{8,9},{9,10},{10,11},{11... | collective-permute-start | bytes 393224 | tf_op jit(solution)/shard_map/while/body/eval_jaxpr/ppermute | solution.py:21
  140.0 4.2 convolution_bitcast_fusion.3
  158.5 4.5 collective-permute-start.3
  163.1 7.9 %collective-permute-start = (f32[32,4,256]{2,1,0:T(4,128)}, f32[32,4,256]{2,1,0:T(4,128)S(1)}, u32[]{:S(2)}, u32[]{:S(2)}) collective-permute-start(f32[32,4,256]{2,1,0:T(4,128)} %get-tuple-element.362), channel_id=1, source_target_pairs={{0,1},{1,2},{2,3},{3,4},{4,5},{5,6},{6,7},{8,9},{9,10},{10,11},{11... | collective-permute-start | bytes 393224 | tf_op jit(solution)/shard_map/while/body/eval_jaxpr/ppermute | solution.py:21
  171.0 4.2 convolution_bitcast_fusion.3
  189.5 4.5 collective-permute-start.3
  194.1 7.9 %collective-permute-start = (f32[32,4,256]{2,1,0:T(4,128)}, f32[32,4,256]{2,1,0:T(4,128)S(1)}, u32[]{:S(2)}, u32[]{:S(2)}) collective-permute-start(f32[32,4,256]{2,1,0:T(4,128)} %get-tuple-element.362), channel_id=1, source_target_pairs={{0,1},{1,2},{2,3},{3,4},{4,5},{5,6},{6,7},{8,9},{9,10},{10,11},{11... | collective-permute-start | bytes 393224 | tf_op jit(solution)/shard_map/while/body/eval_jaxpr/ppermute | solution.py:21
  202.0 4.2 convolution_bitcast_fusion.3
  220.6 4.5 collective-permute-start.3
  225.1 7.9 %collective-permute-start = (f32[32,4,256]{2,1,0:T(4,128)}, f32[32,4,256]{2,1,0:T(4,128)S(1)}, u32[]{:S(2)}, u32[]{:S(2)}) collective-permute-start(f32[32,4,256]{2,1,0:T(4,128)} %get-tuple-element.362), channel_id=1, source_target_pairs={{0,1},{1,2},{2,3},{3,4},{4,5},{5,6},{6,7},{8,9},{9,10},{10,11},{11... | collective-permute-start | bytes 393224 | tf_op jit(solution)/shard_map/while/body/eval_jaxpr/ppermute | solution.py:21
  233.1 4.2 convolution_bitcast_fusion.3
  251.6 4.5 collective-permute-start.3
  256.1 7.9 %collective-permute-start = (f32[32,4,256]{2,1,0:T(4,128)}, f32[32,4,256]{2,1,0:T(4,128)S(1)}, u32[]{:S(2)}, u32[]{:S(2)}) collective-permute-start(f32[32,4,256]{2,1,0:T(4,128)} %get-tuple-element.362), channel_id=1, source_target_pairs={{0,1},{1,2},{2,3},{3,4},{4,5},{5,6},{6,7},{8,9},{9,10},{10,11},{11... | collective-permute-start | bytes 393224 | tf_op jit(solution)/shard_map/while/body/eval_jaxpr/ppermute | solution.py:21
  264.1 4.2 convolution_bitcast_fusion.3
  282.6 4.5 collective-permute-start.3
  287.2 7.9 %collective-permute-start = (f32[32,4,256]{2,1,0:T(4,128)}, f32[32,4,256]{2,1,0:T(4,128)S(1)}, u32[]{:S(2)}, u32[]{:S(2)}) collective-permute-start(f32[32,4,256]{2,1,0:T(4,128)} %get-tuple-element.362), channel_id=1, source_target_pairs={{0,1},{1,2},{2,3},{3,4},{4,5},{5,6},{6,7},{8,9},{9,10},{10,11},{11... | collective-permute-start | bytes 393224 | tf_op jit(solution)/shard_map/while/body/eval_jaxpr/ppermute | solution.py:21
  295.1 4.2 convolution_bitcast_fusion.3
  313.7 4.5 collective-permute-start.3
  318.2 7.9 %collective-permute-start = (f32[32,4,256]{2,1,0:T(4,128)}, f32[32,4,256]{2,1,0:T(4,128)S(1)}, u32[]{:S(2)}, u32[]{:S(2)}) collective-permute-start(f32[32,4,256]{2,1,0:T(4,128)} %get-tuple-element.362), channel_id=1, source_target_pairs={{0,1},{1,2},{2,3},{3,4},{4,5},{5,6},{6,7},{8,9},{9,10},{10,11},{11... | collective-permute-start | bytes 393224 | tf_op jit(solution)/shard_map/while/body/eval_jaxpr/ppermute | solution.py:21
  326.1 4.2 convolution_bitcast_fusion.3
  344.7 4.5 collective-permute-start.3
  349.2 7.9 %collective-permute-start = (f32[32,4,256]{2,1,0:T(4,128)}, f32[32,4,256]{2,1,0:T(4,128)S(1)}, u32[]{:S(2)}, u32[]{:S(2)}) collective-permute-start(f32[32,4,256]{2,1,0:T(4,128)} %get-tuple-element.362), channel_id=1, source_target_pairs={{0,1},{1,2},{2,3},{3,4},{4,5},{5,6},{6,7},{8,9},{9,10},{10,11},{11... | collective-permute-start | bytes 393224 | tf_op jit(solution)/shard_map/while/body/eval_jaxpr/ppermute | solution.py:21
  375.7 4.5 collective-permute-start.3
  380.3 7.9 %collective-permute-start = (f32[32,4,256]{2,1,0:T(4,128)}, f32[32,4,256]{2,1,0:T(4,128)S(1)}, u32[]{:S(2)}, u32[]{:S(2)}) collective-permute-start(f32[32,4,256]{2,1,0:T(4,128)} %get-tuple-element.362), channel_id=1, source_target_pairs={{0,1},{1,2},{2,3},{3,4},{4,5},{5,6},{6,7},{8,9},{9,10},{10,11},{11... | collective-permute-start | bytes 393224 | tf_op jit(solution)/shard_map/while/body/eval_jaxpr/ppermute | solution.py:21
  388.2 4.2 convolution_bitcast_fusion.3
  406.7 4.5 collective-permute-start.3
  411.3 7.9 %collective-permute-start = (f32[32,4,256]{2,1,0:T(4,128)}, f32[32,4,256]{2,1,0:T(4,128)S(1)}, u32[]{:S(2)}, u32[]{:S(2)}) collective-permute-start(f32[32,4,256]{2,1,0:T(4,128)} %get-tuple-element.362), channel_id=1, source_target_pairs={{0,1},{1,2},{2,3},{3,4},{4,5},{5,6},{6,7},{8,9},{9,10},{10,11},{11... | collective-permute-start | bytes 393224 | tf_op jit(solution)/shard_map/while/body/eval_jaxpr/ppermute | solution.py:21
  437.8 4.5 collective-permute-start.3
  442.3 7.9 %collective-permute-start = (f32[32,4,256]{2,1,0:T(4,128)}, f32[32,4,256]{2,1,0:T(4,128)S(1)}, u32[]{:S(2)}, u32[]{:S(2)}) collective-permute-start(f32[32,4,256]{2,1,0:T(4,128)} %get-tuple-element.362), channel_id=1, source_target_pairs={{0,1},{1,2},{2,3},{3,4},{4,5},{5,6},{6,7},{8,9},{9,10},{10,11},{11... | collective-permute-start | bytes 393224 | tf_op jit(solution)/shard_map/while/body/eval_jaxpr/ppermute | solution.py:21
  450.2 4.2 convolution_bitcast_fusion.3
  468.8 4.5 collective-permute-start.3
  473.3 7.9 %collective-permute-start = (f32[32,4,256]{2,1,0:T(4,128)}, f32[32,4,256]{2,1,0:T(4,128)S(1)}, u32[]{:S(2)}, u32[]{:S(2)}) collective-permute-start(f32[32,4,256]{2,1,0:T(4,128)} %get-tuple-element.362), channel_id=1, source_target_pairs={{0,1},{1,2},{2,3},{3,4},{4,5},{5,6},{6,7},{8,9},{9,10},{10,11},{11... | collective-permute-start | bytes 393224 | tf_op jit(solution)/shard_map/while/body/eval_jaxpr/ppermute | solution.py:21
  481.3 4.2 convolution_bitcast_fusion.3
  499.8 4.5 collective-permute-start.3
  504.4 7.9 %collective-permute-start = (f32[32,4,256]{2,1,0:T(4,128)}, f32[32,4,256]{2,1,0:T(4,128)S(1)}, u32[]{:S(2)}, u32[]{:S(2)}) collective-permute-start(f32[32,4,256]{2,1,0:T(4,128)} %get-tuple-element.362), channel_id=1, source_target_pairs={{0,1},{1,2},{2,3},{3,4},{4,5},{5,6},{6,7},{8,9},{9,10},{10,11},{11... | collective-permute-start | bytes 393224 | tf_op jit(solution)/shard_map/while/body/eval_jaxpr/ppermute | solution.py:21
  512.3 4.2 convolution_bitcast_fusion.3
  (540 shorter events, 251.9 us)
Async XLA Ops:
  4.9 18.7 %all-to-all-start = ((f32[17,128,4]{0,2,1:T(4,128)}), f32[17,128,4]{0,2,1:T(4,128)S(1)}, u32[]{:S(2)}, u32[]{:S(2)}) async-start(f32[17,128,4]{0,2,1:T(4,128)} %bitcast.25), calls=%async_computation | async-start | bytes 524288 | tf_op jit(solution)/shard_map/all_to_all | solution.py:87
  29.8 22.8 %collective-permute-start.1 = (f32[4,32,256]{2,1,0:T(8,128)}, f32[4,32,256]{2,1,0:T(8,128)}, u32[]{:S(2)}, u32[]{:S(2)}) collective-permute-start(f32[4,32,256]{2,1,0:T(8,128)} %get-tuple-element.363), channel_id=1, source_target_pairs={{0,8},{8,16},{16,24},{24,32},{32,40},{40,48},{48,56},{56,64},{64,7... | collective-permute-start | bytes 393224 | tf_op jit(solution)/shard_map/while/body/eval_jaxpr/ppermute | solution.py:21
  32.6 21.3 %collective-permute-start.2 = (f32[32,4,256]{2,1,0:T(4,128)}, f32[32,4,256]{2,1,0:T(4,128)S(1)}, u32[]{:S(2)}, u32[]{:S(2)}) collective-permute-start(f32[32,4,256]{2,1,0:T(4,128)} %get-tuple-element.365), channel_id=1, source_target_pairs={{1,0},{2,1},{3,2},{4,3},{5,4},{6,5},{7,6},{9,8},{10,9},{11,10},{12... | collective-permute-start | bytes 393224 | tf_op jit(solution)/shard_map/while/body/eval_jaxpr/ppermute | solution.py:21
  60.9 22.8 %collective-permute-start.1 = (f32[4,32,256]{2,1,0:T(8,128)}, f32[4,32,256]{2,1,0:T(8,128)}, u32[]{:S(2)}, u32[]{:S(2)}) collective-permute-start(f32[4,32,256]{2,1,0:T(8,128)} %get-tuple-element.363), channel_id=1, source_target_pairs={{0,8},{8,16},{16,24},{24,32},{32,40},{40,48},{48,56},{56,64},{64,7... | collective-permute-start | bytes 393224 | tf_op jit(solution)/shard_map/while/body/eval_jaxpr/ppermute | solution.py:21
  63.5 21.5 %collective-permute-start.2 = (f32[32,4,256]{2,1,0:T(4,128)}, f32[32,4,256]{2,1,0:T(4,128)S(1)}, u32[]{:S(2)}, u32[]{:S(2)}) collective-permute-start(f32[32,4,256]{2,1,0:T(4,128)} %get-tuple-element.365), channel_id=1, source_target_pairs={{1,0},{2,1},{3,2},{4,3},{5,4},{6,5},{7,6},{9,8},{10,9},{11,10},{12... | collective-permute-start | bytes 393224 | tf_op jit(solution)/shard_map/while/body/eval_jaxpr/ppermute | solution.py:21
  65.4 19.6 %collective-permute-start.3 = (f32[4,32,256]{2,1,0:T(8,128)}, f32[4,32,256]{2,1,0:T(8,128)S(1)}, u32[]{:S(2)}, u32[]{:S(2)}) collective-permute-start(f32[4,32,256]{2,1,0:T(8,128)} %get-tuple-element.368), channel_id=1, source_target_pairs={{8,0},{16,8},{24,16},{32,24},{40,32},{48,40},{56,48},{64,56},{72,6... | collective-permute-start | bytes 393224 | tf_op jit(solution)/shard_map/while/body/eval_jaxpr/ppermute | solution.py:21
  91.9 22.8 %collective-permute-start.1 = (f32[4,32,256]{2,1,0:T(8,128)}, f32[4,32,256]{2,1,0:T(8,128)}, u32[]{:S(2)}, u32[]{:S(2)}) collective-permute-start(f32[4,32,256]{2,1,0:T(8,128)} %get-tuple-element.363), channel_id=1, source_target_pairs={{0,8},{8,16},{16,24},{24,32},{32,40},{40,48},{48,56},{56,64},{64,7... | collective-permute-start | bytes 393224 | tf_op jit(solution)/shard_map/while/body/eval_jaxpr/ppermute | solution.py:21
  94.6 21.5 %collective-permute-start.2 = (f32[32,4,256]{2,1,0:T(4,128)}, f32[32,4,256]{2,1,0:T(4,128)S(1)}, u32[]{:S(2)}, u32[]{:S(2)}) collective-permute-start(f32[32,4,256]{2,1,0:T(4,128)} %get-tuple-element.365), channel_id=1, source_target_pairs={{1,0},{2,1},{3,2},{4,3},{5,4},{6,5},{7,6},{9,8},{10,9},{11,10},{12... | collective-permute-start | bytes 393224 | tf_op jit(solution)/shard_map/while/body/eval_jaxpr/ppermute | solution.py:21
  96.5 19.6 %collective-permute-start.3 = (f32[4,32,256]{2,1,0:T(8,128)}, f32[4,32,256]{2,1,0:T(8,128)S(1)}, u32[]{:S(2)}, u32[]{:S(2)}) collective-permute-start(f32[4,32,256]{2,1,0:T(8,128)} %get-tuple-element.368), channel_id=1, source_target_pairs={{8,0},{16,8},{24,16},{32,24},{40,32},{48,40},{56,48},{64,56},{72,6... | collective-permute-start | bytes 393224 | tf_op jit(solution)/shard_map/while/body/eval_jaxpr/ppermute | solution.py:21
  122.9 22.8 %collective-permute-start.1 = (f32[4,32,256]{2,1,0:T(8,128)}, f32[4,32,256]{2,1,0:T(8,128)}, u32[]{:S(2)}, u32[]{:S(2)}) collective-permute-start(f32[4,32,256]{2,1,0:T(8,128)} %get-tuple-element.363), channel_id=1, source_target_pairs={{0,8},{8,16},{16,24},{24,32},{32,40},{40,48},{48,56},{56,64},{64,7... | collective-permute-start | bytes 393224 | tf_op jit(solution)/shard_map/while/body/eval_jaxpr/ppermute | solution.py:21
  125.6 21.5 %collective-permute-start.2 = (f32[32,4,256]{2,1,0:T(4,128)}, f32[32,4,256]{2,1,0:T(4,128)S(1)}, u32[]{:S(2)}, u32[]{:S(2)}) collective-permute-start(f32[32,4,256]{2,1,0:T(4,128)} %get-tuple-element.365), channel_id=1, source_target_pairs={{1,0},{2,1},{3,2},{4,3},{5,4},{6,5},{7,6},{9,8},{10,9},{11,10},{12... | collective-permute-start | bytes 393224 | tf_op jit(solution)/shard_map/while/body/eval_jaxpr/ppermute | solution.py:21
  127.5 19.6 %collective-permute-start.3 = (f32[4,32,256]{2,1,0:T(8,128)}, f32[4,32,256]{2,1,0:T(8,128)S(1)}, u32[]{:S(2)}, u32[]{:S(2)}) collective-permute-start(f32[4,32,256]{2,1,0:T(8,128)} %get-tuple-element.368), channel_id=1, source_target_pairs={{8,0},{16,8},{24,16},{32,24},{40,32},{48,40},{56,48},{64,56},{72,6... | collective-permute-start | bytes 393224 | tf_op jit(solution)/shard_map/while/body/eval_jaxpr/ppermute | solution.py:21
  154.0 22.8 %collective-permute-start.1 = (f32[4,32,256]{2,1,0:T(8,128)}, f32[4,32,256]{2,1,0:T(8,128)}, u32[]{:S(2)}, u32[]{:S(2)}) collective-permute-start(f32[4,32,256]{2,1,0:T(8,128)} %get-tuple-element.363), channel_id=1, source_target_pairs={{0,8},{8,16},{16,24},{24,32},{32,40},{40,48},{48,56},{56,64},{64,7... | collective-permute-start | bytes 393224 | tf_op jit(solution)/shard_map/while/body/eval_jaxpr/ppermute | solution.py:21
  156.6 21.5 %collective-permute-start.2 = (f32[32,4,256]{2,1,0:T(4,128)}, f32[32,4,256]{2,1,0:T(4,128)S(1)}, u32[]{:S(2)}, u32[]{:S(2)}) collective-permute-start(f32[32,4,256]{2,1,0:T(4,128)} %get-tuple-element.365), channel_id=1, source_target_pairs={{1,0},{2,1},{3,2},{4,3},{5,4},{6,5},{7,6},{9,8},{10,9},{11,10},{12... | collective-permute-start | bytes 393224 | tf_op jit(solution)/shard_map/while/body/eval_jaxpr/ppermute | solution.py:21
  158.5 19.6 %collective-permute-start.3 = (f32[4,32,256]{2,1,0:T(8,128)}, f32[4,32,256]{2,1,0:T(8,128)S(1)}, u32[]{:S(2)}, u32[]{:S(2)}) collective-permute-start(f32[4,32,256]{2,1,0:T(8,128)} %get-tuple-element.368), channel_id=1, source_target_pairs={{8,0},{16,8},{24,16},{32,24},{40,32},{48,40},{56,48},{64,56},{72,6... | collective-permute-start | bytes 393224 | tf_op jit(solution)/shard_map/while/body/eval_jaxpr/ppermute | solution.py:21
  185.0 22.8 %collective-permute-start.1 = (f32[4,32,256]{2,1,0:T(8,128)}, f32[4,32,256]{2,1,0:T(8,128)}, u32[]{:S(2)}, u32[]{:S(2)}) collective-permute-start(f32[4,32,256]{2,1,0:T(8,128)} %get-tuple-element.363), channel_id=1, source_target_pairs={{0,8},{8,16},{16,24},{24,32},{32,40},{40,48},{48,56},{56,64},{64,7... | collective-permute-start | bytes 393224 | tf_op jit(solution)/shard_map/while/body/eval_jaxpr/ppermute | solution.py:21
  187.6 21.5 %collective-permute-start.2 = (f32[32,4,256]{2,1,0:T(4,128)}, f32[32,4,256]{2,1,0:T(4,128)S(1)}, u32[]{:S(2)}, u32[]{:S(2)}) collective-permute-start(f32[32,4,256]{2,1,0:T(4,128)} %get-tuple-element.365), channel_id=1, source_target_pairs={{1,0},{2,1},{3,2},{4,3},{5,4},{6,5},{7,6},{9,8},{10,9},{11,10},{12... | collective-permute-start | bytes 393224 | tf_op jit(solution)/shard_map/while/body/eval_jaxpr/ppermute | solution.py:21
  189.5 19.6 %collective-permute-start.3 = (f32[4,32,256]{2,1,0:T(8,128)}, f32[4,32,256]{2,1,0:T(8,128)S(1)}, u32[]{:S(2)}, u32[]{:S(2)}) collective-permute-start(f32[4,32,256]{2,1,0:T(8,128)} %get-tuple-element.368), channel_id=1, source_target_pairs={{8,0},{16,8},{24,16},{32,24},{40,32},{48,40},{56,48},{64,56},{72,6... | collective-permute-start | bytes 393224 | tf_op jit(solution)/shard_map/while/body/eval_jaxpr/ppermute | solution.py:21
  216.0 22.8 %collective-permute-start.1 = (f32[4,32,256]{2,1,0:T(8,128)}, f32[4,32,256]{2,1,0:T(8,128)}, u32[]{:S(2)}, u32[]{:S(2)}) collective-permute-start(f32[4,32,256]{2,1,0:T(8,128)} %get-tuple-element.363), channel_id=1, source_target_pairs={{0,8},{8,16},{16,24},{24,32},{32,40},{40,48},{48,56},{56,64},{64,7... | collective-permute-start | bytes 393224 | tf_op jit(solution)/shard_map/while/body/eval_jaxpr/ppermute | solution.py:21
  218.7 21.5 %collective-permute-start.2 = (f32[32,4,256]{2,1,0:T(4,128)}, f32[32,4,256]{2,1,0:T(4,128)S(1)}, u32[]{:S(2)}, u32[]{:S(2)}) collective-permute-start(f32[32,4,256]{2,1,0:T(4,128)} %get-tuple-element.365), channel_id=1, source_target_pairs={{1,0},{2,1},{3,2},{4,3},{5,4},{6,5},{7,6},{9,8},{10,9},{11,10},{12... | collective-permute-start | bytes 393224 | tf_op jit(solution)/shard_map/while/body/eval_jaxpr/ppermute | solution.py:21
  220.6 19.6 %collective-permute-start.3 = (f32[4,32,256]{2,1,0:T(8,128)}, f32[4,32,256]{2,1,0:T(8,128)S(1)}, u32[]{:S(2)}, u32[]{:S(2)}) collective-permute-start(f32[4,32,256]{2,1,0:T(8,128)} %get-tuple-element.368), channel_id=1, source_target_pairs={{8,0},{16,8},{24,16},{32,24},{40,32},{48,40},{56,48},{64,56},{72,6... | collective-permute-start | bytes 393224 | tf_op jit(solution)/shard_map/while/body/eval_jaxpr/ppermute | solution.py:21
  247.0 22.8 %collective-permute-start.1 = (f32[4,32,256]{2,1,0:T(8,128)}, f32[4,32,256]{2,1,0:T(8,128)}, u32[]{:S(2)}, u32[]{:S(2)}) collective-permute-start(f32[4,32,256]{2,1,0:T(8,128)} %get-tuple-element.363), channel_id=1, source_target_pairs={{0,8},{8,16},{16,24},{24,32},{32,40},{40,48},{48,56},{56,64},{64,7... | collective-permute-start | bytes 393224 | tf_op jit(solution)/shard_map/while/body/eval_jaxpr/ppermute | solution.py:21
  249.7 21.5 %collective-permute-start.2 = (f32[32,4,256]{2,1,0:T(4,128)}, f32[32,4,256]{2,1,0:T(4,128)S(1)}, u32[]{:S(2)}, u32[]{:S(2)}) collective-permute-start(f32[32,4,256]{2,1,0:T(4,128)} %get-tuple-element.365), channel_id=1, source_target_pairs={{1,0},{2,1},{3,2},{4,3},{5,4},{6,5},{7,6},{9,8},{10,9},{11,10},{12... | collective-permute-start | bytes 393224 | tf_op jit(solution)/shard_map/while/body/eval_jaxpr/ppermute | solution.py:21
  251.6 19.6 %collective-permute-start.3 = (f32[4,32,256]{2,1,0:T(8,128)}, f32[4,32,256]{2,1,0:T(8,128)S(1)}, u32[]{:S(2)}, u32[]{:S(2)}) collective-permute-start(f32[4,32,256]{2,1,0:T(8,128)} %get-tuple-element.368), channel_id=1, source_target_pairs={{8,0},{16,8},{24,16},{32,24},{40,32},{48,40},{56,48},{64,56},{72,6... | collective-permute-start | bytes 393224 | tf_op jit(solution)/shard_map/while/body/eval_jaxpr/ppermute | solution.py:21
  278.1 22.8 %collective-permute-start.1 = (f32[4,32,256]{2,1,0:T(8,128)}, f32[4,32,256]{2,1,0:T(8,128)}, u32[]{:S(2)}, u32[]{:S(2)}) collective-permute-start(f32[4,32,256]{2,1,0:T(8,128)} %get-tuple-element.363), channel_id=1, source_target_pairs={{0,8},{8,16},{16,24},{24,32},{32,40},{40,48},{48,56},{56,64},{64,7... | collective-permute-start | bytes 393224 | tf_op jit(solution)/shard_map/while/body/eval_jaxpr/ppermute | solution.py:21
  280.7 21.5 %collective-permute-start.2 = (f32[32,4,256]{2,1,0:T(4,128)}, f32[32,4,256]{2,1,0:T(4,128)S(1)}, u32[]{:S(2)}, u32[]{:S(2)}) collective-permute-start(f32[32,4,256]{2,1,0:T(4,128)} %get-tuple-element.365), channel_id=1, source_target_pairs={{1,0},{2,1},{3,2},{4,3},{5,4},{6,5},{7,6},{9,8},{10,9},{11,10},{12... | collective-permute-start | bytes 393224 | tf_op jit(solution)/shard_map/while/body/eval_jaxpr/ppermute | solution.py:21
  282.6 19.6 %collective-permute-start.3 = (f32[4,32,256]{2,1,0:T(8,128)}, f32[4,32,256]{2,1,0:T(8,128)S(1)}, u32[]{:S(2)}, u32[]{:S(2)}) collective-permute-start(f32[4,32,256]{2,1,0:T(8,128)} %get-tuple-element.368), channel_id=1, source_target_pairs={{8,0},{16,8},{24,16},{32,24},{40,32},{48,40},{56,48},{64,56},{72,6... | collective-permute-start | bytes 393224 | tf_op jit(solution)/shard_map/while/body/eval_jaxpr/ppermute | solution.py:21
  309.1 22.8 %collective-permute-start.1 = (f32[4,32,256]{2,1,0:T(8,128)}, f32[4,32,256]{2,1,0:T(8,128)}, u32[]{:S(2)}, u32[]{:S(2)}) collective-permute-start(f32[4,32,256]{2,1,0:T(8,128)} %get-tuple-element.363), channel_id=1, source_target_pairs={{0,8},{8,16},{16,24},{24,32},{32,40},{40,48},{48,56},{56,64},{64,7... | collective-permute-start | bytes 393224 | tf_op jit(solution)/shard_map/while/body/eval_jaxpr/ppermute | solution.py:21
  311.7 21.5 %collective-permute-start.2 = (f32[32,4,256]{2,1,0:T(4,128)}, f32[32,4,256]{2,1,0:T(4,128)S(1)}, u32[]{:S(2)}, u32[]{:S(2)}) collective-permute-start(f32[32,4,256]{2,1,0:T(4,128)} %get-tuple-element.365), channel_id=1, source_target_pairs={{1,0},{2,1},{3,2},{4,3},{5,4},{6,5},{7,6},{9,8},{10,9},{11,10},{12... | collective-permute-start | bytes 393224 | tf_op jit(solution)/shard_map/while/body/eval_jaxpr/ppermute | solution.py:21
  313.7 19.6 %collective-permute-start.3 = (f32[4,32,256]{2,1,0:T(8,128)}, f32[4,32,256]{2,1,0:T(8,128)S(1)}, u32[]{:S(2)}, u32[]{:S(2)}) collective-permute-start(f32[4,32,256]{2,1,0:T(8,128)} %get-tuple-element.368), channel_id=1, source_target_pairs={{8,0},{16,8},{24,16},{32,24},{40,32},{48,40},{56,48},{64,56},{72,6... | collective-permute-start | bytes 393224 | tf_op jit(solution)/shard_map/while/body/eval_jaxpr/ppermute | solution.py:21
  340.1 22.8 %collective-permute-start.1 = (f32[4,32,256]{2,1,0:T(8,128)}, f32[4,32,256]{2,1,0:T(8,128)}, u32[]{:S(2)}, u32[]{:S(2)}) collective-permute-start(f32[4,32,256]{2,1,0:T(8,128)} %get-tuple-element.363), channel_id=1, source_target_pairs={{0,8},{8,16},{16,24},{24,32},{32,40},{40,48},{48,56},{56,64},{64,7... | collective-permute-start | bytes 393224 | tf_op jit(solution)/shard_map/while/body/eval_jaxpr/ppermute | solution.py:21
  342.8 21.5 %collective-permute-start.2 = (f32[32,4,256]{2,1,0:T(4,128)}, f32[32,4,256]{2,1,0:T(4,128)S(1)}, u32[]{:S(2)}, u32[]{:S(2)}) collective-permute-start(f32[32,4,256]{2,1,0:T(4,128)} %get-tuple-element.365), channel_id=1, source_target_pairs={{1,0},{2,1},{3,2},{4,3},{5,4},{6,5},{7,6},{9,8},{10,9},{11,10},{12... | collective-permute-start | bytes 393224 | tf_op jit(solution)/shard_map/while/body/eval_jaxpr/ppermute | solution.py:21
  344.7 19.6 %collective-permute-start.3 = (f32[4,32,256]{2,1,0:T(8,128)}, f32[4,32,256]{2,1,0:T(8,128)S(1)}, u32[]{:S(2)}, u32[]{:S(2)}) collective-permute-start(f32[4,32,256]{2,1,0:T(8,128)} %get-tuple-element.368), channel_id=1, source_target_pairs={{8,0},{16,8},{24,16},{32,24},{40,32},{48,40},{56,48},{64,56},{72,6... | collective-permute-start | bytes 393224 | tf_op jit(solution)/shard_map/while/body/eval_jaxpr/ppermute | solution.py:21
  371.1 22.8 %collective-permute-start.1 = (f32[4,32,256]{2,1,0:T(8,128)}, f32[4,32,256]{2,1,0:T(8,128)}, u32[]{:S(2)}, u32[]{:S(2)}) collective-permute-start(f32[4,32,256]{2,1,0:T(8,128)} %get-tuple-element.363), channel_id=1, source_target_pairs={{0,8},{8,16},{16,24},{24,32},{32,40},{40,48},{48,56},{56,64},{64,7... | collective-permute-start | bytes 393224 | tf_op jit(solution)/shard_map/while/body/eval_jaxpr/ppermute | solution.py:21
  373.8 21.5 %collective-permute-start.2 = (f32[32,4,256]{2,1,0:T(4,128)}, f32[32,4,256]{2,1,0:T(4,128)S(1)}, u32[]{:S(2)}, u32[]{:S(2)}) collective-permute-start(f32[32,4,256]{2,1,0:T(4,128)} %get-tuple-element.365), channel_id=1, source_target_pairs={{1,0},{2,1},{3,2},{4,3},{5,4},{6,5},{7,6},{9,8},{10,9},{11,10},{12... | collective-permute-start | bytes 393224 | tf_op jit(solution)/shard_map/while/body/eval_jaxpr/ppermute | solution.py:21
  375.7 19.6 %collective-permute-start.3 = (f32[4,32,256]{2,1,0:T(8,128)}, f32[4,32,256]{2,1,0:T(8,128)S(1)}, u32[]{:S(2)}, u32[]{:S(2)}) collective-permute-start(f32[4,32,256]{2,1,0:T(8,128)} %get-tuple-element.368), channel_id=1, source_target_pairs={{8,0},{16,8},{24,16},{32,24},{40,32},{48,40},{56,48},{64,56},{72,6... | collective-permute-start | bytes 393224 | tf_op jit(solution)/shard_map/while/body/eval_jaxpr/ppermute | solution.py:21
  402.2 22.8 %collective-permute-start.1 = (f32[4,32,256]{2,1,0:T(8,128)}, f32[4,32,256]{2,1,0:T(8,128)}, u32[]{:S(2)}, u32[]{:S(2)}) collective-permute-start(f32[4,32,256]{2,1,0:T(8,128)} %get-tuple-element.363), channel_id=1, source_target_pairs={{0,8},{8,16},{16,24},{24,32},{32,40},{40,48},{48,56},{56,64},{64,7... | collective-permute-start | bytes 393224 | tf_op jit(solution)/shard_map/while/body/eval_jaxpr/ppermute | solution.py:21
  404.8 21.5 %collective-permute-start.2 = (f32[32,4,256]{2,1,0:T(4,128)}, f32[32,4,256]{2,1,0:T(4,128)S(1)}, u32[]{:S(2)}, u32[]{:S(2)}) collective-permute-start(f32[32,4,256]{2,1,0:T(4,128)} %get-tuple-element.365), channel_id=1, source_target_pairs={{1,0},{2,1},{3,2},{4,3},{5,4},{6,5},{7,6},{9,8},{10,9},{11,10},{12... | collective-permute-start | bytes 393224 | tf_op jit(solution)/shard_map/while/body/eval_jaxpr/ppermute | solution.py:21
  406.7 19.6 %collective-permute-start.3 = (f32[4,32,256]{2,1,0:T(8,128)}, f32[4,32,256]{2,1,0:T(8,128)S(1)}, u32[]{:S(2)}, u32[]{:S(2)}) collective-permute-start(f32[4,32,256]{2,1,0:T(8,128)} %get-tuple-element.368), channel_id=1, source_target_pairs={{8,0},{16,8},{24,16},{32,24},{40,32},{48,40},{56,48},{64,56},{72,6... | collective-permute-start | bytes 393224 | tf_op jit(solution)/shard_map/while/body/eval_jaxpr/ppermute | solution.py:21
  433.2 22.8 %collective-permute-start.1 = (f32[4,32,256]{2,1,0:T(8,128)}, f32[4,32,256]{2,1,0:T(8,128)}, u32[]{:S(2)}, u32[]{:S(2)}) collective-permute-start(f32[4,32,256]{2,1,0:T(8,128)} %get-tuple-element.363), channel_id=1, source_target_pairs={{0,8},{8,16},{16,24},{24,32},{32,40},{40,48},{48,56},{56,64},{64,7... | collective-permute-start | bytes 393224 | tf_op jit(solution)/shard_map/while/body/eval_jaxpr/ppermute | solution.py:21
  435.9 21.5 %collective-permute-start.2 = (f32[32,4,256]{2,1,0:T(4,128)}, f32[32,4,256]{2,1,0:T(4,128)S(1)}, u32[]{:S(2)}, u32[]{:S(2)}) collective-permute-start(f32[32,4,256]{2,1,0:T(4,128)} %get-tuple-element.365), channel_id=1, source_target_pairs={{1,0},{2,1},{3,2},{4,3},{5,4},{6,5},{7,6},{9,8},{10,9},{11,10},{12... | collective-permute-start | bytes 393224 | tf_op jit(solution)/shard_map/while/body/eval_jaxpr/ppermute | solution.py:21
  437.8 19.6 %collective-permute-start.3 = (f32[4,32,256]{2,1,0:T(8,128)}, f32[4,32,256]{2,1,0:T(8,128)S(1)}, u32[]{:S(2)}, u32[]{:S(2)}) collective-permute-start(f32[4,32,256]{2,1,0:T(8,128)} %get-tuple-element.368), channel_id=1, source_target_pairs={{8,0},{16,8},{24,16},{32,24},{40,32},{48,40},{56,48},{64,56},{72,6... | collective-permute-start | bytes 393224 | tf_op jit(solution)/shard_map/while/body/eval_jaxpr/ppermute | solution.py:21
  464.2 22.8 %collective-permute-start.1 = (f32[4,32,256]{2,1,0:T(8,128)}, f32[4,32,256]{2,1,0:T(8,128)}, u32[]{:S(2)}, u32[]{:S(2)}) collective-permute-start(f32[4,32,256]{2,1,0:T(8,128)} %get-tuple-element.363), channel_id=1, source_target_pairs={{0,8},{8,16},{16,24},{24,32},{32,40},{40,48},{48,56},{56,64},{64,7... | collective-permute-start | bytes 393224 | tf_op jit(solution)/shard_map/while/body/eval_jaxpr/ppermute | solution.py:21
  466.9 21.5 %collective-permute-start.2 = (f32[32,4,256]{2,1,0:T(4,128)}, f32[32,4,256]{2,1,0:T(4,128)S(1)}, u32[]{:S(2)}, u32[]{:S(2)}) collective-permute-start(f32[32,4,256]{2,1,0:T(4,128)} %get-tuple-element.365), channel_id=1, source_target_pairs={{1,0},{2,1},{3,2},{4,3},{5,4},{6,5},{7,6},{9,8},{10,9},{11,10},{12... | collective-permute-start | bytes 393224 | tf_op jit(solution)/shard_map/while/body/eval_jaxpr/ppermute | solution.py:21
  468.8 19.6 %collective-permute-start.3 = (f32[4,32,256]{2,1,0:T(8,128)}, f32[4,32,256]{2,1,0:T(8,128)S(1)}, u32[]{:S(2)}, u32[]{:S(2)}) collective-permute-start(f32[4,32,256]{2,1,0:T(8,128)} %get-tuple-element.368), channel_id=1, source_target_pairs={{8,0},{16,8},{24,16},{32,24},{40,32},{48,40},{56,48},{64,56},{72,6... | collective-permute-start | bytes 393224 | tf_op jit(solution)/shard_map/while/body/eval_jaxpr/ppermute | solution.py:21
  495.3 22.8 %collective-permute-start.1 = (f32[4,32,256]{2,1,0:T(8,128)}, f32[4,32,256]{2,1,0:T(8,128)}, u32[]{:S(2)}, u32[]{:S(2)}) collective-permute-start(f32[4,32,256]{2,1,0:T(8,128)} %get-tuple-element.363), channel_id=1, source_target_pairs={{0,8},{8,16},{16,24},{24,32},{32,40},{40,48},{48,56},{56,64},{64,7... | collective-permute-start | bytes 393224 | tf_op jit(solution)/shard_map/while/body/eval_jaxpr/ppermute | solution.py:21
  497.9 21.5 %collective-permute-start.2 = (f32[32,4,256]{2,1,0:T(4,128)}, f32[32,4,256]{2,1,0:T(4,128)S(1)}, u32[]{:S(2)}, u32[]{:S(2)}) collective-permute-start(f32[32,4,256]{2,1,0:T(4,128)} %get-tuple-element.365), channel_id=1, source_target_pairs={{1,0},{2,1},{3,2},{4,3},{5,4},{6,5},{7,6},{9,8},{10,9},{11,10},{12... | collective-permute-start | bytes 393224 | tf_op jit(solution)/shard_map/while/body/eval_jaxpr/ppermute | solution.py:21
  499.8 19.6 %collective-permute-start.3 = (f32[4,32,256]{2,1,0:T(8,128)}, f32[4,32,256]{2,1,0:T(8,128)S(1)}, u32[]{:S(2)}, u32[]{:S(2)}) collective-permute-start(f32[4,32,256]{2,1,0:T(8,128)} %get-tuple-element.368), channel_id=1, source_target_pairs={{8,0},{16,8},{24,16},{32,24},{40,32},{48,40},{56,48},{64,56},{72,6... | collective-permute-start | bytes 393224 | tf_op jit(solution)/shard_map/while/body/eval_jaxpr/ppermute | solution.py:21
  (140 other events, 947.5 us)

commit v2 on v1

--- a/solution.py
+++ b/solution.py
@@ -19,6 +19,11 @@
     last = lax.slice_in_dim(value, length - HALO, length, axis=dim)
     first = lax.slice_in_dim(value, 0, HALO, axis=dim)
     return lax.ppermute(last, axis, up), lax.ppermute(first, axis, down)
+
+
+def split_high(value):
+    scaled = value * 65537.0
+    return scaled - (scaled - value)
 
 
 def laplace(center, x_lo, x_hi, y_lo, y_hi):
@@ -91,15 +96,14 @@
     column = courant.shape[2]
     got_plane = got_cells // column
     got_depth = got_cells % column
-    at_plane = (got_plane[None, :] == jnp.arange(plane, dtype=jnp.int32)[:, None]).astype(jnp.bfloat16)
-    at_plane = jnp.concatenate([at_plane] * 3, axis=1)
+    at_plane = (got_plane[:, None] == jnp.arange(plane, dtype=jnp.int32)[None, :]).astype(jnp.bfloat16)
+    at_plane = jnp.concatenate([at_plane] * 3, axis=0)
     at_depth = got_depth[:, None] == jnp.arange(column, dtype=jnp.int32)[None, :]
     at_depth = jnp.concatenate([at_depth] * 3, axis=0)
-    high = got_values.astype(jnp.bfloat16)
-    rest = got_values - high.astype(jnp.float32)
-    middle = rest.astype(jnp.bfloat16)
-    low = (rest - middle.astype(jnp.float32)).astype(jnp.bfloat16)
-    pieces = jnp.concatenate([high, middle, low], axis=1)
+    top = split_high(got_values)
+    rest = got_values - top
+    second = split_high(rest)
+    pieces = jnp.concatenate([top, second, rest - second], axis=1).astype(jnp.bfloat16)
 
     def advance(position, carry):
         current, before, imaging = carry
@@ -107,9 +111,9 @@
         y_lo, y_hi = faces(current, "gy", 1)
         piece = lax.dynamic_index_in_dim(pieces, position, 0, keepdims=False)
         spread = jnp.where(at_depth, piece[:, None], jnp.zeros((), jnp.bfloat16))
-        source = jnp.dot(at_plane, spread, preferred_element_type=jnp.float32).reshape(
-            current.shape
-        )
+        source = lax.dot_general(
+            spread, at_plane, (((0,), (0,)), ((), ())), preferred_element_type=jnp.float32
+        ).T.reshape(current.shape)
         following = 2.0 * current - before + courant * (
             laplace(current, x_lo, x_hi, y_lo, y_hi) + source
         )

time: 532 us -> 528 us (level)
    dot_general x16 -> x0, local copies, waits for them, and re-layouts: 24.9 us -> none  [advance(): jnp.dot(at_plane, spread, preferred_element_type=jnp.float32)]
    transpose x0 -> x16, local copies, waits for them, and re-layouts: none -> 24.9 us  [advance(): source = lax.dot_general(spread, at_plane, (((0,), (0,)), ((), ())), pref...]
  transfers between devices with their start and end apart: 65 -> 65, of which waited for: 1 -> 1; matrix products, arithmetic and copies ran while one was open for 24% -> 23% of each run, Pallas kernels for 0% -> 0%
where the time goes in v2:
time: 528 us; the launch traced here: 523 us
  starting transfers between devices  270 us (51%)
  local copies, waits for them, and re-layouts  114 us (22%)
  matrix products  65.1 us (12%)
  other arithmetic  62.6 us (12%)
  waiting for transfers between devices  8.7 us (2%)
    ppermute x64, starting transfers between devices, faces(): return (lax.ppermute(last, axis, up), lax.ppermute(first, axis, down))  259 us
    dot_general x16, matrix products, advance(): lax.dot_general(spread, at_plane, (((0,), (0,)), ((), ())), preferred_ele...  63.5 us
    while x288, local copies, waits for them, and re-layouts  59.2 us
    add x16, other arithmetic, advance(): imaging = imaging + snapshot.astype(jnp.float32) * following  57.2 us
    transpose x16, local copies, waits for them, and re-layouts, advance(): source = lax.dot_general(spread, at_plane, (((0,), (0,)), ((), ())), pref...  24.9 us
    slice x32, local copies, waits for them, and re-layouts, faces(): first = lax.slice_in_dim(value, 0, HALO, axis=dim)  24.2 us
  transfers between devices with their start and end apart: 65, of which 1 were waited for; matrix products, arithmetic and copies ran while one was open for 23% of the time, Pallas kernels for 0%

profile of v2, /device:TPU:38, one launch (start us, length us, event | category | flops | bytes accessed | tf_op | source)
XLA Modules:
  0.0 523.4 jit_solution(15646056428383362263)
XLA Ops:
  4.9 10.2 %all-to-all-start = ((f32[17,128,4]{0,2,1:T(4,128)}), f32[17,128,4]{0,2,1:T(4,128)S(1)}, u32[]{:S(2)}, u32[]{:S(2)}) async-start(f32[17,128,4]{0,2,1:T(4,128)} %bitcast.25), calls=%async_computation | async-start | bytes 524288 | tf_op jit(solution)/shard_map/all_to_all | solution.py:92
  15.1 8.5 %all-to-all-done = f32[17,128,4]{0,2,1:T(4,128)S(1)} async-done(((f32[17,128,4]{0,2,1:T(4,128)}), f32[17,128,4]{0,2,1:T(4,128)S(1)}, u32[]{:S(2)}, u32[]{:S(2)}) %all-to-all-start) | async-done | bytes 34848 | tf_op jit(solution)/shard_map/all_to_all | solution.py:92
  29.1 493.0 %while.19 = (s32[]{:T(128)}, f32[32,32,256]{2,1,0:T(8,128)S(1)}, f32[32,32,256]{2,1,0:T(8,128)S(1)}, f32[32,32,256]{2,1,0:T(8,128)}, bf16[16,1536]{1,0:T(8,128)(...) while((s32[]{:T(128)}, f32[32,32,256]{2,1,0:T(8,128)S(1)}, ...), condition=%wide.region_2.3_spmd, body=%wide.region_1.2_spmd.sunk | while | flops 816447488 | bytes 55715288 | solution.py:124
  39.0 7.9 %collective-permute-start = (f32[32,4,256]{2,1,0:T(4,128)}, f32[32,4,256]{2,1,0:T(4,128)S(1)}, u32[]{:S(2)}, u32[]{:S(2)}) collective-permute-start(f32[32,4,256]{2,1,0:T(4,128)} %get-tuple-element.362), channel_id=1, source_target_pairs={{0,1},{1,2},{2,3},{3,4},{4,5},{5,6},{6,7},{8,9},{9,10},{10,11},{11... | collective-permute-start | bytes 393224 | tf_op jit(solution)/shard_map/while/body/eval_jaxpr/ppermute | solution.py:21
  46.9 4.0 convolution_bitcast_fusion.3
  65.3 4.5 collective-permute-start.3
  69.8 7.9 %collective-permute-start = (f32[32,4,256]{2,1,0:T(4,128)}, f32[32,4,256]{2,1,0:T(4,128)S(1)}, u32[]{:S(2)}, u32[]{:S(2)}) collective-permute-start(f32[32,4,256]{2,1,0:T(4,128)} %get-tuple-element.362), channel_id=1, source_target_pairs={{0,1},{1,2},{2,3},{3,4},{4,5},{5,6},{6,7},{8,9},{9,10},{10,11},{11... | collective-permute-start | bytes 393224 | tf_op jit(solution)/shard_map/while/body/eval_jaxpr/ppermute | solution.py:21
  77.7 4.0 convolution_bitcast_fusion.3
  96.1 4.5 collective-permute-start.3
  100.6 7.9 %collective-permute-start = (f32[32,4,256]{2,1,0:T(4,128)}, f32[32,4,256]{2,1,0:T(4,128)S(1)}, u32[]{:S(2)}, u32[]{:S(2)}) collective-permute-start(f32[32,4,256]{2,1,0:T(4,128)} %get-tuple-element.362), channel_id=1, source_target_pairs={{0,1},{1,2},{2,3},{3,4},{4,5},{5,6},{6,7},{8,9},{9,10},{10,11},{11... | collective-permute-start | bytes 393224 | tf_op jit(solution)/shard_map/while/body/eval_jaxpr/ppermute | solution.py:21
  126.9 4.5 collective-permute-start.3
  131.4 7.9 %collective-permute-start = (f32[32,4,256]{2,1,0:T(4,128)}, f32[32,4,256]{2,1,0:T(4,128)S(1)}, u32[]{:S(2)}, u32[]{:S(2)}) collective-permute-start(f32[32,4,256]{2,1,0:T(4,128)} %get-tuple-element.362), channel_id=1, source_target_pairs={{0,1},{1,2},{2,3},{3,4},{4,5},{5,6},{6,7},{8,9},{9,10},{10,11},{11... | collective-permute-start | bytes 393224 | tf_op jit(solution)/shard_map/while/body/eval_jaxpr/ppermute | solution.py:21
  139.4 4.0 convolution_bitcast_fusion.3
  157.7 4.5 collective-permute-start.3
  162.2 7.9 %collective-permute-start = (f32[32,4,256]{2,1,0:T(4,128)}, f32[32,4,256]{2,1,0:T(4,128)S(1)}, u32[]{:S(2)}, u32[]{:S(2)}) collective-permute-start(f32[32,4,256]{2,1,0:T(4,128)} %get-tuple-element.362), channel_id=1, source_target_pairs={{0,1},{1,2},{2,3},{3,4},{4,5},{5,6},{6,7},{8,9},{9,10},{10,11},{11... | collective-permute-start | bytes 393224 | tf_op jit(solution)/shard_map/while/body/eval_jaxpr/ppermute | solution.py:21
  170.2 4.0 convolution_bitcast_fusion.3
  188.5 4.5 collective-permute-start.3
  193.0 7.9 %collective-permute-start = (f32[32,4,256]{2,1,0:T(4,128)}, f32[32,4,256]{2,1,0:T(4,128)S(1)}, u32[]{:S(2)}, u32[]{:S(2)}) collective-permute-start(f32[32,4,256]{2,1,0:T(4,128)} %get-tuple-element.362), channel_id=1, source_target_pairs={{0,1},{1,2},{2,3},{3,4},{4,5},{5,6},{6,7},{8,9},{9,10},{10,11},{11... | collective-permute-start | bytes 393224 | tf_op jit(solution)/shard_map/while/body/eval_jaxpr/ppermute | solution.py:21
  201.0 4.0 convolution_bitcast_fusion.3
  219.3 4.5 collective-permute-start.3
  223.9 7.9 %collective-permute-start = (f32[32,4,256]{2,1,0:T(4,128)}, f32[32,4,256]{2,1,0:T(4,128)S(1)}, u32[]{:S(2)}, u32[]{:S(2)}) collective-permute-start(f32[32,4,256]{2,1,0:T(4,128)} %get-tuple-element.362), channel_id=1, source_target_pairs={{0,1},{1,2},{2,3},{3,4},{4,5},{5,6},{6,7},{8,9},{9,10},{10,11},{11... | collective-permute-start | bytes 393224 | tf_op jit(solution)/shard_map/while/body/eval_jaxpr/ppermute | solution.py:21
  231.8 4.0 convolution_bitcast_fusion.3
  250.1 4.5 collective-permute-start.3
  254.7 7.9 %collective-permute-start = (f32[32,4,256]{2,1,0:T(4,128)}, f32[32,4,256]{2,1,0:T(4,128)S(1)}, u32[]{:S(2)}, u32[]{:S(2)}) collective-permute-start(f32[32,4,256]{2,1,0:T(4,128)} %get-tuple-element.362), channel_id=1, source_target_pairs={{0,1},{1,2},{2,3},{3,4},{4,5},{5,6},{6,7},{8,9},{9,10},{10,11},{11... | collective-permute-start | bytes 393224 | tf_op jit(solution)/shard_map/while/body/eval_jaxpr/ppermute | solution.py:21
  262.6 4.0 convolution_bitcast_fusion.3
  280.9 4.5 collective-permute-start.3
  285.5 7.9 %collective-permute-start = (f32[32,4,256]{2,1,0:T(4,128)}, f32[32,4,256]{2,1,0:T(4,128)S(1)}, u32[]{:S(2)}, u32[]{:S(2)}) collective-permute-start(f32[32,4,256]{2,1,0:T(4,128)} %get-tuple-element.362), channel_id=1, source_target_pairs={{0,1},{1,2},{2,3},{3,4},{4,5},{5,6},{6,7},{8,9},{9,10},{10,11},{11... | collective-permute-start | bytes 393224 | tf_op jit(solution)/shard_map/while/body/eval_jaxpr/ppermute | solution.py:21
  293.4 4.0 convolution_bitcast_fusion.3
  311.7 4.5 collective-permute-start.3
  316.3 7.9 %collective-permute-start = (f32[32,4,256]{2,1,0:T(4,128)}, f32[32,4,256]{2,1,0:T(4,128)S(1)}, u32[]{:S(2)}, u32[]{:S(2)}) collective-permute-start(f32[32,4,256]{2,1,0:T(4,128)} %get-tuple-element.362), channel_id=1, source_target_pairs={{0,1},{1,2},{2,3},{3,4},{4,5},{5,6},{6,7},{8,9},{9,10},{10,11},{11... | collective-permute-start | bytes 393224 | tf_op jit(solution)/shard_map/while/body/eval_jaxpr/ppermute | solution.py:21
  324.2 4.0 convolution_bitcast_fusion.3
  342.5 4.5 collective-permute-start.3
  347.1 7.9 %collective-permute-start = (f32[32,4,256]{2,1,0:T(4,128)}, f32[32,4,256]{2,1,0:T(4,128)S(1)}, u32[]{:S(2)}, u32[]{:S(2)}) collective-permute-start(f32[32,4,256]{2,1,0:T(4,128)} %get-tuple-element.362), channel_id=1, source_target_pairs={{0,1},{1,2},{2,3},{3,4},{4,5},{5,6},{6,7},{8,9},{9,10},{10,11},{11... | collective-permute-start | bytes 393224 | tf_op jit(solution)/shard_map/while/body/eval_jaxpr/ppermute | solution.py:21
  355.0 4.0 convolution_bitcast_fusion.3
  373.3 4.5 collective-permute-start.3
  377.9 7.9 %collective-permute-start = (f32[32,4,256]{2,1,0:T(4,128)}, f32[32,4,256]{2,1,0:T(4,128)S(1)}, u32[]{:S(2)}, u32[]{:S(2)}) collective-permute-start(f32[32,4,256]{2,1,0:T(4,128)} %get-tuple-element.362), channel_id=1, source_target_pairs={{0,1},{1,2},{2,3},{3,4},{4,5},{5,6},{6,7},{8,9},{9,10},{10,11},{11... | collective-permute-start | bytes 393224 | tf_op jit(solution)/shard_map/while/body/eval_jaxpr/ppermute | solution.py:21
  385.8 4.0 convolution_bitcast_fusion.3
  404.2 4.5 collective-permute-start.3
  408.7 7.9 %collective-permute-start = (f32[32,4,256]{2,1,0:T(4,128)}, f32[32,4,256]{2,1,0:T(4,128)S(1)}, u32[]{:S(2)}, u32[]{:S(2)}) collective-permute-start(f32[32,4,256]{2,1,0:T(4,128)} %get-tuple-element.362), channel_id=1, source_target_pairs={{0,1},{1,2},{2,3},{3,4},{4,5},{5,6},{6,7},{8,9},{9,10},{10,11},{11... | collective-permute-start | bytes 393224 | tf_op jit(solution)/shard_map/while/body/eval_jaxpr/ppermute | solution.py:21
  416.6 4.0 convolution_bitcast_fusion.3
  435.0 4.5 collective-permute-start.3
  439.5 7.9 %collective-permute-start = (f32[32,4,256]{2,1,0:T(4,128)}, f32[32,4,256]{2,1,0:T(4,128)S(1)}, u32[]{:S(2)}, u32[]{:S(2)}) collective-permute-start(f32[32,4,256]{2,1,0:T(4,128)} %get-tuple-element.362), channel_id=1, source_target_pairs={{0,1},{1,2},{2,3},{3,4},{4,5},{5,6},{6,7},{8,9},{9,10},{10,11},{11... | collective-permute-start | bytes 393224 | tf_op jit(solution)/shard_map/while/body/eval_jaxpr/ppermute | solution.py:21
  447.4 4.0 convolution_bitcast_fusion.3
  465.8 4.5 collective-permute-start.3
  470.3 7.9 %collective-permute-start = (f32[32,4,256]{2,1,0:T(4,128)}, f32[32,4,256]{2,1,0:T(4,128)S(1)}, u32[]{:S(2)}, u32[]{:S(2)}) collective-permute-start(f32[32,4,256]{2,1,0:T(4,128)} %get-tuple-element.362), channel_id=1, source_target_pairs={{0,1},{1,2},{2,3},{3,4},{4,5},{5,6},{6,7},{8,9},{9,10},{10,11},{11... | collective-permute-start | bytes 393224 | tf_op jit(solution)/shard_map/while/body/eval_jaxpr/ppermute | solution.py:21
  496.6 4.5 collective-permute-start.3
  501.1 7.9 %collective-permute-start = (f32[32,4,256]{2,1,0:T(4,128)}, f32[32,4,256]{2,1,0:T(4,128)S(1)}, u32[]{:S(2)}, u32[]{:S(2)}) collective-permute-start(f32[32,4,256]{2,1,0:T(4,128)} %get-tuple-element.362), channel_id=1, source_target_pairs={{0,1},{1,2},{2,3},{3,4},{4,5},{5,6},{6,7},{8,9},{9,10},{10,11},{11... | collective-permute-start | bytes 393224 | tf_op jit(solution)/shard_map/while/body/eval_jaxpr/ppermute | solution.py:21
  509.1 4.0 convolution_bitcast_fusion.3
  (540 shorter events, 251.4 us)
Async XLA Ops:
  4.9 18.7 %all-to-all-start = ((f32[17,128,4]{0,2,1:T(4,128)}), f32[17,128,4]{0,2,1:T(4,128)S(1)}, u32[]{:S(2)}, u32[]{:S(2)}) async-start(f32[17,128,4]{0,2,1:T(4,128)} %bitcast.25), calls=%async_computation | async-start | bytes 524288 | tf_op jit(solution)/shard_map/all_to_all | solution.py:92
  29.9 22.6 %collective-permute-start.1 = (f32[4,32,256]{2,1,0:T(8,128)}, f32[4,32,256]{2,1,0:T(8,128)}, u32[]{:S(2)}, u32[]{:S(2)}) collective-permute-start(f32[4,32,256]{2,1,0:T(8,128)} %get-tuple-element.363), channel_id=1, source_target_pairs={{0,8},{8,16},{16,24},{24,32},{32,40},{40,48},{48,56},{56,64},{64,7... | collective-permute-start | bytes 393224 | tf_op jit(solution)/shard_map/while/body/eval_jaxpr/ppermute | solution.py:21
  32.7 21.1 %collective-permute-start.2 = (f32[32,4,256]{2,1,0:T(4,128)}, f32[32,4,256]{2,1,0:T(4,128)S(1)}, u32[]{:S(2)}, u32[]{:S(2)}) collective-permute-start(f32[32,4,256]{2,1,0:T(4,128)} %get-tuple-element.365), channel_id=1, source_target_pairs={{1,0},{2,1},{3,2},{4,3},{5,4},{6,5},{7,6},{9,8},{10,9},{11,10},{12... | collective-permute-start | bytes 393224 | tf_op jit(solution)/shard_map/while/body/eval_jaxpr/ppermute | solution.py:21
  60.7 22.6 %collective-permute-start.1 = (f32[4,32,256]{2,1,0:T(8,128)}, f32[4,32,256]{2,1,0:T(8,128)}, u32[]{:S(2)}, u32[]{:S(2)}) collective-permute-start(f32[4,32,256]{2,1,0:T(8,128)} %get-tuple-element.363), channel_id=1, source_target_pairs={{0,8},{8,16},{16,24},{24,32},{32,40},{40,48},{48,56},{56,64},{64,7... | collective-permute-start | bytes 393224 | tf_op jit(solution)/shard_map/while/body/eval_jaxpr/ppermute | solution.py:21
  63.3 21.2 %collective-permute-start.2 = (f32[32,4,256]{2,1,0:T(4,128)}, f32[32,4,256]{2,1,0:T(4,128)S(1)}, u32[]{:S(2)}, u32[]{:S(2)}) collective-permute-start(f32[32,4,256]{2,1,0:T(4,128)} %get-tuple-element.365), channel_id=1, source_target_pairs={{1,0},{2,1},{3,2},{4,3},{5,4},{6,5},{7,6},{9,8},{10,9},{11,10},{12... | collective-permute-start | bytes 393224 | tf_op jit(solution)/shard_map/while/body/eval_jaxpr/ppermute | solution.py:21
  65.3 19.4 %collective-permute-start.3 = (f32[4,32,256]{2,1,0:T(8,128)}, f32[4,32,256]{2,1,0:T(8,128)S(1)}, u32[]{:S(2)}, u32[]{:S(2)}) collective-permute-start(f32[4,32,256]{2,1,0:T(8,128)} %get-tuple-element.368), channel_id=1, source_target_pairs={{8,0},{16,8},{24,16},{32,24},{40,32},{48,40},{56,48},{64,56},{72,6... | collective-permute-start | bytes 393224 | tf_op jit(solution)/shard_map/while/body/eval_jaxpr/ppermute | solution.py:21
  91.5 22.6 %collective-permute-start.1 = (f32[4,32,256]{2,1,0:T(8,128)}, f32[4,32,256]{2,1,0:T(8,128)}, u32[]{:S(2)}, u32[]{:S(2)}) collective-permute-start(f32[4,32,256]{2,1,0:T(8,128)} %get-tuple-element.363), channel_id=1, source_target_pairs={{0,8},{8,16},{16,24},{24,32},{32,40},{40,48},{48,56},{56,64},{64,7... | collective-permute-start | bytes 393224 | tf_op jit(solution)/shard_map/while/body/eval_jaxpr/ppermute | solution.py:21
  94.2 21.2 %collective-permute-start.2 = (f32[32,4,256]{2,1,0:T(4,128)}, f32[32,4,256]{2,1,0:T(4,128)S(1)}, u32[]{:S(2)}, u32[]{:S(2)}) collective-permute-start(f32[32,4,256]{2,1,0:T(4,128)} %get-tuple-element.365), channel_id=1, source_target_pairs={{1,0},{2,1},{3,2},{4,3},{5,4},{6,5},{7,6},{9,8},{10,9},{11,10},{12... | collective-permute-start | bytes 393224 | tf_op jit(solution)/shard_map/while/body/eval_jaxpr/ppermute | solution.py:21
  96.1 19.4 %collective-permute-start.3 = (f32[4,32,256]{2,1,0:T(8,128)}, f32[4,32,256]{2,1,0:T(8,128)S(1)}, u32[]{:S(2)}, u32[]{:S(2)}) collective-permute-start(f32[4,32,256]{2,1,0:T(8,128)} %get-tuple-element.368), channel_id=1, source_target_pairs={{8,0},{16,8},{24,16},{32,24},{40,32},{48,40},{56,48},{64,56},{72,6... | collective-permute-start | bytes 393224 | tf_op jit(solution)/shard_map/while/body/eval_jaxpr/ppermute | solution.py:21
  122.3 22.6 %collective-permute-start.1 = (f32[4,32,256]{2,1,0:T(8,128)}, f32[4,32,256]{2,1,0:T(8,128)}, u32[]{:S(2)}, u32[]{:S(2)}) collective-permute-start(f32[4,32,256]{2,1,0:T(8,128)} %get-tuple-element.363), channel_id=1, source_target_pairs={{0,8},{8,16},{16,24},{24,32},{32,40},{40,48},{48,56},{56,64},{64,7... | collective-permute-start | bytes 393224 | tf_op jit(solution)/shard_map/while/body/eval_jaxpr/ppermute | solution.py:21
  125.0 21.2 %collective-permute-start.2 = (f32[32,4,256]{2,1,0:T(4,128)}, f32[32,4,256]{2,1,0:T(4,128)S(1)}, u32[]{:S(2)}, u32[]{:S(2)}) collective-permute-start(f32[32,4,256]{2,1,0:T(4,128)} %get-tuple-element.365), channel_id=1, source_target_pairs={{1,0},{2,1},{3,2},{4,3},{5,4},{6,5},{7,6},{9,8},{10,9},{11,10},{12... | collective-permute-start | bytes 393224 | tf_op jit(solution)/shard_map/while/body/eval_jaxpr/ppermute | solution.py:21
  126.9 19.4 %collective-permute-start.3 = (f32[4,32,256]{2,1,0:T(8,128)}, f32[4,32,256]{2,1,0:T(8,128)S(1)}, u32[]{:S(2)}, u32[]{:S(2)}) collective-permute-start(f32[4,32,256]{2,1,0:T(8,128)} %get-tuple-element.368), channel_id=1, source_target_pairs={{8,0},{16,8},{24,16},{32,24},{40,32},{48,40},{56,48},{64,56},{72,6... | collective-permute-start | bytes 393224 | tf_op jit(solution)/shard_map/while/body/eval_jaxpr/ppermute | solution.py:21
  153.1 22.6 %collective-permute-start.1 = (f32[4,32,256]{2,1,0:T(8,128)}, f32[4,32,256]{2,1,0:T(8,128)}, u32[]{:S(2)}, u32[]{:S(2)}) collective-permute-start(f32[4,32,256]{2,1,0:T(8,128)} %get-tuple-element.363), channel_id=1, source_target_pairs={{0,8},{8,16},{16,24},{24,32},{32,40},{40,48},{48,56},{56,64},{64,7... | collective-permute-start | bytes 393224 | tf_op jit(solution)/shard_map/while/body/eval_jaxpr/ppermute | solution.py:21
  155.8 21.2 %collective-permute-start.2 = (f32[32,4,256]{2,1,0:T(4,128)}, f32[32,4,256]{2,1,0:T(4,128)S(1)}, u32[]{:S(2)}, u32[]{:S(2)}) collective-permute-start(f32[32,4,256]{2,1,0:T(4,128)} %get-tuple-element.365), channel_id=1, source_target_pairs={{1,0},{2,1},{3,2},{4,3},{5,4},{6,5},{7,6},{9,8},{10,9},{11,10},{12... | collective-permute-start | bytes 393224 | tf_op jit(solution)/shard_map/while/body/eval_jaxpr/ppermute | solution.py:21
  157.7 19.4 %collective-permute-start.3 = (f32[4,32,256]{2,1,0:T(8,128)}, f32[4,32,256]{2,1,0:T(8,128)S(1)}, u32[]{:S(2)}, u32[]{:S(2)}) collective-permute-start(f32[4,32,256]{2,1,0:T(8,128)} %get-tuple-element.368), channel_id=1, source_target_pairs={{8,0},{16,8},{24,16},{32,24},{40,32},{48,40},{56,48},{64,56},{72,6... | collective-permute-start | bytes 393224 | tf_op jit(solution)/shard_map/while/body/eval_jaxpr/ppermute | solution.py:21
  183.9 22.6 %collective-permute-start.1 = (f32[4,32,256]{2,1,0:T(8,128)}, f32[4,32,256]{2,1,0:T(8,128)}, u32[]{:S(2)}, u32[]{:S(2)}) collective-permute-start(f32[4,32,256]{2,1,0:T(8,128)} %get-tuple-element.363), channel_id=1, source_target_pairs={{0,8},{8,16},{16,24},{24,32},{32,40},{40,48},{48,56},{56,64},{64,7... | collective-permute-start | bytes 393224 | tf_op jit(solution)/shard_map/while/body/eval_jaxpr/ppermute | solution.py:21
  186.6 21.2 %collective-permute-start.2 = (f32[32,4,256]{2,1,0:T(4,128)}, f32[32,4,256]{2,1,0:T(4,128)S(1)}, u32[]{:S(2)}, u32[]{:S(2)}) collective-permute-start(f32[32,4,256]{2,1,0:T(4,128)} %get-tuple-element.365), channel_id=1, source_target_pairs={{1,0},{2,1},{3,2},{4,3},{5,4},{6,5},{7,6},{9,8},{10,9},{11,10},{12... | collective-permute-start | bytes 393224 | tf_op jit(solution)/shard_map/while/body/eval_jaxpr/ppermute | solution.py:21
  188.5 19.4 %collective-permute-start.3 = (f32[4,32,256]{2,1,0:T(8,128)}, f32[4,32,256]{2,1,0:T(8,128)S(1)}, u32[]{:S(2)}, u32[]{:S(2)}) collective-permute-start(f32[4,32,256]{2,1,0:T(8,128)} %get-tuple-element.368), channel_id=1, source_target_pairs={{8,0},{16,8},{24,16},{32,24},{40,32},{48,40},{56,48},{64,56},{72,6... | collective-permute-start | bytes 393224 | tf_op jit(solution)/shard_map/while/body/eval_jaxpr/ppermute | solution.py:21
  214.7 22.6 %collective-permute-start.1 = (f32[4,32,256]{2,1,0:T(8,128)}, f32[4,32,256]{2,1,0:T(8,128)}, u32[]{:S(2)}, u32[]{:S(2)}) collective-permute-start(f32[4,32,256]{2,1,0:T(8,128)} %get-tuple-element.363), channel_id=1, source_target_pairs={{0,8},{8,16},{16,24},{24,32},{32,40},{40,48},{48,56},{56,64},{64,7... | collective-permute-start | bytes 393224 | tf_op jit(solution)/shard_map/while/body/eval_jaxpr/ppermute | solution.py:21
  217.4 21.2 %collective-permute-start.2 = (f32[32,4,256]{2,1,0:T(4,128)}, f32[32,4,256]{2,1,0:T(4,128)S(1)}, u32[]{:S(2)}, u32[]{:S(2)}) collective-permute-start(f32[32,4,256]{2,1,0:T(4,128)} %get-tuple-element.365), channel_id=1, source_target_pairs={{1,0},{2,1},{3,2},{4,3},{5,4},{6,5},{7,6},{9,8},{10,9},{11,10},{12... | collective-permute-start | bytes 393224 | tf_op jit(solution)/shard_map/while/body/eval_jaxpr/ppermute | solution.py:21
  219.3 19.4 %collective-permute-start.3 = (f32[4,32,256]{2,1,0:T(8,128)}, f32[4,32,256]{2,1,0:T(8,128)S(1)}, u32[]{:S(2)}, u32[]{:S(2)}) collective-permute-start(f32[4,32,256]{2,1,0:T(8,128)} %get-tuple-element.368), channel_id=1, source_target_pairs={{8,0},{16,8},{24,16},{32,24},{40,32},{48,40},{56,48},{64,56},{72,6... | collective-permute-start | bytes 393224 | tf_op jit(solution)/shard_map/while/body/eval_jaxpr/ppermute | solution.py:21
  245.5 22.6 %collective-permute-start.1 = (f32[4,32,256]{2,1,0:T(8,128)}, f32[4,32,256]{2,1,0:T(8,128)}, u32[]{:S(2)}, u32[]{:S(2)}) collective-permute-start(f32[4,32,256]{2,1,0:T(8,128)} %get-tuple-element.363), channel_id=1, source_target_pairs={{0,8},{8,16},{16,24},{24,32},{32,40},{40,48},{48,56},{56,64},{64,7... | collective-permute-start | bytes 393224 | tf_op jit(solution)/shard_map/while/body/eval_jaxpr/ppermute | solution.py:21
  248.2 21.2 %collective-permute-start.2 = (f32[32,4,256]{2,1,0:T(4,128)}, f32[32,4,256]{2,1,0:T(4,128)S(1)}, u32[]{:S(2)}, u32[]{:S(2)}) collective-permute-start(f32[32,4,256]{2,1,0:T(4,128)} %get-tuple-element.365), channel_id=1, source_target_pairs={{1,0},{2,1},{3,2},{4,3},{5,4},{6,5},{7,6},{9,8},{10,9},{11,10},{12... | collective-permute-start | bytes 393224 | tf_op jit(solution)/shard_map/while/body/eval_jaxpr/ppermute | solution.py:21
  250.1 19.4 %collective-permute-start.3 = (f32[4,32,256]{2,1,0:T(8,128)}, f32[4,32,256]{2,1,0:T(8,128)S(1)}, u32[]{:S(2)}, u32[]{:S(2)}) collective-permute-start(f32[4,32,256]{2,1,0:T(8,128)} %get-tuple-element.368), channel_id=1, source_target_pairs={{8,0},{16,8},{24,16},{32,24},{40,32},{48,40},{56,48},{64,56},{72,6... | collective-permute-start | bytes 393224 | tf_op jit(solution)/shard_map/while/body/eval_jaxpr/ppermute | solution.py:21
  276.4 22.6 %collective-permute-start.1 = (f32[4,32,256]{2,1,0:T(8,128)}, f32[4,32,256]{2,1,0:T(8,128)}, u32[]{:S(2)}, u32[]{:S(2)}) collective-permute-start(f32[4,32,256]{2,1,0:T(8,128)} %get-tuple-element.363), channel_id=1, source_target_pairs={{0,8},{8,16},{16,24},{24,32},{32,40},{40,48},{48,56},{56,64},{64,7... | collective-permute-start | bytes 393224 | tf_op jit(solution)/shard_map/while/body/eval_jaxpr/ppermute | solution.py:21
  279.0 21.2 %collective-permute-start.2 = (f32[32,4,256]{2,1,0:T(4,128)}, f32[32,4,256]{2,1,0:T(4,128)S(1)}, u32[]{:S(2)}, u32[]{:S(2)}) collective-permute-start(f32[32,4,256]{2,1,0:T(4,128)} %get-tuple-element.365), channel_id=1, source_target_pairs={{1,0},{2,1},{3,2},{4,3},{5,4},{6,5},{7,6},{9,8},{10,9},{11,10},{12... | collective-permute-start | bytes 393224 | tf_op jit(solution)/shard_map/while/body/eval_jaxpr/ppermute | solution.py:21
  280.9 19.4 %collective-permute-start.3 = (f32[4,32,256]{2,1,0:T(8,128)}, f32[4,32,256]{2,1,0:T(8,128)S(1)}, u32[]{:S(2)}, u32[]{:S(2)}) collective-permute-start(f32[4,32,256]{2,1,0:T(8,128)} %get-tuple-element.368), channel_id=1, source_target_pairs={{8,0},{16,8},{24,16},{32,24},{40,32},{48,40},{56,48},{64,56},{72,6... | collective-permute-start | bytes 393224 | tf_op jit(solution)/shard_map/while/body/eval_jaxpr/ppermute | solution.py:21
  307.2 22.6 %collective-permute-start.1 = (f32[4,32,256]{2,1,0:T(8,128)}, f32[4,32,256]{2,1,0:T(8,128)}, u32[]{:S(2)}, u32[]{:S(2)}) collective-permute-start(f32[4,32,256]{2,1,0:T(8,128)} %get-tuple-element.363), channel_id=1, source_target_pairs={{0,8},{8,16},{16,24},{24,32},{32,40},{40,48},{48,56},{56,64},{64,7... | collective-permute-start | bytes 393224 | tf_op jit(solution)/shard_map/while/body/eval_jaxpr/ppermute | solution.py:21
  309.8 21.2 %collective-permute-start.2 = (f32[32,4,256]{2,1,0:T(4,128)}, f32[32,4,256]{2,1,0:T(4,128)S(1)}, u32[]{:S(2)}, u32[]{:S(2)}) collective-permute-start(f32[32,4,256]{2,1,0:T(4,128)} %get-tuple-element.365), channel_id=1, source_target_pairs={{1,0},{2,1},{3,2},{4,3},{5,4},{6,5},{7,6},{9,8},{10,9},{11,10},{12... | collective-permute-start | bytes 393224 | tf_op jit(solution)/shard_map/while/body/eval_jaxpr/ppermute | solution.py:21
  311.7 19.4 %collective-permute-start.3 = (f32[4,32,256]{2,1,0:T(8,128)}, f32[4,32,256]{2,1,0:T(8,128)S(1)}, u32[]{:S(2)}, u32[]{:S(2)}) collective-permute-start(f32[4,32,256]{2,1,0:T(8,128)} %get-tuple-element.368), channel_id=1, source_target_pairs={{8,0},{16,8},{24,16},{32,24},{40,32},{48,40},{56,48},{64,56},{72,6... | collective-permute-start | bytes 393224 | tf_op jit(solution)/shard_map/while/body/eval_jaxpr/ppermute | solution.py:21
  338.0 22.6 %collective-permute-start.1 = (f32[4,32,256]{2,1,0:T(8,128)}, f32[4,32,256]{2,1,0:T(8,128)}, u32[]{:S(2)}, u32[]{:S(2)}) collective-permute-start(f32[4,32,256]{2,1,0:T(8,128)} %get-tuple-element.363), channel_id=1, source_target_pairs={{0,8},{8,16},{16,24},{24,32},{32,40},{40,48},{48,56},{56,64},{64,7... | collective-permute-start | bytes 393224 | tf_op jit(solution)/shard_map/while/body/eval_jaxpr/ppermute | solution.py:21
  340.6 21.2 %collective-permute-start.2 = (f32[32,4,256]{2,1,0:T(4,128)}, f32[32,4,256]{2,1,0:T(4,128)S(1)}, u32[]{:S(2)}, u32[]{:S(2)}) collective-permute-start(f32[32,4,256]{2,1,0:T(4,128)} %get-tuple-element.365), channel_id=1, source_target_pairs={{1,0},{2,1},{3,2},{4,3},{5,4},{6,5},{7,6},{9,8},{10,9},{11,10},{12... | collective-permute-start | bytes 393224 | tf_op jit(solution)/shard_map/while/body/eval_jaxpr/ppermute | solution.py:21
  342.5 19.4 %collective-permute-start.3 = (f32[4,32,256]{2,1,0:T(8,128)}, f32[4,32,256]{2,1,0:T(8,128)S(1)}, u32[]{:S(2)}, u32[]{:S(2)}) collective-permute-start(f32[4,32,256]{2,1,0:T(8,128)} %get-tuple-element.368), channel_id=1, source_target_pairs={{8,0},{16,8},{24,16},{32,24},{40,32},{48,40},{56,48},{64,56},{72,6... | collective-permute-start | bytes 393224 | tf_op jit(solution)/shard_map/while/body/eval_jaxpr/ppermute | solution.py:21
  368.8 22.6 %collective-permute-start.1 = (f32[4,32,256]{2,1,0:T(8,128)}, f32[4,32,256]{2,1,0:T(8,128)}, u32[]{:S(2)}, u32[]{:S(2)}) collective-permute-start(f32[4,32,256]{2,1,0:T(8,128)} %get-tuple-element.363), channel_id=1, source_target_pairs={{0,8},{8,16},{16,24},{24,32},{32,40},{40,48},{48,56},{56,64},{64,7... | collective-permute-start | bytes 393224 | tf_op jit(solution)/shard_map/while/body/eval_jaxpr/ppermute | solution.py:21
  371.4 21.2 %collective-permute-start.2 = (f32[32,4,256]{2,1,0:T(4,128)}, f32[32,4,256]{2,1,0:T(4,128)S(1)}, u32[]{:S(2)}, u32[]{:S(2)}) collective-permute-start(f32[32,4,256]{2,1,0:T(4,128)} %get-tuple-element.365), channel_id=1, source_target_pairs={{1,0},{2,1},{3,2},{4,3},{5,4},{6,5},{7,6},{9,8},{10,9},{11,10},{12... | collective-permute-start | bytes 393224 | tf_op jit(solution)/shard_map/while/body/eval_jaxpr/ppermute | solution.py:21
  373.3 19.4 %collective-permute-start.3 = (f32[4,32,256]{2,1,0:T(8,128)}, f32[4,32,256]{2,1,0:T(8,128)S(1)}, u32[]{:S(2)}, u32[]{:S(2)}) collective-permute-start(f32[4,32,256]{2,1,0:T(8,128)} %get-tuple-element.368), channel_id=1, source_target_pairs={{8,0},{16,8},{24,16},{32,24},{40,32},{48,40},{56,48},{64,56},{72,6... | collective-permute-start | bytes 393224 | tf_op jit(solution)/shard_map/while/body/eval_jaxpr/ppermute | solution.py:21
  399.6 22.6 %collective-permute-start.1 = (f32[4,32,256]{2,1,0:T(8,128)}, f32[4,32,256]{2,1,0:T(8,128)}, u32[]{:S(2)}, u32[]{:S(2)}) collective-permute-start(f32[4,32,256]{2,1,0:T(8,128)} %get-tuple-element.363), channel_id=1, source_target_pairs={{0,8},{8,16},{16,24},{24,32},{32,40},{40,48},{48,56},{56,64},{64,7... | collective-permute-start | bytes 393224 | tf_op jit(solution)/shard_map/while/body/eval_jaxpr/ppermute | solution.py:21
  402.2 21.2 %collective-permute-start.2 = (f32[32,4,256]{2,1,0:T(4,128)}, f32[32,4,256]{2,1,0:T(4,128)S(1)}, u32[]{:S(2)}, u32[]{:S(2)}) collective-permute-start(f32[32,4,256]{2,1,0:T(4,128)} %get-tuple-element.365), channel_id=1, source_target_pairs={{1,0},{2,1},{3,2},{4,3},{5,4},{6,5},{7,6},{9,8},{10,9},{11,10},{12... | collective-permute-start | bytes 393224 | tf_op jit(solution)/shard_map/while/body/eval_jaxpr/ppermute | solution.py:21
  404.2 19.4 %collective-permute-start.3 = (f32[4,32,256]{2,1,0:T(8,128)}, f32[4,32,256]{2,1,0:T(8,128)S(1)}, u32[]{:S(2)}, u32[]{:S(2)}) collective-permute-start(f32[4,32,256]{2,1,0:T(8,128)} %get-tuple-element.368), channel_id=1, source_target_pairs={{8,0},{16,8},{24,16},{32,24},{40,32},{48,40},{56,48},{64,56},{72,6... | collective-permute-start | bytes 393224 | tf_op jit(solution)/shard_map/while/body/eval_jaxpr/ppermute | solution.py:21
  430.4 22.6 %collective-permute-start.1 = (f32[4,32,256]{2,1,0:T(8,128)}, f32[4,32,256]{2,1,0:T(8,128)}, u32[]{:S(2)}, u32[]{:S(2)}) collective-permute-start(f32[4,32,256]{2,1,0:T(8,128)} %get-tuple-element.363), channel_id=1, source_target_pairs={{0,8},{8,16},{16,24},{24,32},{32,40},{40,48},{48,56},{56,64},{64,7... | collective-permute-start | bytes 393224 | tf_op jit(solution)/shard_map/while/body/eval_jaxpr/ppermute | solution.py:21
  433.0 21.2 %collective-permute-start.2 = (f32[32,4,256]{2,1,0:T(4,128)}, f32[32,4,256]{2,1,0:T(4,128)S(1)}, u32[]{:S(2)}, u32[]{:S(2)}) collective-permute-start(f32[32,4,256]{2,1,0:T(4,128)} %get-tuple-element.365), channel_id=1, source_target_pairs={{1,0},{2,1},{3,2},{4,3},{5,4},{6,5},{7,6},{9,8},{10,9},{11,10},{12... | collective-permute-start | bytes 393224 | tf_op jit(solution)/shard_map/while/body/eval_jaxpr/ppermute | solution.py:21
  435.0 19.4 %collective-permute-start.3 = (f32[4,32,256]{2,1,0:T(8,128)}, f32[4,32,256]{2,1,0:T(8,128)S(1)}, u32[]{:S(2)}, u32[]{:S(2)}) collective-permute-start(f32[4,32,256]{2,1,0:T(8,128)} %get-tuple-element.368), channel_id=1, source_target_pairs={{8,0},{16,8},{24,16},{32,24},{40,32},{48,40},{56,48},{64,56},{72,6... | collective-permute-start | bytes 393224 | tf_op jit(solution)/shard_map/while/body/eval_jaxpr/ppermute | solution.py:21
  461.2 22.6 %collective-permute-start.1 = (f32[4,32,256]{2,1,0:T(8,128)}, f32[4,32,256]{2,1,0:T(8,128)}, u32[]{:S(2)}, u32[]{:S(2)}) collective-permute-start(f32[4,32,256]{2,1,0:T(8,128)} %get-tuple-element.363), channel_id=1, source_target_pairs={{0,8},{8,16},{16,24},{24,32},{32,40},{40,48},{48,56},{56,64},{64,7... | collective-permute-start | bytes 393224 | tf_op jit(solution)/shard_map/while/body/eval_jaxpr/ppermute | solution.py:21
  463.9 21.2 %collective-permute-start.2 = (f32[32,4,256]{2,1,0:T(4,128)}, f32[32,4,256]{2,1,0:T(4,128)S(1)}, u32[]{:S(2)}, u32[]{:S(2)}) collective-permute-start(f32[32,4,256]{2,1,0:T(4,128)} %get-tuple-element.365), channel_id=1, source_target_pairs={{1,0},{2,1},{3,2},{4,3},{5,4},{6,5},{7,6},{9,8},{10,9},{11,10},{12... | collective-permute-start | bytes 393224 | tf_op jit(solution)/shard_map/while/body/eval_jaxpr/ppermute | solution.py:21
  465.8 19.4 %collective-permute-start.3 = (f32[4,32,256]{2,1,0:T(8,128)}, f32[4,32,256]{2,1,0:T(8,128)S(1)}, u32[]{:S(2)}, u32[]{:S(2)}) collective-permute-start(f32[4,32,256]{2,1,0:T(8,128)} %get-tuple-element.368), channel_id=1, source_target_pairs={{8,0},{16,8},{24,16},{32,24},{40,32},{48,40},{56,48},{64,56},{72,6... | collective-permute-start | bytes 393224 | tf_op jit(solution)/shard_map/while/body/eval_jaxpr/ppermute | solution.py:21
  492.0 22.6 %collective-permute-start.1 = (f32[4,32,256]{2,1,0:T(8,128)}, f32[4,32,256]{2,1,0:T(8,128)}, u32[]{:S(2)}, u32[]{:S(2)}) collective-permute-start(f32[4,32,256]{2,1,0:T(8,128)} %get-tuple-element.363), channel_id=1, source_target_pairs={{0,8},{8,16},{16,24},{24,32},{32,40},{40,48},{48,56},{56,64},{64,7... | collective-permute-start | bytes 393224 | tf_op jit(solution)/shard_map/while/body/eval_jaxpr/ppermute | solution.py:21
  494.7 21.2 %collective-permute-start.2 = (f32[32,4,256]{2,1,0:T(4,128)}, f32[32,4,256]{2,1,0:T(4,128)S(1)}, u32[]{:S(2)}, u32[]{:S(2)}) collective-permute-start(f32[32,4,256]{2,1,0:T(4,128)} %get-tuple-element.365), channel_id=1, source_target_pairs={{1,0},{2,1},{3,2},{4,3},{5,4},{6,5},{7,6},{9,8},{10,9},{11,10},{12... | collective-permute-start | bytes 393224 | tf_op jit(solution)/shard_map/while/body/eval_jaxpr/ppermute | solution.py:21
  496.6 19.4 %collective-permute-start.3 = (f32[4,32,256]{2,1,0:T(8,128)}, f32[4,32,256]{2,1,0:T(8,128)S(1)}, u32[]{:S(2)}, u32[]{:S(2)}) collective-permute-start(f32[4,32,256]{2,1,0:T(8,128)} %get-tuple-element.368), channel_id=1, source_target_pairs={{8,0},{16,8},{24,16},{32,24},{40,32},{48,40},{56,48},{64,56},{72,6... | collective-permute-start | bytes 393224 | tf_op jit(solution)/shard_map/while/body/eval_jaxpr/ppermute | solution.py:21
  (140 other events, 944.1 us)

commit v3 on v2

--- a/solution.py
+++ b/solution.py
@@ -1,7 +1,13 @@
+import functools
+
 import jax
 import jax.numpy as jnp
 from jax import lax
+from jax.experimental import pallas as pl
+from jax.experimental.pallas import tpu as pltpu
 from jax.sharding import PartitionSpec as P
+
+MESH = pl.DeviceIdType.MESH
 
 STEPS = 16
 SHOTS = 16
@@ -19,6 +25,86 @@
     last = lax.slice_in_dim(value, length - HALO, length, axis=dim)
     first = lax.slice_in_dim(value, 0, HALO, axis=dim)
     return lax.ppermute(last, axis, up), lax.ppermute(first, axis, down)
+
+
+def exchange_kernel(grid_x, grid_y, cur_ref, x_lo_ref, x_hi_ref, y_lo_ref, y_hi_ref, held_x, held_y, send_sem, recv_sem):
+    me_x = lax.axis_index("gx")
+    me_y = lax.axis_index("gy")
+    width_x, width_y, _ = cur_ref.shape
+    has = (me_x > 0, me_x < grid_x - 1, me_y > 0, me_y < grid_y - 1)
+    peers = ((me_x - 1, me_y), (me_x + 1, me_y), (me_x, me_y - 1), (me_x, me_y + 1))
+    count = sum(flag.astype(jnp.int32) for flag in has)
+
+    barrier = pltpu.get_barrier_semaphore()
+    for flag, peer in zip(has, peers):
+        @pl.when(flag)
+        def _():
+            pl.semaphore_signal(barrier, inc=1, device_id=peer, device_id_type=MESH)
+    pl.semaphore_wait(barrier, count)
+
+    sources = (
+        cur_ref.at[pl.ds(0, HALO)],
+        cur_ref.at[pl.ds(width_x - HALO, HALO)],
+        cur_ref.at[:, pl.ds(0, HALO)],
+        cur_ref.at[:, pl.ds(width_y - HALO, HALO)],
+    )
+    targets = (held_x.at[1], held_x.at[0], held_y.at[1], held_y.at[0])
+    face_of = (1, 0, 3, 2)
+
+    def copy_to(side):
+        face = face_of[side]
+        return pltpu.make_async_remote_copy(
+            src_ref=sources[side],
+            dst_ref=targets[side],
+            send_sem=send_sem.at[side],
+            recv_sem=recv_sem.at[face],
+            device_id=peers[side],
+            device_id_type=MESH,
+        )
+
+    for side in range(4):
+        @pl.when(has[side])
+        def _():
+            copy_to(side).start()
+
+    for side in range(4):
+        @pl.when(has[side])
+        def _():
+            copy_to(side).wait_send()
+
+    arriving = (copy_to(1), copy_to(0), copy_to(3), copy_to(2))
+    outs = (x_lo_ref, x_hi_ref, y_lo_ref, y_hi_ref)
+    landed = (held_x.at[0], held_x.at[1], held_y.at[0], held_y.at[1])
+    for face in range(4):
+        @pl.when(has[face])
+        def _():
+            arriving[face].wait_recv()
+            outs[face][...] = landed[face][...]
+
+        @pl.when(jnp.logical_not(has[face]))
+        def _():
+            outs[face][...] = jnp.zeros(outs[face].shape, outs[face].dtype)
+
+
+def exchange(current):
+    grid_x, grid_y = lax.axis_size("gx"), lax.axis_size("gy")
+    width_x, width_y, column = current.shape
+    x_face = jax.ShapeDtypeStruct((HALO, width_y, column), current.dtype)
+    y_face = jax.ShapeDtypeStruct((width_x, HALO, column), current.dtype)
+    vmem = pl.BlockSpec(memory_space=pltpu.VMEM)
+    return pl.pallas_call(
+        functools.partial(exchange_kernel, grid_x, grid_y),
+        out_shape=(x_face, x_face, y_face, y_face),
+        in_specs=[pl.BlockSpec(memory_space=pl.ANY)],
+        out_specs=(vmem, vmem, vmem, vmem),
+        scratch_shapes=[
+            pltpu.VMEM((2, HALO, width_y, column), current.dtype),
+            pltpu.VMEM((2, width_x, HALO, column), current.dtype),
+            pltpu.SemaphoreType.DMA((4,)),
+            pltpu.SemaphoreType.DMA((4,)),
+        ],
+        compiler_params=pltpu.CompilerParams(collective_id=0, has_side_effects=True),
+    )(current)
 
 
 def split_high(value):
@@ -107,8 +193,7 @@
 
     def advance(position, carry):
         current, before, imaging = carry
-        x_lo, x_hi = faces(current, "gx", 0)
-        y_lo, y_hi = faces(current, "gy", 1)
+        x_lo, x_hi, y_lo, y_hi = exchange(current)
         piece = lax.dynamic_index_in_dim(pieces, position, 0, keepdims=False)
         spread = jnp.where(at_depth, piece[:, None], jnp.zeros((), jnp.bfloat16))
         source = lax.dot_general(

time: 528 us -> 436 us (0.83)
  starting transfers between devices: 270 us -> 10.2 us
  Pallas kernels: 0 us -> 154 us
  other arithmetic: 62.6 us -> 107 us
  matrix products: 65.1 us -> 35.1 us
    ppermute x64 -> x0, starting transfers between devices: 259 us -> none  [faces(): return (lax.ppermute(last, axis, up), lax.ppermute(first, axis, down))]
    pallas_call x0 -> x16, Pallas kernels: none -> 154 us  [exchange(): pl.pallas_call(functools.partial(exchange_kernel, grid_x, grid_y), out_sh...]
    add x16, other arithmetic: 57.2 us -> 100 us  [advance(): imaging = imaging + snapshot.astype(jnp.float32) * following]
    dot_general x16, matrix products: 63.5 us -> 33.5 us  [advance(): lax.dot_general(spread, at_plane, (((0,), (0,)), ((), ())), preferred_ele...]
    slice x32 -> x0, local copies, waits for them, and re-layouts: 24.2 us -> none  [faces(): first = lax.slice_in_dim(value, 0, HALO, axis=dim)]
    dynamic_slice x16, local copies, waits for them, and re-layouts: 0.65 us -> 17.1 us  [advance(): piece = lax.dynamic_index_in_dim(pieces, position, 0, keepdims=False)]
    transpose x16, local copies, waits for them, and re-layouts: 24.9 us -> 40.7 us  [advance(): source = lax.dot_general(spread, at_plane, (((0,), (0,)), ((), ())), pref...]
    while x288 -> x224, local copies, waits for them, and re-layouts: 59.2 us -> 52.8 us
  transfers between devices with their start and end apart: 65 -> 1, of which waited for: 1 -> 1; matrix products, arithmetic and copies ran while one was open for 23% -> 0% of each run, Pallas kernels for 0% -> 0%
where the time goes in v3:
time: 436 us; the launch traced here: 433 us
  Pallas kernels  154 us (35%)
  local copies, waits for them, and re-layouts  116 us (27%)
  other arithmetic  107 us (25%)
  matrix products  35.1 us (8%)
  starting transfers between devices  10.2 us (2%)
  waiting for transfers between devices  8.53 us (2%)
    pallas_call x16, Pallas kernels, exchange(): pl.pallas_call(functools.partial(exchange_kernel, grid_x, grid_y), out_sh...  154 us
    add x16, other arithmetic, advance(): imaging = imaging + snapshot.astype(jnp.float32) * following  100 us
    while x224, local copies, waits for them, and re-layouts  52.8 us
    transpose x16, local copies, waits for them, and re-layouts, advance(): source = lax.dot_general(spread, at_plane, (((0,), (0,)), ((), ())), pref...  40.7 us
    dot_general x16, matrix products, advance(): lax.dot_general(spread, at_plane, (((0,), (0,)), ((), ())), preferred_ele...  33.5 us
    dynamic_slice x16, local copies, waits for them, and re-layouts, advance(): piece = lax.dynamic_index_in_dim(pieces, position, 0, keepdims=False)  17.1 us
    all_to_all x1, starting transfers between devices, per_device(): lax.all_to_all(parcel, ('gx', 'gy'), split_axis=1, concat_axis=1, tiled=T...  10.2 us
  transfers between devices with their start and end apart: 1, of which 1 were waited for; matrix products, arithmetic and copies ran while one was open for 0% of the time, Pallas kernels for 0%

profile of v3, /device:TPU:38, one launch (start us, length us, event | category | flops | bytes accessed | tf_op | source)
XLA Modules:
  0.0 433.0 jit_solution(8594216014778892773)
XLA Ops:
  6.5 10.2 %all-to-all-start = ((f32[17,128,4]{0,2,1:T(4,128)}), f32[17,128,4]{0,2,1:T(4,128)S(1)}, u32[]{:S(2)}, u32[]{:S(2)}) async-start(f32[17,128,4]{0,2,1:T(4,128)} %bitcast.25), calls=%async_computation | async-start | bytes 524288 | tf_op jit(solution)/shard_map/all_to_all | solution.py:178
  16.7 8.5 %all-to-all-done = f32[17,128,4]{0,2,1:T(4,128)S(1)} async-done(((f32[17,128,4]{0,2,1:T(4,128)}), f32[17,128,4]{0,2,1:T(4,128)S(1)}, u32[]{:S(2)}, u32[]{:S(2)}) %all-to-all-start) | async-done | bytes 34848 | tf_op jit(solution)/shard_map/all_to_all | solution.py:178
  32.0 400.0 %while.19 = (s32[]{:T(128)}, f32[32,32,256]{2,1,0:T(8,128)S(1)}, f32[32,32,256]{2,1,0:T(8,128)}, f32[32,32,256]{2,1,0:T(8,128)}, bf16[16,1536]{1,0:T(8,128)(2,1)...) while((s32[]{:T(128)}, f32[32,32,256]{2,1,0:T(8,128)S(1)}, ...), condition=%wide.region_2.3_spmd, body=%wide.region_1.2_spmd.sunk | while | flops 816447488 | bytes 56370424 | solution.py:209
  32.0 10.0 %eval_jaxpr.8 = (f32[4,32,256]{2,1,0:T(8,128)}, f32[4,32,256]{2,1,0:T(8,128)}, f32[32,4,256]{2,1,0:T(4,128)}, f32[32,4,256]{2,1,0:T(4,128)}) custom-call(f32[32,32,256]{2,1,0:T(8,128)S(1)} %get-tuple-element.368.cur_ref), custom_call_target="tpu_custom_call" | custom-call | tf_op jit(solution)/shard_map/while/body/eval_jaxpr/pallas_call | solution.py:95
  47.6 2.5 copy.33
  50.1 6.3 %fusion.59 = (f32[32,32,256]{2,1,0:T(8,128)}, f32[32,32,256]{2,1,0:T(8,128)S(1)}) fusion(f32[32,32,256]{2,1,0:T(8,128)} %get-tuple-element.370, bf16[16,32,32,256]{3,2,1,0:T(8,128)(2,1)} %get-tuple-element.385, s32[]{:T(128)} %get-tuple-element.367, f32[32,32,256]{2,1,0:T(8,128)} %get-tuple-element.384, f32[32,32,256]{2,1,0:T(8,128)} %bitcast.42, ...), kind=kLoop, calls=%fused_computation.51.clone.1 | loop fusion | flops 10747904 | bytes 20578308 | tf_op jit(solution)/shard_map/while/body/eval_jaxpr/add | solution.py:206
  57.5 9.6 %eval_jaxpr.8 = (f32[4,32,256]{2,1,0:T(8,128)}, f32[4,32,256]{2,1,0:T(8,128)}, f32[32,4,256]{2,1,0:T(4,128)}, f32[32,4,256]{2,1,0:T(4,128)}) custom-call(f32[32,32,256]{2,1,0:T(8,128)S(1)} %get-tuple-element.368.cur_ref), custom_call_target="tpu_custom_call" | custom-call | tf_op jit(solution)/shard_map/while/body/eval_jaxpr/pallas_call | solution.py:95
  72.5 2.5 copy.33
  75.1 6.2 %fusion.59 = (f32[32,32,256]{2,1,0:T(8,128)}, f32[32,32,256]{2,1,0:T(8,128)S(1)}) fusion(f32[32,32,256]{2,1,0:T(8,128)} %get-tuple-element.370, bf16[16,32,32,256]{3,2,1,0:T(8,128)(2,1)} %get-tuple-element.385, s32[]{:T(128)} %get-tuple-element.367, f32[32,32,256]{2,1,0:T(8,128)} %get-tuple-element.384, f32[32,32,256]{2,1,0:T(8,128)} %bitcast.42, ...), kind=kLoop, calls=%fused_computation.51.clone.1 | loop fusion | flops 10747904 | bytes 20578308 | tf_op jit(solution)/shard_map/while/body/eval_jaxpr/add | solution.py:206
  82.4 9.6 %eval_jaxpr.8 = (f32[4,32,256]{2,1,0:T(8,128)}, f32[4,32,256]{2,1,0:T(8,128)}, f32[32,4,256]{2,1,0:T(4,128)}, f32[32,4,256]{2,1,0:T(4,128)}) custom-call(f32[32,32,256]{2,1,0:T(8,128)S(1)} %get-tuple-element.368.cur_ref), custom_call_target="tpu_custom_call" | custom-call | tf_op jit(solution)/shard_map/while/body/eval_jaxpr/pallas_call | solution.py:95
  97.5 2.5 copy.33
  100.0 6.3 %fusion.59 = (f32[32,32,256]{2,1,0:T(8,128)}, f32[32,32,256]{2,1,0:T(8,128)S(1)}) fusion(f32[32,32,256]{2,1,0:T(8,128)} %get-tuple-element.370, bf16[16,32,32,256]{3,2,1,0:T(8,128)(2,1)} %get-tuple-element.385, s32[]{:T(128)} %get-tuple-element.367, f32[32,32,256]{2,1,0:T(8,128)} %get-tuple-element.384, f32[32,32,256]{2,1,0:T(8,128)} %bitcast.42, ...), kind=kLoop, calls=%fused_computation.51.clone.1 | loop fusion | flops 10747904 | bytes 20578308 | tf_op jit(solution)/shard_map/while/body/eval_jaxpr/add | solution.py:206
  107.4 9.6 %eval_jaxpr.8 = (f32[4,32,256]{2,1,0:T(8,128)}, f32[4,32,256]{2,1,0:T(8,128)}, f32[32,4,256]{2,1,0:T(4,128)}, f32[32,4,256]{2,1,0:T(4,128)}) custom-call(f32[32,32,256]{2,1,0:T(8,128)S(1)} %get-tuple-element.368.cur_ref), custom_call_target="tpu_custom_call" | custom-call | tf_op jit(solution)/shard_map/while/body/eval_jaxpr/pallas_call | solution.py:95
  122.5 2.5 copy.33
  125.0 6.2 %fusion.59 = (f32[32,32,256]{2,1,0:T(8,128)}, f32[32,32,256]{2,1,0:T(8,128)S(1)}) fusion(f32[32,32,256]{2,1,0:T(8,128)} %get-tuple-element.370, bf16[16,32,32,256]{3,2,1,0:T(8,128)(2,1)} %get-tuple-element.385, s32[]{:T(128)} %get-tuple-element.367, f32[32,32,256]{2,1,0:T(8,128)} %get-tuple-element.384, f32[32,32,256]{2,1,0:T(8,128)} %bitcast.42, ...), kind=kLoop, calls=%fused_computation.51.clone.1 | loop fusion | flops 10747904 | bytes 20578308 | tf_op jit(solution)/shard_map/while/body/eval_jaxpr/add | solution.py:206
  132.3 9.6 %eval_jaxpr.8 = (f32[4,32,256]{2,1,0:T(8,128)}, f32[4,32,256]{2,1,0:T(8,128)}, f32[32,4,256]{2,1,0:T(4,128)}, f32[32,4,256]{2,1,0:T(4,128)}) custom-call(f32[32,32,256]{2,1,0:T(8,128)S(1)} %get-tuple-element.368.cur_ref), custom_call_target="tpu_custom_call" | custom-call | tf_op jit(solution)/shard_map/while/body/eval_jaxpr/pallas_call | solution.py:95
  147.4 2.5 copy.33
  149.9 6.3 %fusion.59 = (f32[32,32,256]{2,1,0:T(8,128)}, f32[32,32,256]{2,1,0:T(8,128)S(1)}) fusion(f32[32,32,256]{2,1,0:T(8,128)} %get-tuple-element.370, bf16[16,32,32,256]{3,2,1,0:T(8,128)(2,1)} %get-tuple-element.385, s32[]{:T(128)} %get-tuple-element.367, f32[32,32,256]{2,1,0:T(8,128)} %get-tuple-element.384, f32[32,32,256]{2,1,0:T(8,128)} %bitcast.42, ...), kind=kLoop, calls=%fused_computation.51.clone.1 | loop fusion | flops 10747904 | bytes 20578308 | tf_op jit(solution)/shard_map/while/body/eval_jaxpr/add | solution.py:206
  157.3 9.6 %eval_jaxpr.8 = (f32[4,32,256]{2,1,0:T(8,128)}, f32[4,32,256]{2,1,0:T(8,128)}, f32[32,4,256]{2,1,0:T(4,128)}, f32[32,4,256]{2,1,0:T(4,128)}) custom-call(f32[32,32,256]{2,1,0:T(8,128)S(1)} %get-tuple-element.368.cur_ref), custom_call_target="tpu_custom_call" | custom-call | tf_op jit(solution)/shard_map/while/body/eval_jaxpr/pallas_call | solution.py:95
  174.9 6.2 %fusion.59 = (f32[32,32,256]{2,1,0:T(8,128)}, f32[32,32,256]{2,1,0:T(8,128)S(1)}) fusion(f32[32,32,256]{2,1,0:T(8,128)} %get-tuple-element.370, bf16[16,32,32,256]{3,2,1,0:T(8,128)(2,1)} %get-tuple-element.385, s32[]{:T(128)} %get-tuple-element.367, f32[32,32,256]{2,1,0:T(8,128)} %get-tuple-element.384, f32[32,32,256]{2,1,0:T(8,128)} %bitcast.42, ...), kind=kLoop, calls=%fused_computation.51.clone.1 | loop fusion | flops 10747904 | bytes 20578308 | tf_op jit(solution)/shard_map/while/body/eval_jaxpr/add | solution.py:206
  182.2 9.6 %eval_jaxpr.8 = (f32[4,32,256]{2,1,0:T(8,128)}, f32[4,32,256]{2,1,0:T(8,128)}, f32[32,4,256]{2,1,0:T(4,128)}, f32[32,4,256]{2,1,0:T(4,128)}) custom-call(f32[32,32,256]{2,1,0:T(8,128)S(1)} %get-tuple-element.368.cur_ref), custom_call_target="tpu_custom_call" | custom-call | tf_op jit(solution)/shard_map/while/body/eval_jaxpr/pallas_call | solution.py:95
  197.3 2.5 copy.33
  199.9 6.3 %fusion.59 = (f32[32,32,256]{2,1,0:T(8,128)}, f32[32,32,256]{2,1,0:T(8,128)S(1)}) fusion(f32[32,32,256]{2,1,0:T(8,128)} %get-tuple-element.370, bf16[16,32,32,256]{3,2,1,0:T(8,128)(2,1)} %get-tuple-element.385, s32[]{:T(128)} %get-tuple-element.367, f32[32,32,256]{2,1,0:T(8,128)} %get-tuple-element.384, f32[32,32,256]{2,1,0:T(8,128)} %bitcast.42, ...), kind=kLoop, calls=%fused_computation.51.clone.1 | loop fusion | flops 10747904 | bytes 20578308 | tf_op jit(solution)/shard_map/while/body/eval_jaxpr/add | solution.py:206
  207.3 9.6 %eval_jaxpr.8 = (f32[4,32,256]{2,1,0:T(8,128)}, f32[4,32,256]{2,1,0:T(8,128)}, f32[32,4,256]{2,1,0:T(4,128)}, f32[32,4,256]{2,1,0:T(4,128)}) custom-call(f32[32,32,256]{2,1,0:T(8,128)S(1)} %get-tuple-element.368.cur_ref), custom_call_target="tpu_custom_call" | custom-call | tf_op jit(solution)/shard_map/while/body/eval_jaxpr/pallas_call | solution.py:95
  224.9 6.3 %fusion.59 = (f32[32,32,256]{2,1,0:T(8,128)}, f32[32,32,256]{2,1,0:T(8,128)S(1)}) fusion(f32[32,32,256]{2,1,0:T(8,128)} %get-tuple-element.370, bf16[16,32,32,256]{3,2,1,0:T(8,128)(2,1)} %get-tuple-element.385, s32[]{:T(128)} %get-tuple-element.367, f32[32,32,256]{2,1,0:T(8,128)} %get-tuple-element.384, f32[32,32,256]{2,1,0:T(8,128)} %bitcast.42, ...), kind=kLoop, calls=%fused_computation.51.clone.1 | loop fusion | flops 10747904 | bytes 20578308 | tf_op jit(solution)/shard_map/while/body/eval_jaxpr/add | solution.py:206
  232.2 9.6 %eval_jaxpr.8 = (f32[4,32,256]{2,1,0:T(8,128)}, f32[4,32,256]{2,1,0:T(8,128)}, f32[32,4,256]{2,1,0:T(4,128)}, f32[32,4,256]{2,1,0:T(4,128)}) custom-call(f32[32,32,256]{2,1,0:T(8,128)S(1)} %get-tuple-element.368.cur_ref), custom_call_target="tpu_custom_call" | custom-call | tf_op jit(solution)/shard_map/while/body/eval_jaxpr/pallas_call | solution.py:95
  247.3 2.5 copy.33
  249.9 6.2 %fusion.59 = (f32[32,32,256]{2,1,0:T(8,128)}, f32[32,32,256]{2,1,0:T(8,128)S(1)}) fusion(f32[32,32,256]{2,1,0:T(8,128)} %get-tuple-element.370, bf16[16,32,32,256]{3,2,1,0:T(8,128)(2,1)} %get-tuple-element.385, s32[]{:T(128)} %get-tuple-element.367, f32[32,32,256]{2,1,0:T(8,128)} %get-tuple-element.384, f32[32,32,256]{2,1,0:T(8,128)} %bitcast.42, ...), kind=kLoop, calls=%fused_computation.51.clone.1 | loop fusion | flops 10747904 | bytes 20578308 | tf_op jit(solution)/shard_map/while/body/eval_jaxpr/add | solution.py:206
  257.2 9.6 %eval_jaxpr.8 = (f32[4,32,256]{2,1,0:T(8,128)}, f32[4,32,256]{2,1,0:T(8,128)}, f32[32,4,256]{2,1,0:T(4,128)}, f32[32,4,256]{2,1,0:T(4,128)}) custom-call(f32[32,32,256]{2,1,0:T(8,128)S(1)} %get-tuple-element.368.cur_ref), custom_call_target="tpu_custom_call" | custom-call | tf_op jit(solution)/shard_map/while/body/eval_jaxpr/pallas_call | solution.py:95
  272.3 2.5 copy.33
  274.8 6.3 %fusion.59 = (f32[32,32,256]{2,1,0:T(8,128)}, f32[32,32,256]{2,1,0:T(8,128)S(1)}) fusion(f32[32,32,256]{2,1,0:T(8,128)} %get-tuple-element.370, bf16[16,32,32,256]{3,2,1,0:T(8,128)(2,1)} %get-tuple-element.385, s32[]{:T(128)} %get-tuple-element.367, f32[32,32,256]{2,1,0:T(8,128)} %get-tuple-element.384, f32[32,32,256]{2,1,0:T(8,128)} %bitcast.42, ...), kind=kLoop, calls=%fused_computation.51.clone.1 | loop fusion | flops 10747904 | bytes 20578308 | tf_op jit(solution)/shard_map/while/body/eval_jaxpr/add | solution.py:206
  282.2 9.6 %eval_jaxpr.8 = (f32[4,32,256]{2,1,0:T(8,128)}, f32[4,32,256]{2,1,0:T(8,128)}, f32[32,4,256]{2,1,0:T(4,128)}, f32[32,4,256]{2,1,0:T(4,128)}) custom-call(f32[32,32,256]{2,1,0:T(8,128)S(1)} %get-tuple-element.368.cur_ref), custom_call_target="tpu_custom_call" | custom-call | tf_op jit(solution)/shard_map/while/body/eval_jaxpr/pallas_call | solution.py:95
  299.8 6.3 %fusion.59 = (f32[32,32,256]{2,1,0:T(8,128)}, f32[32,32,256]{2,1,0:T(8,128)S(1)}) fusion(f32[32,32,256]{2,1,0:T(8,128)} %get-tuple-element.370, bf16[16,32,32,256]{3,2,1,0:T(8,128)(2,1)} %get-tuple-element.385, s32[]{:T(128)} %get-tuple-element.367, f32[32,32,256]{2,1,0:T(8,128)} %get-tuple-element.384, f32[32,32,256]{2,1,0:T(8,128)} %bitcast.42, ...), kind=kLoop, calls=%fused_computation.51.clone.1 | loop fusion | flops 10747904 | bytes 20578308 | tf_op jit(solution)/shard_map/while/body/eval_jaxpr/add | solution.py:206
  307.2 9.6 %eval_jaxpr.8 = (f32[4,32,256]{2,1,0:T(8,128)}, f32[4,32,256]{2,1,0:T(8,128)}, f32[32,4,256]{2,1,0:T(4,128)}, f32[32,4,256]{2,1,0:T(4,128)}) custom-call(f32[32,32,256]{2,1,0:T(8,128)S(1)} %get-tuple-element.368.cur_ref), custom_call_target="tpu_custom_call" | custom-call | tf_op jit(solution)/shard_map/while/body/eval_jaxpr/pallas_call | solution.py:95
  322.3 2.5 copy.33
  324.8 6.3 %fusion.59 = (f32[32,32,256]{2,1,0:T(8,128)}, f32[32,32,256]{2,1,0:T(8,128)S(1)}) fusion(f32[32,32,256]{2,1,0:T(8,128)} %get-tuple-element.370, bf16[16,32,32,256]{3,2,1,0:T(8,128)(2,1)} %get-tuple-element.385, s32[]{:T(128)} %get-tuple-element.367, f32[32,32,256]{2,1,0:T(8,128)} %get-tuple-element.384, f32[32,32,256]{2,1,0:T(8,128)} %bitcast.42, ...), kind=kLoop, calls=%fused_computation.51.clone.1 | loop fusion | flops 10747904 | bytes 20578308 | tf_op jit(solution)/shard_map/while/body/eval_jaxpr/add | solution.py:206
  332.2 9.6 %eval_jaxpr.8 = (f32[4,32,256]{2,1,0:T(8,128)}, f32[4,32,256]{2,1,0:T(8,128)}, f32[32,4,256]{2,1,0:T(4,128)}, f32[32,4,256]{2,1,0:T(4,128)}) custom-call(f32[32,32,256]{2,1,0:T(8,128)S(1)} %get-tuple-element.368.cur_ref), custom_call_target="tpu_custom_call" | custom-call | tf_op jit(solution)/shard_map/while/body/eval_jaxpr/pallas_call | solution.py:95
  347.3 2.5 copy.33
  349.8 6.2 %fusion.59 = (f32[32,32,256]{2,1,0:T(8,128)}, f32[32,32,256]{2,1,0:T(8,128)S(1)}) fusion(f32[32,32,256]{2,1,0:T(8,128)} %get-tuple-element.370, bf16[16,32,32,256]{3,2,1,0:T(8,128)(2,1)} %get-tuple-element.385, s32[]{:T(128)} %get-tuple-element.367, f32[32,32,256]{2,1,0:T(8,128)} %get-tuple-element.384, f32[32,32,256]{2,1,0:T(8,128)} %bitcast.42, ...), kind=kLoop, calls=%fused_computation.51.clone.1 | loop fusion | flops 10747904 | bytes 20578308 | tf_op jit(solution)/shard_map/while/body/eval_jaxpr/add | solution.py:206
  357.1 9.6 %eval_jaxpr.8 = (f32[4,32,256]{2,1,0:T(8,128)}, f32[4,32,256]{2,1,0:T(8,128)}, f32[32,4,256]{2,1,0:T(4,128)}, f32[32,4,256]{2,1,0:T(4,128)}) custom-call(f32[32,32,256]{2,1,0:T(8,128)S(1)} %get-tuple-element.368.cur_ref), custom_call_target="tpu_custom_call" | custom-call | tf_op jit(solution)/shard_map/while/body/eval_jaxpr/pallas_call | solution.py:95
  372.2 2.5 copy.33
  374.8 6.3 %fusion.59 = (f32[32,32,256]{2,1,0:T(8,128)}, f32[32,32,256]{2,1,0:T(8,128)S(1)}) fusion(f32[32,32,256]{2,1,0:T(8,128)} %get-tuple-element.370, bf16[16,32,32,256]{3,2,1,0:T(8,128)(2,1)} %get-tuple-element.385, s32[]{:T(128)} %get-tuple-element.367, f32[32,32,256]{2,1,0:T(8,128)} %get-tuple-element.384, f32[32,32,256]{2,1,0:T(8,128)} %bitcast.42, ...), kind=kLoop, calls=%fused_computation.51.clone.1 | loop fusion | flops 10747904 | bytes 20578308 | tf_op jit(solution)/shard_map/while/body/eval_jaxpr/add | solution.py:206
  382.1 9.6 %eval_jaxpr.8 = (f32[4,32,256]{2,1,0:T(8,128)}, f32[4,32,256]{2,1,0:T(8,128)}, f32[32,4,256]{2,1,0:T(4,128)}, f32[32,4,256]{2,1,0:T(4,128)}) custom-call(f32[32,32,256]{2,1,0:T(8,128)S(1)} %get-tuple-element.368.cur_ref), custom_call_target="tpu_custom_call" | custom-call | tf_op jit(solution)/shard_map/while/body/eval_jaxpr/pallas_call | solution.py:95
  397.2 2.5 copy.33
  399.8 6.2 %fusion.59 = (f32[32,32,256]{2,1,0:T(8,128)}, f32[32,32,256]{2,1,0:T(8,128)S(1)}) fusion(f32[32,32,256]{2,1,0:T(8,128)} %get-tuple-element.370, bf16[16,32,32,256]{3,2,1,0:T(8,128)(2,1)} %get-tuple-element.385, s32[]{:T(128)} %get-tuple-element.367, f32[32,32,256]{2,1,0:T(8,128)} %get-tuple-element.384, f32[32,32,256]{2,1,0:T(8,128)} %bitcast.42, ...), kind=kLoop, calls=%fused_computation.51.clone.1 | loop fusion | flops 10747904 | bytes 20578308 | tf_op jit(solution)/shard_map/while/body/eval_jaxpr/add | solution.py:206
  407.1 9.6 %eval_jaxpr.8 = (f32[4,32,256]{2,1,0:T(8,128)}, f32[4,32,256]{2,1,0:T(8,128)}, f32[32,4,256]{2,1,0:T(4,128)}, f32[32,4,256]{2,1,0:T(4,128)}) custom-call(f32[32,32,256]{2,1,0:T(8,128)S(1)} %get-tuple-element.368.cur_ref), custom_call_target="tpu_custom_call" | custom-call | tf_op jit(solution)/shard_map/while/body/eval_jaxpr/pallas_call | solution.py:95
  422.2 2.5 copy.33
  424.7 6.3 %fusion.59 = (f32[32,32,256]{2,1,0:T(8,128)}, f32[32,32,256]{2,1,0:T(8,128)S(1)}) fusion(f32[32,32,256]{2,1,0:T(8,128)} %get-tuple-element.370, bf16[16,32,32,256]{3,2,1,0:T(8,128)(2,1)} %get-tuple-element.385, s32[]{:T(128)} %get-tuple-element.367, f32[32,32,256]{2,1,0:T(8,128)} %get-tuple-element.384, f32[32,32,256]{2,1,0:T(8,128)} %bitcast.42, ...), kind=kLoop, calls=%fused_computation.51.clone.1 | loop fusion | flops 10747904 | bytes 20578308 | tf_op jit(solution)/shard_map/while/body/eval_jaxpr/add | solution.py:206
  (331 shorter events, 125.1 us)
Async XLA Ops:
  0.6 3.8 copy-start
  0.6 1.2 copy-start.8
  1.9 1.6 copy-start.9
  3.5 1.3 copy-start.12
  3.5 1.5 copy-start.13
  3.5 1.5 copy-start.7
  3.5 1.5 copy-start.11
  6.5 18.7 %all-to-all-start = ((f32[17,128,4]{0,2,1:T(4,128)}), f32[17,128,4]{0,2,1:T(4,128)S(1)}, u32[]{:S(2)}, u32[]{:S(2)}) async-start(f32[17,128,4]{0,2,1:T(4,128)} %bitcast.25), calls=%async_computation | async-start | bytes 524288 | tf_op jit(solution)/shard_map/all_to_all | solution.py:178
  28.1 3.9 copy-start.2
  43.0 2.5 copy-start.6
  43.0 2.5 copy-start.10
  43.2 1.0 copy-start.3
  68.0 2.5 copy-start.6
  68.0 2.5 copy-start.10
  92.9 2.5 copy-start.6
  92.9 2.5 copy-start.10
  93.2 1.0 copy-start.3
  117.9 2.5 copy-start.6
  117.9 2.5 copy-start.10
  142.8 2.5 copy-start.6
  142.8 2.5 copy-start.10
  143.1 1.0 copy-start.3
  167.8 2.5 copy-start.6
  167.8 2.5 copy-start.10
  192.7 2.5 copy-start.6
  192.8 2.5 copy-start.10
  217.8 2.5 copy-start.6
  217.8 2.5 copy-start.10
  218.1 1.0 copy-start.3
  242.8 2.5 copy-start.6
  242.8 2.5 copy-start.10
  267.7 2.5 copy-start.6
  267.7 2.5 copy-start.10
  268.0 1.0 copy-start.3
  292.7 2.5 copy-start.6
  292.7 2.5 copy-start.10
  293.0 1.0 copy-start.3
  317.7 2.5 copy-start.6
  317.7 2.5 copy-start.10
  318.0 1.0 copy-start.3
  342.7 2.5 copy-start.6
  342.7 2.5 copy-start.10
  367.7 2.5 copy-start.6
  367.7 2.5 copy-start.10
  392.6 2.5 copy-start.6
  392.6 2.5 copy-start.10
  417.6 2.5 copy-start.6
  417.6 2.5 copy-start.10
  (43 other events, 41.0 us)

commit v4 on v3

--- a/solution.py
+++ b/solution.py
@@ -27,14 +27,22 @@
     return lax.ppermute(last, axis, up), lax.ppermute(first, axis, down)
 
 
-def exchange_kernel(grid_x, grid_y, cur_ref, x_lo_ref, x_hi_ref, y_lo_ref, y_hi_ref, held_x, held_y, send_sem, recv_sem):
+def step_kernel(
+    grid_x, grid_y, cur_ref, prev_ref, courant_ref, snap_ref, image_ref, source_ref,
+    next_ref, image_out_ref, ext_x, ext_y, send_sem, recv_sem, local_sem,
+):
     me_x = lax.axis_index("gx")
     me_y = lax.axis_index("gy")
-    width_x, width_y, _ = cur_ref.shape
+    width_x, width_y, column = cur_ref.shape
     has = (me_x > 0, me_x < grid_x - 1, me_y > 0, me_y < grid_y - 1)
     peers = ((me_x - 1, me_y), (me_x + 1, me_y), (me_x, me_y - 1), (me_x, me_y + 1))
     count = sum(flag.astype(jnp.int32) for flag in has)
 
+    center_x = pltpu.make_async_copy(cur_ref, ext_x.at[pl.ds(HALO, width_x)], local_sem.at[0])
+    center_y = pltpu.make_async_copy(cur_ref, ext_y.at[:, pl.ds(2 * HALO, width_y)], local_sem.at[1])
+    center_x.start()
+    center_y.start()
+
     barrier = pltpu.get_barrier_semaphore()
     for flag, peer in zip(has, peers):
         @pl.when(flag)
@@ -42,22 +50,27 @@
             pl.semaphore_signal(barrier, inc=1, device_id=peer, device_id_type=MESH)
     pl.semaphore_wait(barrier, count)
 
-    sources = (
+    zones = (
+        ext_x.at[pl.ds(0, HALO)],
+        ext_x.at[pl.ds(HALO + width_x, HALO)],
+        ext_y.at[:, pl.ds(HALO, HALO)],
+        ext_y.at[:, pl.ds(2 * HALO + width_y, HALO)],
+    )
+    faces = (
         cur_ref.at[pl.ds(0, HALO)],
         cur_ref.at[pl.ds(width_x - HALO, HALO)],
         cur_ref.at[:, pl.ds(0, HALO)],
         cur_ref.at[:, pl.ds(width_y - HALO, HALO)],
     )
-    targets = (held_x.at[1], held_x.at[0], held_y.at[1], held_y.at[0])
-    face_of = (1, 0, 3, 2)
+    zone_of = (1, 0, 3, 2)
 
     def copy_to(side):
-        face = face_of[side]
+        zone = zone_of[side]
         return pltpu.make_async_remote_copy(
-            src_ref=sources[side],
-            dst_ref=targets[side],
+            src_ref=faces[side],
+            dst_ref=zones[zone],
             send_sem=send_sem.at[side],
-            recv_sem=recv_sem.at[face],
+            recv_sem=recv_sem.at[zone],
             device_id=peers[side],
             device_id_type=MESH,
         )
@@ -67,44 +80,67 @@
         def _():
             copy_to(side).start()
 
+    arriving = (copy_to(1), copy_to(0), copy_to(3), copy_to(2))
+    for zone in range(4):
+        @pl.when(has[zone])
+        def _():
+            arriving[zone].wait_recv()
+
+        @pl.when(jnp.logical_not(has[zone]))
+        def _():
+            zones[zone][...] = jnp.zeros(zones[zone].shape, jnp.float32)
+
+    center_x.wait()
+    center_y.wait()
+
+    lane = lax.broadcasted_iota(jnp.int32, (width_y, column), 1)
+
+    def row(x, carry):
+        center = ext_x[x + HALO]
+        summed = 3.0 * stencil_weights[0] * center
+        for offset in range(1, 5):
+            along_x = ext_x[x + HALO + offset] + ext_x[x + HALO - offset]
+            along_y = (
+                ext_y[x, pl.ds(2 * HALO + offset, width_y), :]
+                + ext_y[x, pl.ds(2 * HALO - offset, width_y), :]
+            )
+            above = jnp.where(lane < column - offset, pltpu.roll(center, column - offset, 1), 0.0)
+            below = jnp.where(lane >= offset, pltpu.roll(center, offset, 1), 0.0)
+            summed = summed + stencil_weights[offset] * (along_x + along_y + (above + below))
+        following = 2.0 * center - prev_ref[x] + courant_ref[x] * (summed + source_ref[x])
+        next_ref[x] = following
+        image_out_ref[x] = image_ref[x] + snap_ref[x].astype(jnp.float32) * following
+        return carry
+
+    lax.fori_loop(0, width_x, row, 0)
+
     for side in range(4):
         @pl.when(has[side])
         def _():
             copy_to(side).wait_send()
 
-    arriving = (copy_to(1), copy_to(0), copy_to(3), copy_to(2))
-    outs = (x_lo_ref, x_hi_ref, y_lo_ref, y_hi_ref)
-    landed = (held_x.at[0], held_x.at[1], held_y.at[0], held_y.at[1])
-    for face in range(4):
-        @pl.when(has[face])
-        def _():
-            arriving[face].wait_recv()
-            outs[face][...] = landed[face][...]
-
-        @pl.when(jnp.logical_not(has[face]))
-        def _():
-            outs[face][...] = jnp.zeros(outs[face].shape, outs[face].dtype)
-
-
-def exchange(current):
+
+def fused_step(current, before, courant, snapshot, imaging, source):
     grid_x, grid_y = lax.axis_size("gx"), lax.axis_size("gy")
     width_x, width_y, column = current.shape
-    x_face = jax.ShapeDtypeStruct((HALO, width_y, column), current.dtype)
-    y_face = jax.ShapeDtypeStruct((width_x, HALO, column), current.dtype)
+    field = jax.ShapeDtypeStruct(current.shape, jnp.float32)
     vmem = pl.BlockSpec(memory_space=pltpu.VMEM)
     return pl.pallas_call(
-        functools.partial(exchange_kernel, grid_x, grid_y),
-        out_shape=(x_face, x_face, y_face, y_face),
-        in_specs=[pl.BlockSpec(memory_space=pl.ANY)],
-        out_specs=(vmem, vmem, vmem, vmem),
+        functools.partial(step_kernel, grid_x, grid_y),
+        out_shape=(field, field),
+        in_specs=[vmem] * 6,
+        out_specs=(vmem, vmem),
         scratch_shapes=[
-            pltpu.VMEM((2, HALO, width_y, column), current.dtype),
-            pltpu.VMEM((2, width_x, HALO, column), current.dtype),
+            pltpu.VMEM((width_x + 2 * HALO, width_y, column), jnp.float32),
+            pltpu.VMEM((width_x, width_y + 4 * HALO, column), jnp.float32),
             pltpu.SemaphoreType.DMA((4,)),
             pltpu.SemaphoreType.DMA((4,)),
+            pltpu.SemaphoreType.DMA((2,)),
         ],
-        compiler_params=pltpu.CompilerParams(collective_id=0, has_side_effects=True),
-    )(current)
+        compiler_params=pltpu.CompilerParams(
+            collective_id=0, has_side_effects=True, vmem_limit_bytes=48 * 1024 * 1024
+        ),
+    )(current, before, courant, snapshot, imaging, source)
 
 
 def split_high(value):
@@ -193,17 +229,13 @@
 
     def advance(position, carry):
         current, before, imaging = carry
-        x_lo, x_hi, y_lo, y_hi = exchange(current)
         piece = lax.dynamic_index_in_dim(pieces, position, 0, keepdims=False)
         spread = jnp.where(at_depth, piece[:, None], jnp.zeros((), jnp.bfloat16))
         source = lax.dot_general(
             spread, at_plane, (((0,), (0,)), ((), ())), preferred_element_type=jnp.float32
         ).T.reshape(current.shape)
-        following = 2.0 * current - before + courant * (
-            laplace(current, x_lo, x_hi, y_lo, y_hi) + source
-        )
         snapshot = lax.dynamic_index_in_dim(forward_field, position, 0, keepdims=False)
-        imaging = imaging + snapshot.astype(jnp.float32) * following
+        following, imaging = fused_step(current, before, courant, snapshot, imaging, source)
         return (following, current, imaging)
 
     current, before, imaging = lax.fori_loop(

time: 436 us -> 425 us (0.975)
  Pallas kernels: 154 us -> 267 us
  other arithmetic: 107 us -> 5.39 us
  local copies, waits for them, and re-layouts: 116 us -> 94.6 us
    pallas_call x16, Pallas kernels: 154 us -> 267 us  [fused_step(): pl.pallas_call(functools.partial(step_kernel, grid_x, grid_y), out_shape=...]
    add x16 -> x0, other arithmetic: 100 us -> none  [advance(): imaging = imaging + snapshot.astype(jnp.float32) * following]
    squeeze x0 -> x16, local copies, waits for them, and re-layouts: none -> 19.7 us  [advance(): lax.dynamic_index_in_dim(forward_field, position, 0, keepdims=False)]
    dynamic_slice x16, local copies, waits for them, and re-layouts: 17.1 us -> 0.65 us  [advance(): piece = lax.dynamic_index_in_dim(pieces, position, 0, keepdims=False)]
    transpose x16, local copies, waits for them, and re-layouts: 40.7 us -> 24.9 us  [advance(): source = lax.dot_general(spread, at_plane, (((0,), (0,)), ((), ())), pref...]
    while x224 -> x144, local copies, waits for them, and re-layouts: 52.8 us -> 43.4 us
where the time goes in v4:
time: 425 us; the launch traced here: 423 us
  Pallas kernels  267 us (63%)
  local copies, waits for them, and re-layouts  94.6 us (22%)
  matrix products  35.2 us (8%)
  starting transfers between devices  10.2 us (2%)
  waiting for transfers between devices  8.53 us (2%)
  other arithmetic  5.39 us (1%)
    pallas_call x16, Pallas kernels, fused_step(): pl.pallas_call(functools.partial(step_kernel, grid_x, grid_y), out_shape=...  267 us
    while x144, local copies, waits for them, and re-layouts  43.4 us
    dot_general x16, matrix products, advance(): lax.dot_general(spread, at_plane, (((0,), (0,)), ((), ())), preferred_ele...  33.5 us
    transpose x16, local copies, waits for them, and re-layouts, advance(): source = lax.dot_general(spread, at_plane, (((0,), (0,)), ((), ())), pref...  24.9 us
    squeeze x16, local copies, waits for them, and re-layouts, advance(): lax.dynamic_index_in_dim(forward_field, position, 0, keepdims=False)  19.7 us
    all_to_all x1, starting transfers between devices, per_device(): lax.all_to_all(parcel, ('gx', 'gy'), split_axis=1, concat_axis=1, tiled=T...  10.2 us
    all_to_all x1, waiting for transfers between devices, per_device(): lax.all_to_all(parcel, ('gx', 'gy'), split_axis=1, concat_axis=1, tiled=T...  8.53 us
  transfers between devices with their start and end apart: 1, of which 1 were waited for; matrix products, arithmetic and copies ran while one was open for 0% of the time, Pallas kernels for 0%

profile of v4, /device:TPU:38, one launch (start us, length us, event | category | flops | bytes accessed | tf_op | source)
XLA Modules:
  0.0 422.5 jit_solution(9585363715512728713)
XLA Ops:
  0.7 2.3 copy.56
  3.0 2.3 copy.57
  7.3 10.2 %all-to-all-start = ((f32[17,128,4]{0,2,1:T(4,128)}), f32[17,128,4]{0,2,1:T(4,128)S(1)}, u32[]{:S(2)}, u32[]{:S(2)}) async-start(f32[17,128,4]{0,2,1:T(4,128)} %bitcast.25), calls=%async_computation | async-start | bytes 524288 | tf_op jit(solution)/shard_map/all_to_all | solution.py:214
  17.5 8.5 %all-to-all-done = f32[17,128,4]{0,2,1:T(4,128)S(1)} async-done(((f32[17,128,4]{0,2,1:T(4,128)}), f32[17,128,4]{0,2,1:T(4,128)S(1)}, u32[]{:S(2)}, u32[]{:S(2)}) %all-to-all-start) | async-done | bytes 34848 | tf_op jit(solution)/shard_map/all_to_all | solution.py:214
  26.3 2.4 fusion.5
  29.4 2.1 add_convert_fusion
  31.5 390.0 %while.17 = (s32[]{:T(128)}, f32[32,32,256]{2,1,0:T(8,128)}, f32[32,32,256]{2,1,0:T(8,128)}, f32[32,32,256]{2,1,0:T(8,128)S(1)}, bf16[16,32,32,256]{3,2,1,0:T(8,...) while((s32[]{:T(128)}, f32[32,32,256]{2,1,0:T(8,128)}, ...), condition=%wide.region_2.3_spmd, body=%wide.region_1.2_spmd.sunk | while | flops 805699584 | bytes 35005640 | solution.py:241
  33.6 2.1 convolution_bitcast_fusion.3
  35.7 1.6 copy.33
  37.3 17.2 %eval_jaxpr.5 = (f32[32,32,256]{2,1,0:T(8,128)S(1)}, f32[32,32,256]{2,1,0:T(8,128)}) custom-call(f32[32,32,256]{2,1,0:T(8,128)} %get-tuple-element.277.cur_ref, f32[32,32,256]{2,1,0:T(8,128)} %get-tuple-element.278.prev_ref, f32[32,32,256]{2,1,0:T(8,128)} %get-tuple-element.294.courant_ref, bf16[32,32,256]{2,1,0:T(8,128)(2,1)S(1)} %dynamic-slice_bitcast_fusion.2.snap_ref, ...), custom_call_target="tpu_custom_call" | custom-call | tf_op jit(solution)/shard_map/while/body/eval_jaxpr/pallas_call | solution.py:128
  58.5 2.1 convolution_bitcast_fusion.3
  60.6 1.6 copy.33
  62.2 16.6 %eval_jaxpr.5 = (f32[32,32,256]{2,1,0:T(8,128)S(1)}, f32[32,32,256]{2,1,0:T(8,128)}) custom-call(f32[32,32,256]{2,1,0:T(8,128)} %get-tuple-element.277.cur_ref, f32[32,32,256]{2,1,0:T(8,128)} %get-tuple-element.278.prev_ref, f32[32,32,256]{2,1,0:T(8,128)} %get-tuple-element.294.courant_ref, bf16[32,32,256]{2,1,0:T(8,128)(2,1)S(1)} %dynamic-slice_bitcast_fusion.2.snap_ref, ...), custom_call_target="tpu_custom_call" | custom-call | tf_op jit(solution)/shard_map/while/body/eval_jaxpr/pallas_call | solution.py:128
  82.8 2.1 convolution_bitcast_fusion.3
  84.9 1.6 copy.33
  86.5 16.6 %eval_jaxpr.5 = (f32[32,32,256]{2,1,0:T(8,128)S(1)}, f32[32,32,256]{2,1,0:T(8,128)}) custom-call(f32[32,32,256]{2,1,0:T(8,128)} %get-tuple-element.277.cur_ref, f32[32,32,256]{2,1,0:T(8,128)} %get-tuple-element.278.prev_ref, f32[32,32,256]{2,1,0:T(8,128)} %get-tuple-element.294.courant_ref, bf16[32,32,256]{2,1,0:T(8,128)(2,1)S(1)} %dynamic-slice_bitcast_fusion.2.snap_ref, ...), custom_call_target="tpu_custom_call" | custom-call | tf_op jit(solution)/shard_map/while/body/eval_jaxpr/pallas_call | solution.py:128
  107.2 2.1 convolution_bitcast_fusion.3
  109.3 1.6 copy.33
  110.9 16.6 %eval_jaxpr.5 = (f32[32,32,256]{2,1,0:T(8,128)S(1)}, f32[32,32,256]{2,1,0:T(8,128)}) custom-call(f32[32,32,256]{2,1,0:T(8,128)} %get-tuple-element.277.cur_ref, f32[32,32,256]{2,1,0:T(8,128)} %get-tuple-element.278.prev_ref, f32[32,32,256]{2,1,0:T(8,128)} %get-tuple-element.294.courant_ref, bf16[32,32,256]{2,1,0:T(8,128)(2,1)S(1)} %dynamic-slice_bitcast_fusion.2.snap_ref, ...), custom_call_target="tpu_custom_call" | custom-call | tf_op jit(solution)/shard_map/while/body/eval_jaxpr/pallas_call | solution.py:128
  131.5 2.1 convolution_bitcast_fusion.3
  133.6 1.6 copy.33
  135.2 16.6 %eval_jaxpr.5 = (f32[32,32,256]{2,1,0:T(8,128)S(1)}, f32[32,32,256]{2,1,0:T(8,128)}) custom-call(f32[32,32,256]{2,1,0:T(8,128)} %get-tuple-element.277.cur_ref, f32[32,32,256]{2,1,0:T(8,128)} %get-tuple-element.278.prev_ref, f32[32,32,256]{2,1,0:T(8,128)} %get-tuple-element.294.courant_ref, bf16[32,32,256]{2,1,0:T(8,128)(2,1)S(1)} %dynamic-slice_bitcast_fusion.2.snap_ref, ...), custom_call_target="tpu_custom_call" | custom-call | tf_op jit(solution)/shard_map/while/body/eval_jaxpr/pallas_call | solution.py:128
  155.9 2.1 convolution_bitcast_fusion.3
  158.0 1.6 copy.33
  159.5 16.6 %eval_jaxpr.5 = (f32[32,32,256]{2,1,0:T(8,128)S(1)}, f32[32,32,256]{2,1,0:T(8,128)}) custom-call(f32[32,32,256]{2,1,0:T(8,128)} %get-tuple-element.277.cur_ref, f32[32,32,256]{2,1,0:T(8,128)} %get-tuple-element.278.prev_ref, f32[32,32,256]{2,1,0:T(8,128)} %get-tuple-element.294.courant_ref, bf16[32,32,256]{2,1,0:T(8,128)(2,1)S(1)} %dynamic-slice_bitcast_fusion.2.snap_ref, ...), custom_call_target="tpu_custom_call" | custom-call | tf_op jit(solution)/shard_map/while/body/eval_jaxpr/pallas_call | solution.py:128
  180.2 2.1 convolution_bitcast_fusion.3
  182.3 1.6 copy.33
  183.9 16.6 %eval_jaxpr.5 = (f32[32,32,256]{2,1,0:T(8,128)S(1)}, f32[32,32,256]{2,1,0:T(8,128)}) custom-call(f32[32,32,256]{2,1,0:T(8,128)} %get-tuple-element.277.cur_ref, f32[32,32,256]{2,1,0:T(8,128)} %get-tuple-element.278.prev_ref, f32[32,32,256]{2,1,0:T(8,128)} %get-tuple-element.294.courant_ref, bf16[32,32,256]{2,1,0:T(8,128)(2,1)S(1)} %dynamic-slice_bitcast_fusion.2.snap_ref, ...), custom_call_target="tpu_custom_call" | custom-call | tf_op jit(solution)/shard_map/while/body/eval_jaxpr/pallas_call | solution.py:128
  204.6 2.1 convolution_bitcast_fusion.3
  208.2 16.6 %eval_jaxpr.5 = (f32[32,32,256]{2,1,0:T(8,128)S(1)}, f32[32,32,256]{2,1,0:T(8,128)}) custom-call(f32[32,32,256]{2,1,0:T(8,128)} %get-tuple-element.277.cur_ref, f32[32,32,256]{2,1,0:T(8,128)} %get-tuple-element.278.prev_ref, f32[32,32,256]{2,1,0:T(8,128)} %get-tuple-element.294.courant_ref, bf16[32,32,256]{2,1,0:T(8,128)(2,1)S(1)} %dynamic-slice_bitcast_fusion.2.snap_ref, ...), custom_call_target="tpu_custom_call" | custom-call | tf_op jit(solution)/shard_map/while/body/eval_jaxpr/pallas_call | solution.py:128
  228.9 2.1 convolution_bitcast_fusion.3
  231.0 1.6 copy.33
  232.6 16.6 %eval_jaxpr.5 = (f32[32,32,256]{2,1,0:T(8,128)S(1)}, f32[32,32,256]{2,1,0:T(8,128)}) custom-call(f32[32,32,256]{2,1,0:T(8,128)} %get-tuple-element.277.cur_ref, f32[32,32,256]{2,1,0:T(8,128)} %get-tuple-element.278.prev_ref, f32[32,32,256]{2,1,0:T(8,128)} %get-tuple-element.294.courant_ref, bf16[32,32,256]{2,1,0:T(8,128)(2,1)S(1)} %dynamic-slice_bitcast_fusion.2.snap_ref, ...), custom_call_target="tpu_custom_call" | custom-call | tf_op jit(solution)/shard_map/while/body/eval_jaxpr/pallas_call | solution.py:128
  253.2 2.1 convolution_bitcast_fusion.3
  256.9 16.6 %eval_jaxpr.5 = (f32[32,32,256]{2,1,0:T(8,128)S(1)}, f32[32,32,256]{2,1,0:T(8,128)}) custom-call(f32[32,32,256]{2,1,0:T(8,128)} %get-tuple-element.277.cur_ref, f32[32,32,256]{2,1,0:T(8,128)} %get-tuple-element.278.prev_ref, f32[32,32,256]{2,1,0:T(8,128)} %get-tuple-element.294.courant_ref, bf16[32,32,256]{2,1,0:T(8,128)(2,1)S(1)} %dynamic-slice_bitcast_fusion.2.snap_ref, ...), custom_call_target="tpu_custom_call" | custom-call | tf_op jit(solution)/shard_map/while/body/eval_jaxpr/pallas_call | solution.py:128
  277.6 2.1 convolution_bitcast_fusion.3
  281.2 16.6 %eval_jaxpr.5 = (f32[32,32,256]{2,1,0:T(8,128)S(1)}, f32[32,32,256]{2,1,0:T(8,128)}) custom-call(f32[32,32,256]{2,1,0:T(8,128)} %get-tuple-element.277.cur_ref, f32[32,32,256]{2,1,0:T(8,128)} %get-tuple-element.278.prev_ref, f32[32,32,256]{2,1,0:T(8,128)} %get-tuple-element.294.courant_ref, bf16[32,32,256]{2,1,0:T(8,128)(2,1)S(1)} %dynamic-slice_bitcast_fusion.2.snap_ref, ...), custom_call_target="tpu_custom_call" | custom-call | tf_op jit(solution)/shard_map/while/body/eval_jaxpr/pallas_call | solution.py:128
  301.9 2.1 convolution_bitcast_fusion.3
  305.6 16.6 %eval_jaxpr.5 = (f32[32,32,256]{2,1,0:T(8,128)S(1)}, f32[32,32,256]{2,1,0:T(8,128)}) custom-call(f32[32,32,256]{2,1,0:T(8,128)} %get-tuple-element.277.cur_ref, f32[32,32,256]{2,1,0:T(8,128)} %get-tuple-element.278.prev_ref, f32[32,32,256]{2,1,0:T(8,128)} %get-tuple-element.294.courant_ref, bf16[32,32,256]{2,1,0:T(8,128)(2,1)S(1)} %dynamic-slice_bitcast_fusion.2.snap_ref, ...), custom_call_target="tpu_custom_call" | custom-call | tf_op jit(solution)/shard_map/while/body/eval_jaxpr/pallas_call | solution.py:128
  326.3 2.1 convolution_bitcast_fusion.3
  329.9 16.6 %eval_jaxpr.5 = (f32[32,32,256]{2,1,0:T(8,128)S(1)}, f32[32,32,256]{2,1,0:T(8,128)}) custom-call(f32[32,32,256]{2,1,0:T(8,128)} %get-tuple-element.277.cur_ref, f32[32,32,256]{2,1,0:T(8,128)} %get-tuple-element.278.prev_ref, f32[32,32,256]{2,1,0:T(8,128)} %get-tuple-element.294.courant_ref, bf16[32,32,256]{2,1,0:T(8,128)(2,1)S(1)} %dynamic-slice_bitcast_fusion.2.snap_ref, ...), custom_call_target="tpu_custom_call" | custom-call | tf_op jit(solution)/shard_map/while/body/eval_jaxpr/pallas_call | solution.py:128
  350.6 2.1 convolution_bitcast_fusion.3
  352.7 1.6 copy.33
  354.3 16.6 %eval_jaxpr.5 = (f32[32,32,256]{2,1,0:T(8,128)S(1)}, f32[32,32,256]{2,1,0:T(8,128)}) custom-call(f32[32,32,256]{2,1,0:T(8,128)} %get-tuple-element.277.cur_ref, f32[32,32,256]{2,1,0:T(8,128)} %get-tuple-element.278.prev_ref, f32[32,32,256]{2,1,0:T(8,128)} %get-tuple-element.294.courant_ref, bf16[32,32,256]{2,1,0:T(8,128)(2,1)S(1)} %dynamic-slice_bitcast_fusion.2.snap_ref, ...), custom_call_target="tpu_custom_call" | custom-call | tf_op jit(solution)/shard_map/while/body/eval_jaxpr/pallas_call | solution.py:128
  374.9 2.1 convolution_bitcast_fusion.3
  378.6 16.6 %eval_jaxpr.5 = (f32[32,32,256]{2,1,0:T(8,128)S(1)}, f32[32,32,256]{2,1,0:T(8,128)}) custom-call(f32[32,32,256]{2,1,0:T(8,128)} %get-tuple-element.277.cur_ref, f32[32,32,256]{2,1,0:T(8,128)} %get-tuple-element.278.prev_ref, f32[32,32,256]{2,1,0:T(8,128)} %get-tuple-element.294.courant_ref, bf16[32,32,256]{2,1,0:T(8,128)(2,1)S(1)} %dynamic-slice_bitcast_fusion.2.snap_ref, ...), custom_call_target="tpu_custom_call" | custom-call | tf_op jit(solution)/shard_map/while/body/eval_jaxpr/pallas_call | solution.py:128
  399.3 2.1 convolution_bitcast_fusion.3
  403.0 16.6 %eval_jaxpr.5 = (f32[32,32,256]{2,1,0:T(8,128)S(1)}, f32[32,32,256]{2,1,0:T(8,128)}) custom-call(f32[32,32,256]{2,1,0:T(8,128)} %get-tuple-element.277.cur_ref, f32[32,32,256]{2,1,0:T(8,128)} %get-tuple-element.278.prev_ref, f32[32,32,256]{2,1,0:T(8,128)} %get-tuple-element.294.courant_ref, bf16[32,32,256]{2,1,0:T(8,128)(2,1)S(1)} %dynamic-slice_bitcast_fusion.2.snap_ref, ...), custom_call_target="tpu_custom_call" | custom-call | tf_op jit(solution)/shard_map/while/body/eval_jaxpr/pallas_call | solution.py:128
  (214 shorter events, 78.5 us)
Async XLA Ops:
  0.6 4.9 %copy-start = (f32[16,17]{1,0:T(8,128)S(1)}, f32[16,17]{1,0:T(8,128)}, u32[]{:S(2)}) copy-start(f32[16,17]{1,0:T(8,128)} %param.15) | copy-start | bytes 3268
  0.6 5.2 %copy-start.6 = (f32[16,256]{1,0:T(8,128)S(1)}, f32[16,256]{1,0:T(8,128)}, u32[]{:S(2)}) copy-start(f32[16,256]{1,0:T(8,128)} %param.13) | copy-start | bytes 49156
  0.7 5.2 %copy-start.5 = (f32[32,256]{1,0:T(8,128)S(1)}, f32[32,256]{1,0:T(8,128)}, u32[]{:S(2)}) copy-start(f32[32,256]{1,0:T(8,128)} %param.14) | copy-start | bytes 98308
  0.7 4.9 %copy-start.9 = (s32[256]{0:T(256)S(1)}, s32[256]{0:T(256)}, u32[]{:S(2)}) copy-start(s32[256]{0:T(256)} %param.16) | copy-start | bytes 3076
  0.7 4.7 %copy-start.7 = (s32[256,1]{0,1:T(1,128)S(1)}, s32[256,1]{0,1:T(1,128)}, u32[]{:S(2)}) copy-start(s32[256,1]{0,1:T(1,128)} %param.17) | copy-start | bytes 3076
  0.7 4.7 %copy-start.8 = (s32[256]{0:T(256)S(1)}, s32[256]{0:T(256)}, u32[]{:S(2)}) copy-start(s32[256]{0:T(256)} %param.18) | copy-start | bytes 3076
  7.3 24.2 %copy-start.3 = (f32[32,32,256]{2,1,0:T(8,128)S(1)}, f32[32,32,256]{2,1,0:T(8,128)}, u32[]{:S(2)}) copy-start(f32[32,32,256]{2,1,0:T(8,128)} %param.23) | copy-start | bytes 3145732
  7.3 18.7 %all-to-all-start = ((f32[17,128,4]{0,2,1:T(4,128)}), f32[17,128,4]{0,2,1:T(4,128)S(1)}, u32[]{:S(2)}, u32[]{:S(2)}) async-start(f32[17,128,4]{0,2,1:T(4,128)} %bitcast.25), calls=%async_computation | async-start | bytes 524288 | tf_op jit(solution)/shard_map/all_to_all | solution.py:214
  31.6 2.0 copy-start.4
  37.3 17.2 %copy-start.1 = (f32[32,32,256]{2,1,0:T(8,128)S(1)}, f32[32,32,256]{2,1,0:T(8,128)}, u32[]{:S(2)}) copy-start(f32[32,32,256]{2,1,0:T(8,128)} %get-tuple-element.277.cur_ref) | copy-start | bytes 3145732 | tf_op jit(solution)/shard_map/while
  54.5 2.0 copy-start.2
  56.5 2.0 copy-start.4
  62.2 16.7 %copy-start.1 = (f32[32,32,256]{2,1,0:T(8,128)S(1)}, f32[32,32,256]{2,1,0:T(8,128)}, u32[]{:S(2)}) copy-start(f32[32,32,256]{2,1,0:T(8,128)} %get-tuple-element.277.cur_ref) | copy-start | bytes 3145732 | tf_op jit(solution)/shard_map/while
  78.8 2.0 copy-start.2
  80.8 2.0 copy-start.4
  86.5 16.7 %copy-start.1 = (f32[32,32,256]{2,1,0:T(8,128)S(1)}, f32[32,32,256]{2,1,0:T(8,128)}, u32[]{:S(2)}) copy-start(f32[32,32,256]{2,1,0:T(8,128)} %get-tuple-element.277.cur_ref) | copy-start | bytes 3145732 | tf_op jit(solution)/shard_map/while
  103.2 2.0 copy-start.2
  105.1 2.0 copy-start.4
  110.8 16.7 %copy-start.1 = (f32[32,32,256]{2,1,0:T(8,128)S(1)}, f32[32,32,256]{2,1,0:T(8,128)}, u32[]{:S(2)}) copy-start(f32[32,32,256]{2,1,0:T(8,128)} %get-tuple-element.277.cur_ref) | copy-start | bytes 3145732 | tf_op jit(solution)/shard_map/while
  127.5 2.0 copy-start.2
  129.5 2.0 copy-start.4
  135.2 16.7 %copy-start.1 = (f32[32,32,256]{2,1,0:T(8,128)S(1)}, f32[32,32,256]{2,1,0:T(8,128)}, u32[]{:S(2)}) copy-start(f32[32,32,256]{2,1,0:T(8,128)} %get-tuple-element.277.cur_ref) | copy-start | bytes 3145732 | tf_op jit(solution)/shard_map/while
  151.9 2.0 copy-start.2
  153.8 2.0 copy-start.4
  159.5 16.7 %copy-start.1 = (f32[32,32,256]{2,1,0:T(8,128)S(1)}, f32[32,32,256]{2,1,0:T(8,128)}, u32[]{:S(2)}) copy-start(f32[32,32,256]{2,1,0:T(8,128)} %get-tuple-element.277.cur_ref) | copy-start | bytes 3145732 | tf_op jit(solution)/shard_map/while
  176.2 2.0 copy-start.2
  178.2 2.0 copy-start.4
  183.9 16.7 %copy-start.1 = (f32[32,32,256]{2,1,0:T(8,128)S(1)}, f32[32,32,256]{2,1,0:T(8,128)}, u32[]{:S(2)}) copy-start(f32[32,32,256]{2,1,0:T(8,128)} %get-tuple-element.277.cur_ref) | copy-start | bytes 3145732 | tf_op jit(solution)/shard_map/while
  202.5 2.0 copy-start.4
  208.2 16.7 %copy-start.1 = (f32[32,32,256]{2,1,0:T(8,128)S(1)}, f32[32,32,256]{2,1,0:T(8,128)}, u32[]{:S(2)}) copy-start(f32[32,32,256]{2,1,0:T(8,128)} %get-tuple-element.277.cur_ref) | copy-start | bytes 3145732 | tf_op jit(solution)/shard_map/while
  226.8 2.0 copy-start.4
  232.6 16.7 %copy-start.1 = (f32[32,32,256]{2,1,0:T(8,128)S(1)}, f32[32,32,256]{2,1,0:T(8,128)}, u32[]{:S(2)}) copy-start(f32[32,32,256]{2,1,0:T(8,128)} %get-tuple-element.277.cur_ref) | copy-start | bytes 3145732 | tf_op jit(solution)/shard_map/while
  251.2 2.0 copy-start.4
  256.9 16.7 %copy-start.1 = (f32[32,32,256]{2,1,0:T(8,128)S(1)}, f32[32,32,256]{2,1,0:T(8,128)}, u32[]{:S(2)}) copy-start(f32[32,32,256]{2,1,0:T(8,128)} %get-tuple-element.277.cur_ref) | copy-start | bytes 3145732 | tf_op jit(solution)/shard_map/while
  275.5 2.0 copy-start.4
  281.2 16.7 %copy-start.1 = (f32[32,32,256]{2,1,0:T(8,128)S(1)}, f32[32,32,256]{2,1,0:T(8,128)}, u32[]{:S(2)}) copy-start(f32[32,32,256]{2,1,0:T(8,128)} %get-tuple-element.277.cur_ref) | copy-start | bytes 3145732 | tf_op jit(solution)/shard_map/while
  299.9 2.0 copy-start.4
  305.6 16.7 %copy-start.1 = (f32[32,32,256]{2,1,0:T(8,128)S(1)}, f32[32,32,256]{2,1,0:T(8,128)}, u32[]{:S(2)}) copy-start(f32[32,32,256]{2,1,0:T(8,128)} %get-tuple-element.277.cur_ref) | copy-start | bytes 3145732 | tf_op jit(solution)/shard_map/while
  324.2 2.0 copy-start.4
  329.9 16.7 %copy-start.1 = (f32[32,32,256]{2,1,0:T(8,128)S(1)}, f32[32,32,256]{2,1,0:T(8,128)}, u32[]{:S(2)}) copy-start(f32[32,32,256]{2,1,0:T(8,128)} %get-tuple-element.277.cur_ref) | copy-start | bytes 3145732 | tf_op jit(solution)/shard_map/while
  346.6 2.0 copy-start.2
  348.6 2.0 copy-start.4
  354.3 16.7 %copy-start.1 = (f32[32,32,256]{2,1,0:T(8,128)S(1)}, f32[32,32,256]{2,1,0:T(8,128)}, u32[]{:S(2)}) copy-start(f32[32,32,256]{2,1,0:T(8,128)} %get-tuple-element.277.cur_ref) | copy-start | bytes 3145732 | tf_op jit(solution)/shard_map/while
  372.9 2.0 copy-start.4
  378.6 16.7 %copy-start.1 = (f32[32,32,256]{2,1,0:T(8,128)S(1)}, f32[32,32,256]{2,1,0:T(8,128)}, u32[]{:S(2)}) copy-start(f32[32,32,256]{2,1,0:T(8,128)} %get-tuple-element.277.cur_ref) | copy-start | bytes 3145732 | tf_op jit(solution)/shard_map/while
  397.2 2.0 copy-start.4
  402.9 16.7 %copy-start.1 = (f32[32,32,256]{2,1,0:T(8,128)S(1)}, f32[32,32,256]{2,1,0:T(8,128)}, u32[]{:S(2)}) copy-start(f32[32,32,256]{2,1,0:T(8,128)} %get-tuple-element.277.cur_ref) | copy-start | bytes 3145732 | tf_op jit(solution)/shard_map/while
  419.6 2.0 copy-start.2
  (8 other events, 15.7 us)

commit v5 on v4

--- a/solution.py
+++ b/solution.py
@@ -28,8 +28,8 @@
 
 
 def step_kernel(
-    grid_x, grid_y, cur_ref, prev_ref, courant_ref, snap_ref, image_ref, source_ref,
-    next_ref, image_out_ref, ext_x, ext_y, send_sem, recv_sem, local_sem,
+    grid_x, grid_y, cur_ref, prev_ref, courant_ref, snap_ref, image_ref, plane_ref, spread_ref,
+    next_ref, image_out_ref, ext_x, ext_y, source_ref, send_sem, recv_sem, local_sem,
 ):
     me_x = lax.axis_index("gx")
     me_y = lax.axis_index("gy")
@@ -79,6 +79,8 @@
         @pl.when(has[side])
         def _():
             copy_to(side).start()
+
+    source_ref[...] = jnp.dot(plane_ref[...], spread_ref[...], preferred_element_type=jnp.float32)
 
     arriving = (copy_to(1), copy_to(0), copy_to(3), copy_to(2))
     for zone in range(4):
@@ -107,7 +109,11 @@
             above = jnp.where(lane < column - offset, pltpu.roll(center, column - offset, 1), 0.0)
             below = jnp.where(lane >= offset, pltpu.roll(center, offset, 1), 0.0)
             summed = summed + stencil_weights[offset] * (along_x + along_y + (above + below))
-        following = 2.0 * center - prev_ref[x] + courant_ref[x] * (summed + source_ref[x])
+        rows = pl.ds(pl.multiple_of(x * width_y, width_y), width_y)
+        source = (
+            source_ref[rows, pl.ds(0, column)] + source_ref[rows, pl.ds(column, column)]
+        ) + source_ref[rows, pl.ds(2 * column, column)]
+        following = 2.0 * center - prev_ref[x] + courant_ref[x] * (summed + source)
         next_ref[x] = following
         image_out_ref[x] = image_ref[x] + snap_ref[x].astype(jnp.float32) * following
         return carry
@@ -120,7 +126,7 @@
             copy_to(side).wait_send()
 
 
-def fused_step(current, before, courant, snapshot, imaging, source):
+def fused_step(current, before, courant, snapshot, imaging, at_plane, spread):
     grid_x, grid_y = lax.axis_size("gx"), lax.axis_size("gy")
     width_x, width_y, column = current.shape
     field = jax.ShapeDtypeStruct(current.shape, jnp.float32)
@@ -128,11 +134,12 @@
     return pl.pallas_call(
         functools.partial(step_kernel, grid_x, grid_y),
         out_shape=(field, field),
-        in_specs=[vmem] * 6,
+        in_specs=[vmem] * 7,
         out_specs=(vmem, vmem),
         scratch_shapes=[
             pltpu.VMEM((width_x + 2 * HALO, width_y, column), jnp.float32),
             pltpu.VMEM((width_x, width_y + 4 * HALO, column), jnp.float32),
+            pltpu.VMEM((width_x * width_y, 3 * column), jnp.float32),
             pltpu.SemaphoreType.DMA((4,)),
             pltpu.SemaphoreType.DMA((4,)),
             pltpu.SemaphoreType.DMA((2,)),
@@ -140,7 +147,7 @@
         compiler_params=pltpu.CompilerParams(
             collective_id=0, has_side_effects=True, vmem_limit_bytes=48 * 1024 * 1024
         ),
-    )(current, before, courant, snapshot, imaging, source)
+    )(current, before, courant, snapshot, imaging, at_plane, spread)
 
 
 def split_high(value):
@@ -218,24 +225,23 @@
     column = courant.shape[2]
     got_plane = got_cells // column
     got_depth = got_cells % column
-    at_plane = (got_plane[:, None] == jnp.arange(plane, dtype=jnp.int32)[None, :]).astype(jnp.bfloat16)
-    at_plane = jnp.concatenate([at_plane] * 3, axis=0)
+    at_plane = (got_plane[None, :] == jnp.arange(plane, dtype=jnp.int32)[:, None]).astype(jnp.bfloat16)
     at_depth = got_depth[:, None] == jnp.arange(column, dtype=jnp.int32)[None, :]
-    at_depth = jnp.concatenate([at_depth] * 3, axis=0)
     top = split_high(got_values)
     rest = got_values - top
     second = split_high(rest)
-    pieces = jnp.concatenate([top, second, rest - second], axis=1).astype(jnp.bfloat16)
+    pieces = jnp.stack([top, second, rest - second], axis=2).astype(jnp.bfloat16)
 
     def advance(position, carry):
         current, before, imaging = carry
         piece = lax.dynamic_index_in_dim(pieces, position, 0, keepdims=False)
-        spread = jnp.where(at_depth, piece[:, None], jnp.zeros((), jnp.bfloat16))
-        source = lax.dot_general(
-            spread, at_plane, (((0,), (0,)), ((), ())), preferred_element_type=jnp.float32
-        ).T.reshape(current.shape)
+        spread = jnp.where(
+            at_depth[:, None, :], piece[:, :, None], jnp.zeros((), jnp.bfloat16)
+        ).reshape(piece.shape[0], 3 * column)
         snapshot = lax.dynamic_index_in_dim(forward_field, position, 0, keepdims=False)
-        following, imaging = fused_step(current, before, courant, snapshot, imaging, source)
+        following, imaging = fused_step(
+            current, before, courant, snapshot, imaging, at_plane, spread
+        )
         return (following, current, imaging)
 
     current, before, imaging = lax.fori_loop(

time: 425 us -> 403 us (0.948)
  matrix products: 35.2 us -> 2.32 us
  other arithmetic: 5.39 us -> 29.6 us
  local copies, waits for them, and re-layouts: 94.6 us -> 84.4 us
  Pallas kernels: 267 us -> 262 us
    dot_general x16 -> x0, matrix products: 33.5 us -> none  [advance(): lax.dot_general(spread, at_plane, (((0,), (0,)), ((), ())), preferred_ele...]
    transpose x16 -> x0, local copies, waits for them, and re-layouts: 24.9 us -> none  [advance(): source = lax.dot_general(spread, at_plane, (((0,), (0,)), ((), ())), pref...]
    select_n x0 -> x16, local copies, waits for them, and re-layouts: none -> 22.4 us  [advance(): jnp.where(at_depth[:, None, :], piece[:, :, None], jnp.zeros((), jnp.bflo...]
    select_n x0 -> x16, other arithmetic: none -> 15.5 us  [advance(): jnp.where(at_depth[:, None, :], piece[:, :, None], jnp.zeros((), jnp.bflo...]
    convert_element_type x0 -> x16, other arithmetic: none -> 6.74 us  [per_device(): (got_plane[None, :] == jnp.arange(plane, dtype=jnp.int32)[:, None]).astyp...]
    while x144 -> x48, local copies, waits for them, and re-layouts: 43.4 us -> 36.8 us
    pallas_call x16, Pallas kernels: 267 us -> 262 us  [fused_step(): pl.pallas_call(functools.partial(step_kernel, grid_x, grid_y), out_shape=...]
where the time goes in v5:
time: 403 us; the launch traced here: 398 us
  Pallas kernels  262 us (65%)
  local copies, waits for them, and re-layouts  84.4 us (21%)
  other arithmetic  29.6 us (7%)
  starting transfers between devices  10.2 us (3%)
  waiting for transfers between devices  8.53 us (2%)
    pallas_call x16, Pallas kernels, fused_step(): pl.pallas_call(functools.partial(step_kernel, grid_x, grid_y), out_shape=...  262 us
    while x48, local copies, waits for them, and re-layouts  36.8 us
    select_n x16, local copies, waits for them, and re-layouts, advance(): jnp.where(at_depth[:, None, :], piece[:, :, None], jnp.zeros((), jnp.bflo...  22.4 us
    squeeze x16, local copies, waits for them, and re-layouts, advance(): lax.dynamic_index_in_dim(forward_field, position, 0, keepdims=False)  17.3 us
    select_n x16, other arithmetic, advance(): jnp.where(at_depth[:, None, :], piece[:, :, None], jnp.zeros((), jnp.bflo...  15.5 us
    all_to_all x1, starting transfers between devices, per_device(): lax.all_to_all(parcel, ('gx', 'gy'), split_axis=1, concat_axis=1, tiled=T...  10.2 us
    all_to_all x1, waiting for transfers between devices, per_device(): lax.all_to_all(parcel, ('gx', 'gy'), split_axis=1, concat_axis=1, tiled=T...  8.53 us
  transfers between devices with their start and end apart: 1, of which 1 were waited for; matrix products, arithmetic and copies ran while one was open for 0% of the time, Pallas kernels for 0%

profile of v5, /device:TPU:38, one launch (start us, length us, event | category | flops | bytes accessed | tf_op | source)
XLA Modules:
  0.0 398.4 jit_solution(17470410082511459315)
XLA Ops:
  0.7 2.4 copy.59
  3.1 2.3 copy.60
  8.6 1.4 multiply_add_fusion
  10.0 1.4 fusion.5
  11.4 10.2 %all-to-all-start = ((f32[17,128,4]{0,2,1:T(4,128)}), f32[17,128,4]{0,2,1:T(4,128)S(1)}, u32[]{:S(2)}, u32[]{:S(2)}) async-start(f32[17,128,4]{0,2,1:T(4,128)} %bitcast.22), calls=%async_computation | async-start | bytes 524288 | tf_op jit(solution)/shard_map/all_to_all | solution.py:221
  21.6 8.5 %all-to-all-done = f32[17,128,4]{0,2,1:T(4,128)S(1)} async-done(((f32[17,128,4]{0,2,1:T(4,128)}), f32[17,128,4]{0,2,1:T(4,128)S(1)}, u32[]{:S(2)}, u32[]{:S(2)}) %all-to-all-start) | async-done | bytes 34848 | tf_op jit(solution)/shard_map/all_to_all | solution.py:221
  30.4 2.4 fusion.6
  32.9 362.7 %while.18 = (s32[]{:T(128)}, f32[32,32,256]{2,1,0:T(8,128)S(1)}, f32[32,32,256]{2,1,0:T(8,128)}, f32[32,32,256]{2,1,0:T(8,128)}, bf16[16,32,32,256]{3,2,1,0:T(8,...) while((s32[]{:T(128)}, f32[32,32,256]{2,1,0:T(8,128)S(1)}, ...), condition=%wide.region_2.3_spmd.clone, body=%wide.region_1.2_spmd.clone.sunk | while | flops 1572866 | bytes 11023477 | solution.py:247
  33.0 1.2 copy.62.image_ref
  36.3 1.4 copy.39.spread_ref
  38.2 16.9 %eval_jaxpr.5 = (f32[32,32,256]{2,1,0:T(8,128)S(1)}, f32[32,32,256]{2,1,0:T(8,128)}) custom-call(f32[32,32,256]{2,1,0:T(8,128)S(1)} %get-tuple-element.327.cur_ref, f32[32,32,256]{2,1,0:T(8,128)} %get-tuple-element.328.prev_ref, f32[32,32,256]{2,1,0:T(8,128)} %get-tuple-element.342.courant_ref, ...), custom_call_target="tpu_custom_call" | custom-call | tf_op jit(solution)/shard_map/while/body/eval_jaxpr/pallas_call | solution.py:134
  59.5 1.4 copy.39.spread_ref
  61.4 16.3 %eval_jaxpr.5 = (f32[32,32,256]{2,1,0:T(8,128)S(1)}, f32[32,32,256]{2,1,0:T(8,128)}) custom-call(f32[32,32,256]{2,1,0:T(8,128)S(1)} %get-tuple-element.327.cur_ref, f32[32,32,256]{2,1,0:T(8,128)} %get-tuple-element.328.prev_ref, f32[32,32,256]{2,1,0:T(8,128)} %get-tuple-element.342.courant_ref, ...), custom_call_target="tpu_custom_call" | custom-call | tf_op jit(solution)/shard_map/while/body/eval_jaxpr/pallas_call | solution.py:134
  78.8 1.2 copy.62.image_ref
  82.2 1.4 copy.39.spread_ref
  84.0 16.3 %eval_jaxpr.5 = (f32[32,32,256]{2,1,0:T(8,128)S(1)}, f32[32,32,256]{2,1,0:T(8,128)}) custom-call(f32[32,32,256]{2,1,0:T(8,128)S(1)} %get-tuple-element.327.cur_ref, f32[32,32,256]{2,1,0:T(8,128)} %get-tuple-element.328.prev_ref, f32[32,32,256]{2,1,0:T(8,128)} %get-tuple-element.342.courant_ref, ...), custom_call_target="tpu_custom_call" | custom-call | tf_op jit(solution)/shard_map/while/body/eval_jaxpr/pallas_call | solution.py:134
  104.8 1.4 copy.39.spread_ref
  106.6 16.3 %eval_jaxpr.5 = (f32[32,32,256]{2,1,0:T(8,128)S(1)}, f32[32,32,256]{2,1,0:T(8,128)}) custom-call(f32[32,32,256]{2,1,0:T(8,128)S(1)} %get-tuple-element.327.cur_ref, f32[32,32,256]{2,1,0:T(8,128)} %get-tuple-element.328.prev_ref, f32[32,32,256]{2,1,0:T(8,128)} %get-tuple-element.342.courant_ref, ...), custom_call_target="tpu_custom_call" | custom-call | tf_op jit(solution)/shard_map/while/body/eval_jaxpr/pallas_call | solution.py:134
  124.1 1.2 copy.62.image_ref
  127.4 1.4 copy.39.spread_ref
  129.3 16.3 %eval_jaxpr.5 = (f32[32,32,256]{2,1,0:T(8,128)S(1)}, f32[32,32,256]{2,1,0:T(8,128)}) custom-call(f32[32,32,256]{2,1,0:T(8,128)S(1)} %get-tuple-element.327.cur_ref, f32[32,32,256]{2,1,0:T(8,128)} %get-tuple-element.328.prev_ref, f32[32,32,256]{2,1,0:T(8,128)} %get-tuple-element.342.courant_ref, ...), custom_call_target="tpu_custom_call" | custom-call | tf_op jit(solution)/shard_map/while/body/eval_jaxpr/pallas_call | solution.py:134
  146.7 1.2 copy.62.image_ref
  150.1 1.4 copy.39.spread_ref
  151.9 16.3 %eval_jaxpr.5 = (f32[32,32,256]{2,1,0:T(8,128)S(1)}, f32[32,32,256]{2,1,0:T(8,128)}) custom-call(f32[32,32,256]{2,1,0:T(8,128)S(1)} %get-tuple-element.327.cur_ref, f32[32,32,256]{2,1,0:T(8,128)} %get-tuple-element.328.prev_ref, f32[32,32,256]{2,1,0:T(8,128)} %get-tuple-element.342.courant_ref, ...), custom_call_target="tpu_custom_call" | custom-call | tf_op jit(solution)/shard_map/while/body/eval_jaxpr/pallas_call | solution.py:134
  169.3 1.2 copy.62.image_ref
  172.7 1.4 copy.39.spread_ref
  174.5 16.3 %eval_jaxpr.5 = (f32[32,32,256]{2,1,0:T(8,128)S(1)}, f32[32,32,256]{2,1,0:T(8,128)}) custom-call(f32[32,32,256]{2,1,0:T(8,128)S(1)} %get-tuple-element.327.cur_ref, f32[32,32,256]{2,1,0:T(8,128)} %get-tuple-element.328.prev_ref, f32[32,32,256]{2,1,0:T(8,128)} %get-tuple-element.342.courant_ref, ...), custom_call_target="tpu_custom_call" | custom-call | tf_op jit(solution)/shard_map/while/body/eval_jaxpr/pallas_call | solution.py:134
  192.0 1.2 copy.62.image_ref
  195.3 1.4 copy.39.spread_ref
  197.2 16.3 %eval_jaxpr.5 = (f32[32,32,256]{2,1,0:T(8,128)S(1)}, f32[32,32,256]{2,1,0:T(8,128)}) custom-call(f32[32,32,256]{2,1,0:T(8,128)S(1)} %get-tuple-element.327.cur_ref, f32[32,32,256]{2,1,0:T(8,128)} %get-tuple-element.328.prev_ref, f32[32,32,256]{2,1,0:T(8,128)} %get-tuple-element.342.courant_ref, ...), custom_call_target="tpu_custom_call" | custom-call | tf_op jit(solution)/shard_map/while/body/eval_jaxpr/pallas_call | solution.py:134
  214.6 1.2 copy.62.image_ref
  218.0 1.4 copy.39.spread_ref
  219.8 16.3 %eval_jaxpr.5 = (f32[32,32,256]{2,1,0:T(8,128)S(1)}, f32[32,32,256]{2,1,0:T(8,128)}) custom-call(f32[32,32,256]{2,1,0:T(8,128)S(1)} %get-tuple-element.327.cur_ref, f32[32,32,256]{2,1,0:T(8,128)} %get-tuple-element.328.prev_ref, f32[32,32,256]{2,1,0:T(8,128)} %get-tuple-element.342.courant_ref, ...), custom_call_target="tpu_custom_call" | custom-call | tf_op jit(solution)/shard_map/while/body/eval_jaxpr/pallas_call | solution.py:134
  240.6 1.4 copy.39.spread_ref
  242.4 16.3 %eval_jaxpr.5 = (f32[32,32,256]{2,1,0:T(8,128)S(1)}, f32[32,32,256]{2,1,0:T(8,128)}) custom-call(f32[32,32,256]{2,1,0:T(8,128)S(1)} %get-tuple-element.327.cur_ref, f32[32,32,256]{2,1,0:T(8,128)} %get-tuple-element.328.prev_ref, f32[32,32,256]{2,1,0:T(8,128)} %get-tuple-element.342.courant_ref, ...), custom_call_target="tpu_custom_call" | custom-call | tf_op jit(solution)/shard_map/while/body/eval_jaxpr/pallas_call | solution.py:134
  263.2 1.4 copy.39.spread_ref
  265.1 16.3 %eval_jaxpr.5 = (f32[32,32,256]{2,1,0:T(8,128)S(1)}, f32[32,32,256]{2,1,0:T(8,128)}) custom-call(f32[32,32,256]{2,1,0:T(8,128)S(1)} %get-tuple-element.327.cur_ref, f32[32,32,256]{2,1,0:T(8,128)} %get-tuple-element.328.prev_ref, f32[32,32,256]{2,1,0:T(8,128)} %get-tuple-element.342.courant_ref, ...), custom_call_target="tpu_custom_call" | custom-call | tf_op jit(solution)/shard_map/while/body/eval_jaxpr/pallas_call | solution.py:134
  285.9 1.4 copy.39.spread_ref
  287.7 16.3 %eval_jaxpr.5 = (f32[32,32,256]{2,1,0:T(8,128)S(1)}, f32[32,32,256]{2,1,0:T(8,128)}) custom-call(f32[32,32,256]{2,1,0:T(8,128)S(1)} %get-tuple-element.327.cur_ref, f32[32,32,256]{2,1,0:T(8,128)} %get-tuple-element.328.prev_ref, f32[32,32,256]{2,1,0:T(8,128)} %get-tuple-element.342.courant_ref, ...), custom_call_target="tpu_custom_call" | custom-call | tf_op jit(solution)/shard_map/while/body/eval_jaxpr/pallas_call | solution.py:134
  308.5 1.4 copy.39.spread_ref
  310.3 16.3 %eval_jaxpr.5 = (f32[32,32,256]{2,1,0:T(8,128)S(1)}, f32[32,32,256]{2,1,0:T(8,128)}) custom-call(f32[32,32,256]{2,1,0:T(8,128)S(1)} %get-tuple-element.327.cur_ref, f32[32,32,256]{2,1,0:T(8,128)} %get-tuple-element.328.prev_ref, f32[32,32,256]{2,1,0:T(8,128)} %get-tuple-element.342.courant_ref, ...), custom_call_target="tpu_custom_call" | custom-call | tf_op jit(solution)/shard_map/while/body/eval_jaxpr/pallas_call | solution.py:134
  331.1 1.4 copy.39.spread_ref
  333.0 16.3 %eval_jaxpr.5 = (f32[32,32,256]{2,1,0:T(8,128)S(1)}, f32[32,32,256]{2,1,0:T(8,128)}) custom-call(f32[32,32,256]{2,1,0:T(8,128)S(1)} %get-tuple-element.327.cur_ref, f32[32,32,256]{2,1,0:T(8,128)} %get-tuple-element.328.prev_ref, f32[32,32,256]{2,1,0:T(8,128)} %get-tuple-element.342.courant_ref, ...), custom_call_target="tpu_custom_call" | custom-call | tf_op jit(solution)/shard_map/while/body/eval_jaxpr/pallas_call | solution.py:134
  353.8 1.4 copy.39.spread_ref
  355.6 16.3 %eval_jaxpr.5 = (f32[32,32,256]{2,1,0:T(8,128)S(1)}, f32[32,32,256]{2,1,0:T(8,128)}) custom-call(f32[32,32,256]{2,1,0:T(8,128)S(1)} %get-tuple-element.327.cur_ref, f32[32,32,256]{2,1,0:T(8,128)} %get-tuple-element.328.prev_ref, f32[32,32,256]{2,1,0:T(8,128)} %get-tuple-element.342.courant_ref, ...), custom_call_target="tpu_custom_call" | custom-call | tf_op jit(solution)/shard_map/while/body/eval_jaxpr/pallas_call | solution.py:134
  376.4 1.4 copy.39.spread_ref
  378.3 16.3 %eval_jaxpr.5 = (f32[32,32,256]{2,1,0:T(8,128)S(1)}, f32[32,32,256]{2,1,0:T(8,128)}) custom-call(f32[32,32,256]{2,1,0:T(8,128)S(1)} %get-tuple-element.327.cur_ref, f32[32,32,256]{2,1,0:T(8,128)} %get-tuple-element.328.prev_ref, f32[32,32,256]{2,1,0:T(8,128)} %get-tuple-element.342.courant_ref, ...), custom_call_target="tpu_custom_call" | custom-call | tf_op jit(solution)/shard_map/while/body/eval_jaxpr/pallas_call | solution.py:134
  395.7 2.7 copy.63
  (139 shorter events, 72.7 us)
Async XLA Ops:
  0.6 7.0 %copy-start = (f32[16,17]{1,0:T(8,128)S(1)}, f32[16,17]{1,0:T(8,128)}, u32[]{:S(2)}) copy-start(f32[16,17]{1,0:T(8,128)} %param.15) | copy-start | bytes 3268
  0.6 32.3 %copy-start.2 = (f32[32,32,256]{2,1,0:T(8,128)S(1)}, f32[32,32,256]{2,1,0:T(8,128)}, u32[]{:S(2)}) copy-start(f32[32,32,256]{2,1,0:T(8,128)} %param.20) | copy-start | bytes 3145732
  11.4 18.7 %all-to-all-start = ((f32[17,128,4]{0,2,1:T(4,128)}), f32[17,128,4]{0,2,1:T(4,128)S(1)}, u32[]{:S(2)}, u32[]{:S(2)}) async-start(f32[17,128,4]{0,2,1:T(4,128)} %bitcast.22), calls=%async_computation | async-start | bytes 524288 | tf_op jit(solution)/shard_map/all_to_all | solution.py:221
  395.7 2.7 copy-start.1

commit v6 on v2

--- a/solution.py
+++ b/solution.py
@@ -1,7 +1,13 @@
+import functools
+
 import jax
 import jax.numpy as jnp
 from jax import lax
+from jax.experimental import pallas as pl
+from jax.experimental.pallas import tpu as pltpu
 from jax.sharding import PartitionSpec as P
+
+MESH = pl.DeviceIdType.MESH
 
 STEPS = 16
 SHOTS = 16
@@ -19,6 +25,166 @@
     last = lax.slice_in_dim(value, length - HALO, length, axis=dim)
     first = lax.slice_in_dim(value, 0, HALO, axis=dim)
     return lax.ppermute(last, axis, up), lax.ppermute(first, axis, down)
+
+
+def window_kernel(
+    grid_x, grid_y, now_ref, prev_ref, courant_ref, image_ref, plane_ref, snaps_hbm, spreads_hbm,
+    field_ref, before_ref, image_out_ref,
+    ext_x, ext_y, source_ref, spread_buf, snap_buf, send_sem, recv_sem, local_sem,
+):
+    me_x = lax.axis_index("gx")
+    me_y = lax.axis_index("gy")
+    width_x, width_y, column = now_ref.shape
+    steps = snaps_hbm.shape[0]
+    has = (me_x > 0, me_x < grid_x - 1, me_y > 0, me_y < grid_y - 1)
+    peers = ((me_x - 1, me_y), (me_x + 1, me_y), (me_x, me_y - 1), (me_x, me_y + 1))
+    count = sum(flag.astype(jnp.int32) for flag in has)
+    mid_x = pl.ds(HALO, width_x)
+    mid_y = pl.ds(2 * HALO, width_y)
+
+    starts = (
+        pltpu.make_async_copy(now_ref, ext_x.at[0, mid_x], local_sem.at[0]),
+        pltpu.make_async_copy(now_ref, ext_y.at[0, :, mid_y], local_sem.at[1]),
+        pltpu.make_async_copy(prev_ref, ext_x.at[2, mid_x], local_sem.at[2]),
+        pltpu.make_async_copy(image_ref, image_out_ref, local_sem.at[3]),
+    )
+    for copy in starts:
+        copy.start()
+
+    def zones(slot):
+        return (
+            ext_x.at[slot, pl.ds(0, HALO)],
+            ext_x.at[slot, pl.ds(HALO + width_x, HALO)],
+            ext_y.at[slot, :, pl.ds(HALO, HALO)],
+            ext_y.at[slot, :, pl.ds(2 * HALO + width_y, HALO)],
+        )
+
+    for slot in range(3):
+        for zone in range(4):
+            @pl.when(jnp.logical_not(has[zone]))
+            def _():
+                target = zones(slot)[zone]
+                target[...] = jnp.zeros(target.shape, jnp.float32)
+
+    for copy in starts:
+        copy.wait()
+
+    barrier = pltpu.get_barrier_semaphore()
+    for flag, peer in zip(has, peers):
+        @pl.when(flag)
+        def _():
+            pl.semaphore_signal(barrier, inc=1, device_id=peer, device_id_type=MESH)
+    pl.semaphore_wait(barrier, count)
+
+    zone_of = (1, 0, 3, 2)
+    lane = lax.broadcasted_iota(jnp.int32, (width_y, column), 1)
+
+    def copy_to(slot, side):
+        faces = (
+            ext_x.at[slot, pl.ds(HALO, HALO)],
+            ext_x.at[slot, pl.ds(width_x, HALO)],
+            ext_y.at[slot, :, pl.ds(2 * HALO, HALO)],
+            ext_y.at[slot, :, pl.ds(HALO + width_y, HALO)],
+        )
+        zone = zone_of[side]
+        return pltpu.make_async_remote_copy(
+            src_ref=faces[side],
+            dst_ref=zones(slot)[zone],
+            send_sem=send_sem.at[side],
+            recv_sem=recv_sem.at[slot, zone],
+            device_id=peers[side],
+            device_id_type=MESH,
+        )
+
+    def step(position, carry):
+        now = position % 3
+        after = (position + 1) % 3
+        last = (position + 2) % 3
+        spread_in = pltpu.make_async_copy(spreads_hbm.at[position], spread_buf, local_sem.at[4])
+        snap_in = pltpu.make_async_copy(snaps_hbm.at[position], snap_buf, local_sem.at[5])
+        spread_in.start()
+        snap_in.start()
+        for side in range(4):
+            @pl.when(has[side])
+            def _():
+                copy_to(now, side).start()
+
+        spread_in.wait()
+        source_ref[...] = jnp.dot(plane_ref[...], spread_buf[...], preferred_element_type=jnp.float32)
+
+        for zone, side in enumerate(zone_of):
+            @pl.when(has[zone])
+            def _():
+                copy_to(now, side).wait_recv()
+        snap_in.wait()
+
+        def row(x, inner):
+            center = ext_x[now, x + HALO]
+            summed = 3.0 * stencil_weights[0] * center
+            for offset in range(1, 5):
+                along_x = ext_x[now, x + HALO + offset] + ext_x[now, x + HALO - offset]
+                along_y = (
+                    ext_y[now, x, pl.ds(2 * HALO + offset, width_y), :]
+                    + ext_y[now, x, pl.ds(2 * HALO - offset, width_y), :]
+                )
+                above = jnp.where(lane < column - offset, pltpu.roll(center, column - offset, 1), 0.0)
+                below = jnp.where(lane >= offset, pltpu.roll(center, offset, 1), 0.0)
+                summed = summed + stencil_weights[offset] * (along_x + along_y + (above + below))
+            rows = pl.ds(pl.multiple_of(x * width_y, width_y), width_y)
+            source = (
+                source_ref[rows, pl.ds(0, column)] + source_ref[rows, pl.ds(column, column)]
+            ) + source_ref[rows, pl.ds(2 * column, column)]
+            following = 2.0 * center - ext_x[last, x + HALO] + courant_ref[x] * (summed + source)
+            ext_x[after, x + HALO] = following
+            ext_y[after, x, mid_y, :] = following
+            image_out_ref[x] = image_out_ref[x] + snap_buf[x].astype(jnp.float32) * following
+            return inner
+
+        lax.fori_loop(0, width_x, row, 0)
+
+        for side in range(4):
+            @pl.when(has[side])
+            def _():
+                copy_to(now, side).wait_send()
+        return carry
+
+    lax.fori_loop(0, steps, step, 0)
+
+    ends = (
+        pltpu.make_async_copy(ext_x.at[steps % 3, mid_x], field_ref, local_sem.at[0]),
+        pltpu.make_async_copy(ext_x.at[(steps - 1) % 3, mid_x], before_ref, local_sem.at[1]),
+    )
+    for copy in ends:
+        copy.start()
+    for copy in ends:
+        copy.wait()
+
+
+def whole_window(now, before, courant, imaging, at_plane, snaps, spreads):
+    grid_x, grid_y = lax.axis_size("gx"), lax.axis_size("gy")
+    width_x, width_y, column = now.shape
+    field = jax.ShapeDtypeStruct(now.shape, jnp.float32)
+    vmem = pl.BlockSpec(memory_space=pltpu.VMEM)
+    hbm = pl.BlockSpec(memory_space=pl.ANY)
+    return pl.pallas_call(
+        functools.partial(window_kernel, grid_x, grid_y),
+        out_shape=(field, field, field),
+        in_specs=[vmem] * 5 + [hbm, hbm],
+        out_specs=(vmem, vmem, vmem),
+        scratch_shapes=[
+            pltpu.VMEM((3, width_x + 2 * HALO, width_y, column), jnp.float32),
+            pltpu.VMEM((3, width_x, width_y + 4 * HALO, column), jnp.float32),
+            pltpu.VMEM((width_x * width_y, 3 * column), jnp.float32),
+            pltpu.VMEM(spreads.shape[1:], spreads.dtype),
+            pltpu.VMEM(snaps.shape[1:], snaps.dtype),
+            pltpu.SemaphoreType.DMA((4,)),
+            pltpu.SemaphoreType.DMA((3, 4)),
+            pltpu.SemaphoreType.DMA((6,)),
+        ],
+        compiler_params=pltpu.CompilerParams(
+            collective_id=0, has_side_effects=True, vmem_limit_bytes=60 * 1024 * 1024
+        ),
+    )(now, before, courant, imaging, at_plane, snaps, spreads)
 
 
 def split_high(value):
@@ -96,33 +262,18 @@
     column = courant.shape[2]
     got_plane = got_cells // column
     got_depth = got_cells % column
-    at_plane = (got_plane[:, None] == jnp.arange(plane, dtype=jnp.int32)[None, :]).astype(jnp.bfloat16)
-    at_plane = jnp.concatenate([at_plane] * 3, axis=0)
+    at_plane = (got_plane[None, :] == jnp.arange(plane, dtype=jnp.int32)[:, None]).astype(jnp.bfloat16)
     at_depth = got_depth[:, None] == jnp.arange(column, dtype=jnp.int32)[None, :]
-    at_depth = jnp.concatenate([at_depth] * 3, axis=0)
     top = split_high(got_values)
     rest = got_values - top
     second = split_high(rest)
-    pieces = jnp.concatenate([top, second, rest - second], axis=1).astype(jnp.bfloat16)
-
-    def advance(position, carry):
-        current, before, imaging = carry
-        x_lo, x_hi = faces(current, "gx", 0)
-        y_lo, y_hi = faces(current, "gy", 1)
-        piece = lax.dynamic_index_in_dim(pieces, position, 0, keepdims=False)
-        spread = jnp.where(at_depth, piece[:, None], jnp.zeros((), jnp.bfloat16))
-        source = lax.dot_general(
-            spread, at_plane, (((0,), (0,)), ((), ())), preferred_element_type=jnp.float32
-        ).T.reshape(current.shape)
-        following = 2.0 * current - before + courant * (
-            laplace(current, x_lo, x_hi, y_lo, y_hi) + source
-        )
-        snapshot = lax.dynamic_index_in_dim(forward_field, position, 0, keepdims=False)
-        imaging = imaging + snapshot.astype(jnp.float32) * following
-        return (following, current, imaging)
-
-    current, before, imaging = lax.fori_loop(
-        0, STEPS, advance, (adjoint_now, adjoint_prev, image_start)
+    pieces = jnp.stack([top, second, rest - second], axis=2).astype(jnp.bfloat16)
+
+    spreads = jnp.where(
+        at_depth[None, :, None, :], pieces[:, :, :, None], jnp.zeros((), jnp.bfloat16)
+    ).reshape(pieces.shape[0], pieces.shape[1], 3 * column)
+    current, before, imaging = whole_window(
+        adjoint_now, adjoint_prev, courant, image_start, at_plane, forward_field, spreads
     )
     return (current, before, imaging)
 

time: 528 us -> 256 us (0.48)
  starting transfers between devices: 270 us -> 0 us
  Pallas kernels: 0 us -> 182 us
  local copies, waits for them, and re-layouts: 114 us -> 30.8 us
  matrix products: 65.1 us -> 1.61 us
  other arithmetic: 62.6 us -> 18.3 us
  blocking collectives: 0 us -> 18.5 us
  waiting for transfers between devices: 8.7 us -> 0 us
    ppermute x64 -> x0, starting transfers between devices: 259 us -> none  [faces(): return (lax.ppermute(last, axis, up), lax.ppermute(first, axis, down))]
    pallas_call x0 -> x1, Pallas kernels: none -> 182 us  [whole_window(): pl.pallas_call(functools.partial(window_kernel, grid_x, grid_y), out_shap...]
    dot_general x16 -> x0, matrix products: 63.5 us -> none  [advance(): lax.dot_general(spread, at_plane, (((0,), (0,)), ((), ())), preferred_ele...]
    while x288 -> x0, local copies, waits for them, and re-layouts: 59.2 us -> none
    add x16 -> x0, other arithmetic: 57.2 us -> none  [advance(): imaging = imaging + snapshot.astype(jnp.float32) * following]
    transpose x16 -> x0, local copies, waits for them, and re-layouts: 24.9 us -> none  [advance(): source = lax.dot_general(spread, at_plane, (((0,), (0,)), ((), ())), pref...]
    slice x32 -> x0, local copies, waits for them, and re-layouts: 24.2 us -> none  [faces(): first = lax.slice_in_dim(value, 0, HALO, axis=dim)]
    broadcast_in_dim x0 -> x4, local copies, waits for them, and re-layouts: none -> 22.9 us  [per_device(): jnp.where(at_depth[None, :, None, :], pieces[:, :, :, None], jnp.zeros(()...]
  transfers between devices with their start and end apart: 65 -> 0, of which waited for: 1 -> 0; matrix products, arithmetic and copies ran while one was open for 23% -> 0% of each run, Pallas kernels for 0% -> 0%
where the time goes in v6:
time: 256 us; the launch traced here: 252 us
  Pallas kernels  182 us (71%)
  local copies, waits for them, and re-layouts  30.8 us (12%)
  blocking collectives  18.5 us (7%)
  other arithmetic  18.3 us (7%)
    pallas_call x1, Pallas kernels, whole_window(): pl.pallas_call(functools.partial(window_kernel, grid_x, grid_y), out_shap...  182 us
    broadcast_in_dim x4, local copies, waits for them, and re-layouts, per_device(): jnp.where(at_depth[None, :, None, :], pieces[:, :, :, None], jnp.zeros(()...  22.9 us
    all_to_all x1, blocking collectives, per_device(): lax.all_to_all(parcel, ('gx', 'gy'), split_axis=1, concat_axis=1, tiled=T...  18.5 us
    select_n x1, other arithmetic, per_device(): jnp.where(at_depth[None, :, None, :], pieces[:, :, :, None], jnp.zeros(()...  10.7 us
    unnamed x5, local copies, waits for them, and re-layouts  7.62 us

profile of v6, /device:TPU:38, one launch (start us, length us, event | category | flops | bytes accessed | tf_op | source)
XLA Modules:
  0.0 252.0 jit_solution(6267759879762966769)
XLA Ops:
  0.6 0.0 copy-start
  0.6 0.7 copy-done
  1.3 0.9 convolution_bitcast_fusion
  2.3 0.9 convert_reduce_fusion
  3.2 0.7 multiply_add_fusion.1
  3.9 0.7 convert_element_type.30
  4.6 1.4 multiply_add_fusion
  6.0 0.7 fusion.1
  6.7 18.5 %all_to_all.9 = f32[17,128,4]{0,2,1:T(4,128)S(1)} all-to-all(f32[17,128,4]{0,2,1:T(4,128)S(1)} %bitcast.38), channel_id=1, replica_groups=mesh['gx'=16,'gy'=8] {'gx','gy'}, dimensions={1} | all-to-all | bytes 69632 | tf_op jit(solution)/shard_map/all_to_all | solution.py:258
  25.2 0.1 copy.37
  25.3 0.1 rev.3
  25.5 5.6 %broadcast_in_dim.45 = bf16[16,512,3,256]{1,3,2,0:T(8,128)(2,1)} broadcast(bf16[16,512,3]{1,2,0:T(4,128)(2,1)S(1)} %copy.38), dimensions={0,1,2} | broadcast | bytes 12632064 | tf_op jit(solution)/shard_map/jit(_where)/broadcast_in_dim | solution.py:272
  31.0 16.6 %copy.39 = bf16[16,512,768]{2,1,0:T(8,128)(2,1)} copy(bf16[16,512,768]{1,2,0:T(8,128)(2,1)} %bitcast.35) | data formatting | bytes 25165824 | tf_op jit(solution)/shard_map/jit(_where)/broadcast_in_dim | solution.py:272
  47.7 2.4 fusion.2
  50.1 0.1 convert_element_type.33
  50.2 0.1 iota_compare_fusion.1
  50.3 0.1 broadcast_in_dim.42
  50.4 0.6 copy.36
  51.0 1.4 fusion.plane_ref
  52.4 10.7 %broadcast_select_fusion.spreads_hbm = bf16[16,512,768]{2,1,0:T(8,128)(2,1)} fusion(bf16[16,512,768]{2,1,0:T(8,128)(2,1)} %copy.39, pred[512,768]{1,0:T(8,128)(4,1)S(1)} %copy.36), kind=kLoop, calls=%fused_computation | loop fusion | flops 6291456 | bytes 25559040 | tf_op jit(solution)/shard_map/jit(_where)/select_n | solution.py:272
  63.1 182.0 %shard_map.130 = (f32[32,32,256]{2,1,0:T(8,128)}, f32[32,32,256]{2,1,0:T(8,128)}, f32[32,32,256]{2,1,0:T(8,128)}) custom-call(f32[32,32,256]{2,1,0:T(8,128)} %now_ref.1, f32[32,32,256]{2,1,0:T(8,128)} %prev_ref.1, f32[32,32,256]{2,1,0:T(8,128)} %courant_ref.1, f32[32,32,256]{2,1,0:T(8,128)} %image_ref.1, bf16[1024,512]{1,0:T(8,128)(2,1)} %fusion.plane_ref, ...), custom_call_target="tpu_custom_call" | custom-call | tf_op jit(solution)/shard_map/pallas_call | solution.py:169
  245.1 2.3 copy.44
  247.4 2.3 copy.45
  249.7 2.3 copy.46
  (5 shorter events, 0.1 us)
Async XLA Ops:
  0.6 0.7 copy-start

commit v7 on v6

--- a/solution.py
+++ b/solution.py
@@ -140,7 +140,7 @@
             image_out_ref[x] = image_out_ref[x] + snap_buf[x].astype(jnp.float32) * following
             return inner
 
-        lax.fori_loop(0, width_x, row, 0)
+        lax.fori_loop(0, width_x, row, 0, unroll=2)
 
         for side in range(4):
             @pl.when(has[side])
@@ -269,9 +269,13 @@
     second = split_high(rest)
     pieces = jnp.stack([top, second, rest - second], axis=2).astype(jnp.bfloat16)
 
-    spreads = jnp.where(
-        at_depth[None, :, None, :], pieces[:, :, :, None], jnp.zeros((), jnp.bfloat16)
-    ).reshape(pieces.shape[0], pieces.shape[1], 3 * column)
+    spreads = jnp.concatenate(
+        [
+            jnp.where(at_depth[None], pieces[:, :, j, None], jnp.zeros((), jnp.bfloat16))
+            for j in range(3)
+        ],
+        axis=2,
+    )
     current, before, imaging = whole_window(
         adjoint_now, adjoint_prev, courant, image_start, at_plane, forward_field, spreads
     )

time: 256 us -> 233 us (0.910)
  local copies, waits for them, and re-layouts: 30.8 us -> 6.68 us
  other arithmetic: 18.3 us -> 20.9 us
    broadcast_in_dim x4 -> x0, local copies, waits for them, and re-layouts: 22.9 us -> none  [per_device(): jnp.where(at_depth[None, :, None, :], pieces[:, :, :, None], jnp.zeros(()...]
    concatenate x0 -> x1, other arithmetic: none -> 9.36 us  [per_device(): jnp.concatenate([jnp.where(at_depth[None], pieces[:, :, j, None], jnp.zer...]
    select_n x1, other arithmetic: 10.7 us -> 3.89 us  [per_device(): jnp.where(at_depth[None], pieces[:, :, j, None], jnp.zeros((), jnp.bfloat...]
    unnamed x5 -> x7, local copies, waits for them, and re-layouts: 7.62 us -> 6.37 us
where the time goes in v7:
time: 233 us; the launch traced here: 229 us
  Pallas kernels  181 us (78%)
  other arithmetic  20.9 us (9%)
  blocking collectives  18.5 us (8%)
  local copies, waits for them, and re-layouts  6.68 us (3%)
    pallas_call x1, Pallas kernels, whole_window(): pl.pallas_call(functools.partial(window_kernel, grid_x, grid_y), out_shap...  181 us
    all_to_all x1, blocking collectives, per_device(): lax.all_to_all(parcel, ('gx', 'gy'), split_axis=1, concat_axis=1, tiled=T...  18.5 us
    concatenate x1, other arithmetic, per_device(): jnp.concatenate([jnp.where(at_depth[None], pieces[:, :, j, None], jnp.zer...  9.36 us
    unnamed x7, local copies, waits for them, and re-layouts  6.37 us

profile of v7, /device:TPU:38, one launch (start us, length us, event | category | flops | bytes accessed | tf_op | source)
XLA Modules:
  0.0 229.1 jit_solution(12398659379689273352)
XLA Ops:
  0.6 0.0 copy-start
  0.6 0.7 copy-done
  1.3 0.9 convolution_bitcast_fusion
  2.3 0.9 convert_reduce_fusion
  3.2 0.7 multiply_add_fusion.1
  3.9 0.7 convert_element_type.26
  4.6 1.4 multiply_add_fusion
  6.0 0.7 fusion.1
  6.7 18.5 %all_to_all.9 = f32[17,128,4]{0,2,1:T(4,128)S(1)} all-to-all(f32[17,128,4]{0,2,1:T(4,128)S(1)} %bitcast.28), channel_id=1, replica_groups=mesh['gx'=16,'gy'=8] {'gx','gy'}, dimensions={1} | all-to-all | bytes 69632 | tf_op jit(solution)/shard_map/all_to_all | solution.py:258
  25.2 2.4 %fusion.2 = s32[128,4]{1,0:T(8,128)S(1)} fusion(f32[17,128,4]{0,2,1:T(4,128)S(1)} %all_to_all.9), kind=kLoop, calls=%fused_computation.11 | loop fusion | flops 512 | bytes 4096 | tf_op jit(solution)/shard_map/convert_element_type | solution.py:260
  27.6 0.1 convert_element_type.29
  27.7 0.1 iota_compare_fusion.1
  27.9 0.1 copy.23
  28.0 0.1 rev.3
  28.1 1.4 fusion.plane_ref
  29.5 3.9 %broadcast_select_fusion.2 = (bf16[16,512,256]{2,1,0:T(8,128)(2,1)S(1)}, bf16[16,512,256]{2,1,0:T(8,128)(2,1)S(1)}, bf16[16,512,256]{2,1,0:T(8,128)(2,1)S(1)}) fusion(pred[512,256]{1,0:T(8,128)(4,1)S(1)} %iota_compare_fusion.1, bf16[16,512]{1,0:T(8,128)(2,1)S(1)} %get-tuple-element.6, bf16[16,512]{1,0:T(8,128)(2,1)S(1)} %get-tuple-element.7, ...), kind=kLoop, calls=%fused_computation.3 | loop fusion | flops 6291456 | bytes 12763136 | tf_op jit(solution)/shard_map/jit(_where)/select_n | solution.py:274
  33.4 9.4 %pad_maximum_fusion.spreads_hbm = bf16[16,512,768]{2,1,0:T(8,128)(2,1)} fusion(bf16[16,512,256]{2,1,0:T(8,128)(2,1)S(1)} %get-tuple-element.5, bf16[16,512,256]{2,1,0:T(8,128)(2,1)S(1)} %get-tuple-element.4, bf16[16,512,256]{2,1,0:T(8,128)(2,1)S(1)} %get-tuple-element.3), kind=kLoop, calls=%fused_computation | loop fusion | flops 37748736 | bytes 25165824 | tf_op jit(solution)/shard_map/concatenate | solution.py:272
  42.7 180.7 %shard_map.130 = (f32[32,32,256]{2,1,0:T(8,128)}, f32[32,32,256]{2,1,0:T(8,128)}, f32[32,32,256]{2,1,0:T(8,128)}) custom-call(f32[32,32,256]{2,1,0:T(8,128)} %now_ref.1, f32[32,32,256]{2,1,0:T(8,128)} %prev_ref.1, f32[32,32,256]{2,1,0:T(8,128)} %courant_ref.1, f32[32,32,256]{2,1,0:T(8,128)} %image_ref.1, bf16[1024,512]{1,0:T(8,128)(2,1)} %fusion.plane_ref, ...), custom_call_target="tpu_custom_call" | custom-call | tf_op jit(solution)/shard_map/pallas_call | solution.py:169
  223.4 0.0 copy-start.1
  223.4 2.4 %copy.28 = f32[32,32,256]{2,1,0:T(8,128)} copy(f32[32,32,256]{2,1,0:T(8,128)} %get-tuple-element.31) | data formatting | bytes 2097152
  225.8 2.3 %copy.29 = f32[32,32,256]{2,1,0:T(8,128)} copy(f32[32,32,256]{2,1,0:T(8,128)} %get-tuple-element.32) | data formatting | bytes 2097152
  228.1 0.0 copy-done.1
  228.1 1.0 copy.30
  (3 shorter events, 0.1 us)
Async XLA Ops:
  0.6 0.7 copy-start
  223.4 4.7 %copy-start.1 = (f32[32,32,256]{2,1,0:T(8,128)S(1)}, f32[32,32,256]{2,1,0:T(8,128)}, u32[]{:S(2)}) copy-start(f32[32,32,256]{2,1,0:T(8,128)} %get-tuple-element.33) | copy-start | bytes 3145732

commit v8 on v7

--- a/solution.py
+++ b/solution.py
@@ -90,11 +90,42 @@
         return pltpu.make_async_remote_copy(
             src_ref=faces[side],
             dst_ref=zones(slot)[zone],
-            send_sem=send_sem.at[side],
+            send_sem=send_sem.at[slot, side],
             recv_sem=recv_sem.at[slot, zone],
             device_id=peers[side],
             device_id_type=MESH,
         )
+
+    def band(now, after, last, x, low, size):
+        ys = pl.ds(low, size)
+        lane = lax.broadcasted_iota(jnp.int32, (size, column), 1)
+        center = ext_x[now, x + HALO, ys, :]
+        summed = 3.0 * stencil_weights[0] * center
+        for offset in range(1, 5):
+            along_x = ext_x[now, x + HALO + offset, ys, :] + ext_x[now, x + HALO - offset, ys, :]
+            along_y = (
+                ext_y[now, x, pl.ds(2 * HALO + low + offset, size), :]
+                + ext_y[now, x, pl.ds(2 * HALO + low - offset, size), :]
+            )
+            above = jnp.where(lane < column - offset, pltpu.roll(center, column - offset, 1), 0.0)
+            below = jnp.where(lane >= offset, pltpu.roll(center, offset, 1), 0.0)
+            summed = summed + stencil_weights[offset] * (along_x + along_y + (above + below))
+        rows = pl.ds(pl.multiple_of(x * width_y + low, 8), size)
+        source = (
+            source_ref[rows, pl.ds(0, column)] + source_ref[rows, pl.ds(column, column)]
+        ) + source_ref[rows, pl.ds(2 * column, column)]
+        following = 2.0 * center - ext_x[last, x + HALO, ys, :] + courant_ref[x, ys, :] * (
+            summed + source
+        )
+        ext_x[after, x + HALO, ys, :] = following
+        ext_y[after, x, pl.ds(2 * HALO + low, size), :] = following
+        snap = snap_buf[x].astype(jnp.float32)[low : low + size]
+        image_out_ref[x, ys, :] = image_out_ref[x, ys, :] + snap * following
+
+    for side in range(4):
+        @pl.when(has[side])
+        def _():
+            copy_to(0, side).start()
 
     def step(position, carry):
         now = position % 3
@@ -104,10 +135,6 @@
         snap_in = pltpu.make_async_copy(snaps_hbm.at[position], snap_buf, local_sem.at[5])
         spread_in.start()
         snap_in.start()
-        for side in range(4):
-            @pl.when(has[side])
-            def _():
-                copy_to(now, side).start()
 
         spread_in.wait()
         source_ref[...] = jnp.dot(plane_ref[...], spread_buf[...], preferred_element_type=jnp.float32)
@@ -118,29 +145,32 @@
                 copy_to(now, side).wait_recv()
         snap_in.wait()
 
-        def row(x, inner):
-            center = ext_x[now, x + HALO]
-            summed = 3.0 * stencil_weights[0] * center
-            for offset in range(1, 5):
-                along_x = ext_x[now, x + HALO + offset] + ext_x[now, x + HALO - offset]
-                along_y = (
-                    ext_y[now, x, pl.ds(2 * HALO + offset, width_y), :]
-                    + ext_y[now, x, pl.ds(2 * HALO - offset, width_y), :]
-                )
-                above = jnp.where(lane < column - offset, pltpu.roll(center, column - offset, 1), 0.0)
-                below = jnp.where(lane >= offset, pltpu.roll(center, offset, 1), 0.0)
-                summed = summed + stencil_weights[offset] * (along_x + along_y + (above + below))
-            rows = pl.ds(pl.multiple_of(x * width_y, width_y), width_y)
-            source = (
-                source_ref[rows, pl.ds(0, column)] + source_ref[rows, pl.ds(column, column)]
-            ) + source_ref[rows, pl.ds(2 * column, column)]
-            following = 2.0 * center - ext_x[last, x + HALO] + courant_ref[x] * (summed + source)
-            ext_x[after, x + HALO] = following
-            ext_y[after, x, mid_y, :] = following
-            image_out_ref[x] = image_out_ref[x] + snap_buf[x].astype(jnp.float32) * following
+        def edges(x, inner):
+            band(now, after, last, x, 0, 8)
+            band(now, after, last, x, width_y - 8, 8)
             return inner
 
-        lax.fori_loop(0, width_x, row, 0, unroll=2)
+        lax.fori_loop(0, width_x, edges, 0)
+
+        def face_rows(i, inner):
+            x = jnp.where(i < HALO, i, i + width_x - 2 * HALO)
+            band(now, after, last, x, 8, width_y - 16)
+            return inner
+
+        lax.fori_loop(0, 2 * HALO, face_rows, 0)
+
+        @pl.when(position + 1 < steps)
+        def _():
+            for side in range(4):
+                @pl.when(has[side])
+                def _():
+                    copy_to(after, side).start()
+
+        def inside(x, inner):
+            band(now, after, last, x, 8, width_y - 16)
+            return inner
+
+        lax.fori_loop(HALO, width_x - HALO, inside, 0)
 
         for side in range(4):
             @pl.when(has[side])
@@ -177,7 +207,7 @@
             pltpu.VMEM((width_x * width_y, 3 * column), jnp.float32),
             pltpu.VMEM(spreads.shape[1:], spreads.dtype),
             pltpu.VMEM(snaps.shape[1:], snaps.dtype),
-            pltpu.SemaphoreType.DMA((4,)),
+            pltpu.SemaphoreType.DMA((3, 4)),
             pltpu.SemaphoreType.DMA((3, 4)),
             pltpu.SemaphoreType.DMA((6,)),
         ],

time: 233 us -> 270 us (1.16)
  Pallas kernels: 181 us -> 217 us
    pallas_call x1, Pallas kernels: 181 us -> 217 us  [whole_window(): pl.pallas_call(functools.partial(window_kernel, grid_x, grid_y), out_shap...]
where the time goes in v8:
time: 270 us; the launch traced here: 265 us
  Pallas kernels  217 us (80%)
  other arithmetic  20.9 us (8%)
  blocking collectives  18.5 us (7%)
  local copies, waits for them, and re-layouts  6.68 us (2%)
    pallas_call x1, Pallas kernels, whole_window(): pl.pallas_call(functools.partial(window_kernel, grid_x, grid_y), out_shap...  217 us
    all_to_all x1, blocking collectives, per_device(): lax.all_to_all(parcel, ('gx', 'gy'), split_axis=1, concat_axis=1, tiled=T...  18.5 us
    concatenate x1, other arithmetic, per_device(): jnp.concatenate([jnp.where(at_depth[None], pieces[:, :, j, None], jnp.zer...  9.36 us
    unnamed x7, local copies, waits for them, and re-layouts  6.37 us

profile of v8, /device:TPU:38, one launch (start us, length us, event | category | flops | bytes accessed | tf_op | source)
XLA Modules:
  0.0 265.3 jit_solution(14410711492615770830)
XLA Ops:
  0.6 0.0 copy-start
  0.6 0.7 copy-done
  1.3 0.9 convolution_bitcast_fusion
  2.3 0.9 convert_reduce_fusion
  3.2 0.7 multiply_add_fusion.1
  3.9 0.7 convert_element_type.26
  4.6 1.4 multiply_add_fusion
  6.0 0.7 fusion.1
  6.7 18.5 %all_to_all.9 = f32[17,128,4]{0,2,1:T(4,128)S(1)} all-to-all(f32[17,128,4]{0,2,1:T(4,128)S(1)} %bitcast.28), channel_id=1, replica_groups=mesh['gx'=16,'gy'=8] {'gx','gy'}, dimensions={1} | all-to-all | bytes 69632 | tf_op jit(solution)/shard_map/all_to_all | solution.py:288
  25.2 2.4 fusion.2
  27.6 0.1 convert_element_type.29
  27.7 0.1 iota_compare_fusion.1
  27.9 0.1 copy.23
  28.0 0.1 rev.3
  28.1 1.4 fusion.plane_ref
  29.5 3.9 %broadcast_select_fusion.2 = (bf16[16,512,256]{2,1,0:T(8,128)(2,1)S(1)}, bf16[16,512,256]{2,1,0:T(8,128)(2,1)S(1)}, bf16[16,512,256]{2,1,0:T(8,128)(2,1)S(1)}) fusion(pred[512,256]{1,0:T(8,128)(4,1)S(1)} %iota_compare_fusion.1, bf16[16,512]{1,0:T(8,128)(2,1)S(1)} %get-tuple-element.6, bf16[16,512]{1,0:T(8,128)(2,1)S(1)} %get-tuple-element.7, ...), kind=kLoop, calls=%fused_computation.3 | loop fusion | flops 6291456 | bytes 12763136 | tf_op jit(solution)/shard_map/jit(_where)/select_n | solution.py:304
  33.4 9.4 %pad_maximum_fusion.spreads_hbm = bf16[16,512,768]{2,1,0:T(8,128)(2,1)} fusion(bf16[16,512,256]{2,1,0:T(8,128)(2,1)S(1)} %get-tuple-element.5, bf16[16,512,256]{2,1,0:T(8,128)(2,1)S(1)} %get-tuple-element.4, bf16[16,512,256]{2,1,0:T(8,128)(2,1)S(1)} %get-tuple-element.3), kind=kLoop, calls=%fused_computation | loop fusion | flops 37748736 | bytes 25165824 | tf_op jit(solution)/shard_map/concatenate | solution.py:302
  42.7 216.8 %shard_map.130 = (f32[32,32,256]{2,1,0:T(8,128)}, f32[32,32,256]{2,1,0:T(8,128)}, f32[32,32,256]{2,1,0:T(8,128)}) custom-call(f32[32,32,256]{2,1,0:T(8,128)} %now_ref.1, f32[32,32,256]{2,1,0:T(8,128)} %prev_ref.1, f32[32,32,256]{2,1,0:T(8,128)} %courant_ref.1, f32[32,32,256]{2,1,0:T(8,128)} %image_ref.1, bf16[1024,512]{1,0:T(8,128)(2,1)} %fusion.plane_ref, ...), custom_call_target="tpu_custom_call" | custom-call | tf_op jit(solution)/shard_map/pallas_call | solution.py:199
  259.6 0.0 copy-start.1
  259.6 2.4 copy.28
  262.0 2.3 copy.29
  264.3 0.0 copy-done.1
  264.3 1.0 copy.30
  (3 shorter events, 0.1 us)
Async XLA Ops:
  0.6 0.7 copy-start
  259.6 4.7 %copy-start.1 = (f32[32,32,256]{2,1,0:T(8,128)S(1)}, f32[32,32,256]{2,1,0:T(8,128)}, u32[]{:S(2)}) copy-start(f32[32,32,256]{2,1,0:T(8,128)} %get-tuple-element.33) | copy-start | bytes 3145732

commit v9 on v6

--- a/solution.py
+++ b/solution.py
@@ -28,9 +28,9 @@
 
 
 def window_kernel(
-    grid_x, grid_y, now_ref, prev_ref, courant_ref, image_ref, plane_ref, snaps_hbm, spreads_hbm,
-    field_ref, before_ref, image_out_ref,
-    ext_x, ext_y, source_ref, spread_buf, snap_buf, send_sem, recv_sem, local_sem,
+    grid_x, grid_y, now_ref, prev_ref, courant_ref, image_ref, plane_ref, pieces_ref, depth_ref,
+    snaps_hbm, field_ref, before_ref, image_out_ref,
+    ext_x, ext_y, source_ref, weighted, snap_buf, send_sem, recv_sem, local_sem,
 ):
     me_x = lax.axis_index("gx")
     me_y = lax.axis_index("gy")
@@ -100,17 +100,19 @@
         now = position % 3
         after = (position + 1) % 3
         last = (position + 2) % 3
-        spread_in = pltpu.make_async_copy(spreads_hbm.at[position], spread_buf, local_sem.at[4])
         snap_in = pltpu.make_async_copy(snaps_hbm.at[position], snap_buf, local_sem.at[5])
-        spread_in.start()
         snap_in.start()
         for side in range(4):
             @pl.when(has[side])
             def _():
                 copy_to(now, side).start()
 
-        spread_in.wait()
-        source_ref[...] = jnp.dot(plane_ref[...], spread_buf[...], preferred_element_type=jnp.float32)
+        slots = plane_ref.shape[1]
+        for piece in range(3):
+            weighted[:, pl.ds(piece * slots, slots)] = (
+                plane_ref[...] * pieces_ref[position, pl.ds(piece, 1), :]
+            )
+        source_ref[...] = jnp.dot(weighted[...], depth_ref[...], preferred_element_type=jnp.float32)
 
         for zone, side in enumerate(zone_of):
             @pl.when(has[zone])
@@ -131,16 +133,14 @@
                 below = jnp.where(lane >= offset, pltpu.roll(center, offset, 1), 0.0)
                 summed = summed + stencil_weights[offset] * (along_x + along_y + (above + below))
             rows = pl.ds(pl.multiple_of(x * width_y, width_y), width_y)
-            source = (
-                source_ref[rows, pl.ds(0, column)] + source_ref[rows, pl.ds(column, column)]
-            ) + source_ref[rows, pl.ds(2 * column, column)]
+            source = source_ref[rows, :]
             following = 2.0 * center - ext_x[last, x + HALO] + courant_ref[x] * (summed + source)
             ext_x[after, x + HALO] = following
             ext_y[after, x, mid_y, :] = following
             image_out_ref[x] = image_out_ref[x] + snap_buf[x].astype(jnp.float32) * following
             return inner
 
-        lax.fori_loop(0, width_x, row, 0)
+        lax.fori_loop(0, width_x, row, 0, unroll=2)
 
         for side in range(4):
             @pl.when(has[side])
@@ -160,7 +160,7 @@
         copy.wait()
 
 
-def whole_window(now, before, courant, imaging, at_plane, snaps, spreads):
+def whole_window(now, before, courant, imaging, at_plane, pieces, at_depth, snaps):
     grid_x, grid_y = lax.axis_size("gx"), lax.axis_size("gy")
     width_x, width_y, column = now.shape
     field = jax.ShapeDtypeStruct(now.shape, jnp.float32)
@@ -169,13 +169,13 @@
     return pl.pallas_call(
         functools.partial(window_kernel, grid_x, grid_y),
         out_shape=(field, field, field),
-        in_specs=[vmem] * 5 + [hbm, hbm],
+        in_specs=[vmem] * 7 + [hbm],
         out_specs=(vmem, vmem, vmem),
         scratch_shapes=[
             pltpu.VMEM((3, width_x + 2 * HALO, width_y, column), jnp.float32),
             pltpu.VMEM((3, width_x, width_y + 4 * HALO, column), jnp.float32),
-            pltpu.VMEM((width_x * width_y, 3 * column), jnp.float32),
-            pltpu.VMEM(spreads.shape[1:], spreads.dtype),
+            pltpu.VMEM((width_x * width_y, column), jnp.float32),
+            pltpu.VMEM((width_x * width_y, 3 * at_plane.shape[1]), jnp.bfloat16),
             pltpu.VMEM(snaps.shape[1:], snaps.dtype),
             pltpu.SemaphoreType.DMA((4,)),
             pltpu.SemaphoreType.DMA((3, 4)),
@@ -184,7 +184,7 @@
         compiler_params=pltpu.CompilerParams(
             collective_id=0, has_side_effects=True, vmem_limit_bytes=60 * 1024 * 1024
         ),
-    )(now, before, courant, imaging, at_plane, snaps, spreads)
+    )(now, before, courant, imaging, at_plane, pieces, at_depth, snaps)
 
 
 def split_high(value):
@@ -267,13 +267,11 @@
     top = split_high(got_values)
     rest = got_values - top
     second = split_high(rest)
-    pieces = jnp.stack([top, second, rest - second], axis=2).astype(jnp.bfloat16)
-
-    spreads = jnp.where(
-        at_depth[None, :, None, :], pieces[:, :, :, None], jnp.zeros((), jnp.bfloat16)
-    ).reshape(pieces.shape[0], pieces.shape[1], 3 * column)
+    pieces = jnp.stack([top, second, rest - second], axis=1).astype(jnp.bfloat16)
+
+    at_depth = jnp.concatenate([at_depth.astype(jnp.bfloat16)] * 3, axis=0)
     current, before, imaging = whole_window(
-        adjoint_now, adjoint_prev, courant, image_start, at_plane, forward_field, spreads
+        adjoint_now, adjoint_prev, courant, image_start, at_plane, pieces, at_depth, forward_field
     )
     return (current, before, imaging)
 

time: 256 us -> 218 us (0.85)
  local copies, waits for them, and re-layouts: 30.8 us -> 4.8 us
  other arithmetic: 18.3 us -> 9.35 us
  Pallas kernels: 182 us -> 179 us
    broadcast_in_dim x4 -> x0, local copies, waits for them, and re-layouts: 22.9 us -> none  [per_device(): jnp.where(at_depth[None, :, None, :], pieces[:, :, :, None], jnp.zeros(()...]
    select_n x1 -> x0, other arithmetic: 10.7 us -> none  [per_device(): jnp.where(at_depth[None, :, None, :], pieces[:, :, :, None], jnp.zeros(()...]
    unnamed x5 -> x9, local copies, waits for them, and re-layouts: 7.62 us -> 4.41 us
where the time goes in v9:
time: 218 us; the launch traced here: 215 us
  Pallas kernels  179 us (82%)
  blocking collectives  18.5 us (8%)
  other arithmetic  9.35 us (4%)
  local copies, waits for them, and re-layouts  4.8 us (2%)
    pallas_call x1, Pallas kernels, whole_window(): pl.pallas_call(functools.partial(window_kernel, grid_x, grid_y), out_shap...  179 us
    all_to_all x1, blocking collectives, per_device(): lax.all_to_all(parcel, ('gx', 'gy'), split_axis=1, concat_axis=1, tiled=T...  18.5 us
    unnamed x9, local copies, waits for them, and re-layouts  4.41 us

profile of v9, /device:TPU:38, one launch (start us, length us, event | category | flops | bytes accessed | tf_op | source)
XLA Modules:
  0.0 214.5 jit_solution(6393635626378954919)
XLA Ops:
  0.6 0.0 copy-start
  0.6 0.7 convert_element_type.27
  1.3 0.9 convert_reduce_fusion
  2.3 0.7 multiply_add_fusion.1
  3.0 0.0 copy-done
  3.0 0.9 convolution_bitcast_fusion
  3.9 1.4 multiply_add_fusion
  5.3 0.7 fusion.1
  6.0 18.5 %all_to_all.9 = f32[17,128,4]{0,2,1:T(4,128)S(1)} all-to-all(f32[17,128,4]{0,2,1:T(4,128)S(1)} %bitcast.34), channel_id=1, replica_groups=mesh['gx'=16,'gy'=8] {'gx','gy'}, dimensions={1} | all-to-all | bytes 69632 | tf_op jit(solution)/shard_map/all_to_all | solution.py:258
  24.5 0.1 copy.39
  24.6 0.1 rev.3
  24.8 2.4 %fusion.2 = s32[128,4]{1,0:T(8,128)S(1)} fusion(f32[17,128,4]{0,2,1:T(4,128)S(1)} %all_to_all.9), kind=kLoop, calls=%fused_computation.8 | loop fusion | flops 512 | bytes 4096 | tf_op jit(solution)/shard_map/convert_element_type | solution.py:260
  27.2 0.1 convert_element_type.30
  27.4 0.1 iota_compare_fusion.1
  27.5 1.0 add_convert_fusion.depth_ref
  28.5 1.4 fusion.plane_ref
  29.9 0.7 pad_maximum_fusion.pieces_ref
  30.6 179.5 %shard_map.130 = (f32[32,32,256]{2,1,0:T(8,128)}, f32[32,32,256]{2,1,0:T(8,128)}, f32[32,32,256]{2,1,0:T(8,128)}) custom-call(f32[32,32,256]{2,1,0:T(8,128)} %now_ref.1, f32[32,32,256]{2,1,0:T(8,128)} %prev_ref.1, f32[32,32,256]{2,1,0:T(8,128)} %courant_ref.1, f32[32,32,256]{2,1,0:T(8,128)} %image_ref.1, bf16[1024,512]{1,0:T(8,128)(2,1)} %fusion.plane_ref, ...), custom_call_target="tpu_custom_call" | custom-call | tf_op jit(solution)/shard_map/pallas_call | solution.py:169
  210.1 0.0 copy-start.2
  210.1 0.0 copy-start.1
  210.1 2.5 %copy.47 = f32[32,32,256]{2,1,0:T(8,128)} copy(f32[32,32,256]{2,1,0:T(8,128)} %get-tuple-element.28) | data formatting | bytes 2097152
  212.6 0.0 copy-done.2
  212.6 1.0 copy.48
  213.5 0.0 copy-done.1
  213.6 1.0 copy.49
  (6 shorter events, 0.1 us)
Async XLA Ops:
  0.6 2.3 %copy-start = (f32[16,17]{1,0:T(8,128)S(1)}, f32[16,17]{1,0:T(8,128)}, u32[]{:S(2)}) copy-start(f32[16,17]{1,0:T(8,128)} %param.13) | copy-start | bytes 3268
  210.1 2.5 %copy-start.2 = (f32[32,32,256]{2,1,0:T(8,128)S(1)}, f32[32,32,256]{2,1,0:T(8,128)}, u32[]{:S(2)}) copy-start(f32[32,32,256]{2,1,0:T(8,128)} %get-tuple-element.29) | copy-start | bytes 3145732
  210.1 3.4 %copy-start.1 = (f32[32,32,256]{2,1,0:T(8,128)S(1)}, f32[32,32,256]{2,1,0:T(8,128)}, u32[]{:S(2)}) copy-start(f32[32,32,256]{2,1,0:T(8,128)} %get-tuple-element.30) | copy-start | bytes 3145732

commit v10 on v9

--- a/solution.py
+++ b/solution.py
@@ -255,7 +255,10 @@
     )
     payload = jnp.concatenate([residual, trace_cell.astype(jnp.float32)[None, :]], axis=0)
     parcel = jnp.dot(payload, slot_table, precision=lax.Precision.HIGHEST)
-    received = lax.all_to_all(parcel, ("gx", "gy"), split_axis=1, concat_axis=1, tiled=True)
+    parcel = parcel.reshape(parcel.shape[0], grid_x, grid_y, capacity)
+    parcel = lax.all_to_all(parcel, "gy", split_axis=2, concat_axis=2)
+    parcel = lax.all_to_all(parcel, "gx", split_axis=1, concat_axis=1)
+    received = parcel.reshape(parcel.shape[0], slot_count)
     got_values = received[:STEPS][::-1]
     got_cells = received[STEPS].astype(jnp.int32)
     plane = courant.shape[0] * courant.shape[1]

time: 218 us -> 225 us (1.032)
  blocking collectives: 18.5 us -> 23 us
    all_to_all x1 -> x2, blocking collectives: 18.5 us -> 23 us  [the longest x1 13 us: per_device(): parcel = lax.all_to_all(parcel, 'gy', split_axis=2, concat_axis=2)]
    unnamed x9 -> x14, local copies, waits for them, and re-layouts: 4.41 us -> 5.76 us
where the time goes in v10:
time: 225 us; the launch traced here: 221 us
  Pallas kernels  178 us (79%)
  blocking collectives  23 us (10%)
  other arithmetic  10.8 us (5%)
  local copies, waits for them, and re-layouts  6.71 us (3%)
    pallas_call x1, Pallas kernels, whole_window(): pl.pallas_call(functools.partial(window_kernel, grid_x, grid_y), out_shap...  178 us
    all_to_all x1, blocking collectives, per_device(): parcel = lax.all_to_all(parcel, 'gy', split_axis=2, concat_axis=2)  13 us
    all_to_all x1, blocking collectives, per_device(): parcel = lax.all_to_all(parcel, 'gx', split_axis=1, concat_axis=1)  10.1 us
    unnamed x14, local copies, waits for them, and re-layouts  5.76 us

profile of v10, /device:TPU:38, one launch (start us, length us, event | category | flops | bytes accessed | tf_op | source)
XLA Modules:
  0.0 221.4 jit_solution(2624585533525424967)
XLA Ops:
  0.6 0.0 copy-start
  0.6 0.7 convert_element_type.27
  1.3 0.9 convert_reduce_fusion
  2.3 0.7 multiply_add_fusion.1
  3.0 0.0 copy-done
  3.0 0.9 convolution_bitcast_fusion
  3.9 1.4 multiply_add_fusion
  5.3 0.7 fusion.1
  6.1 0.3 reshape.55
  6.4 13.0 %all_to_all.10 = f32[8,1,1088]{2,1,0:T(1,128)S(1)} all-to-all(f32[8,1,1088]{2,1,0:T(1,128)S(1)} %reshape.55), channel_id=1, replica_groups=mesh['gx'=16,'gy'=8] {'gy'}, dimensions={0} | all-to-all | bytes 69632 | tf_op jit(solution)/shard_map/all_to_all | solution.py:259
  19.3 0.5 broadcast.78
  19.9 0.7 reduce.2
  20.6 0.3 reshape.56
  20.9 0.1 copy_bitcast_fusion
  21.0 0.3 reshape.57
  21.3 10.1 %all_to_all.11 = f32[16,1,544]{2,1,0:T(1,128)S(1)} all-to-all(f32[16,1,544]{2,1,0:T(1,128)S(1)} %reshape.57), channel_id=1, replica_groups=mesh['gx'=16,'gy'=8] {'gx'}, dimensions={0} | all-to-all | bytes 69632 | tf_op jit(solution)/shard_map/all_to_all | solution.py:260
  31.4 0.7 reduce.3
  32.1 0.4 reshape.58
  32.5 2.4 %fusion.2 = s32[16,8,4]{2,1,0:T(8,128)S(1)} fusion(f32[17,16,8,4]{0,3,2,1:T(4,128)S(1)} %bitcast.42), kind=kLoop, calls=%fused_computation.8 | loop fusion | flops 512 | bytes 4096 | tf_op jit(solution)/shard_map/convert_element_type | solution.py:263
  34.9 0.1 copy.62
  35.0 0.1 rev.3
  35.2 0.1 convert_element_type.30
  35.3 0.1 iota_compare_fusion.1
  35.5 1.0 add_convert_fusion.depth_ref
  36.4 1.4 fusion.plane_ref
  37.8 0.7 pad_maximum_fusion.pieces_ref
  38.6 178.4 %shard_map.130 = (f32[32,32,256]{2,1,0:T(8,128)}, f32[32,32,256]{2,1,0:T(8,128)}, f32[32,32,256]{2,1,0:T(8,128)}) custom-call(f32[32,32,256]{2,1,0:T(8,128)} %now_ref.1, f32[32,32,256]{2,1,0:T(8,128)} %prev_ref.1, f32[32,32,256]{2,1,0:T(8,128)} %courant_ref.1, f32[32,32,256]{2,1,0:T(8,128)} %image_ref.1, bf16[1024,512]{1,0:T(8,128)(2,1)} %fusion.plane_ref, ...), custom_call_target="tpu_custom_call" | custom-call | tf_op jit(solution)/shard_map/pallas_call | solution.py:169
  217.0 0.0 copy-start.2
  217.0 0.0 copy-start.1
  217.0 2.5 %copy.73 = f32[32,32,256]{2,1,0:T(8,128)} copy(f32[32,32,256]{2,1,0:T(8,128)} %get-tuple-element.28) | data formatting | bytes 2097152
  219.5 0.0 copy-done.2
  219.5 1.0 copy.74
  220.5 0.0 copy-done.1
  220.5 1.0 copy.75
  (7 shorter events, 0.2 us)
Async XLA Ops:
  0.6 2.3 %copy-start = (f32[16,17]{1,0:T(8,128)S(1)}, f32[16,17]{1,0:T(8,128)}, u32[]{:S(2)}) copy-start(f32[16,17]{1,0:T(8,128)} %param.13) | copy-start | bytes 3268
  217.0 2.5 %copy-start.2 = (f32[32,32,256]{2,1,0:T(8,128)S(1)}, f32[32,32,256]{2,1,0:T(8,128)}, u32[]{:S(2)}) copy-start(f32[32,32,256]{2,1,0:T(8,128)} %get-tuple-element.29) | copy-start | bytes 3145732
  217.0 3.4 %copy-start.1 = (f32[32,32,256]{2,1,0:T(8,128)S(1)}, f32[32,32,256]{2,1,0:T(8,128)}, u32[]{:S(2)}) copy-start(f32[32,32,256]{2,1,0:T(8,128)} %get-tuple-element.30) | copy-start | bytes 3145732

commit v11 on v9

--- a/solution.py
+++ b/solution.py
@@ -28,9 +28,9 @@
 
 
 def window_kernel(
-    grid_x, grid_y, now_ref, prev_ref, courant_ref, image_ref, plane_ref, pieces_ref, depth_ref,
+    grid_x, grid_y, now_ref, prev_ref, courant_ref, image_ref, plane_of_ref, pieces_ref, depth_of_ref,
     snaps_hbm, field_ref, before_ref, image_out_ref,
-    ext_x, ext_y, source_ref, weighted, snap_buf, send_sem, recv_sem, local_sem,
+    ext_x, ext_y, source_ref, weighted, snap_buf, plane_ref, depth_ref, send_sem, recv_sem, local_sem,
 ):
     me_x = lax.axis_index("gx")
     me_y = lax.axis_index("gy")
@@ -65,6 +65,16 @@
             def _():
                 target = zones(slot)[zone]
                 target[...] = jnp.zeros(target.shape, jnp.float32)
+
+    plane_ref[...] = jnp.where(
+        lax.broadcasted_iota(jnp.int32, plane_ref.shape, 0) == plane_of_ref[...], 1.0, 0.0
+    ).astype(plane_ref.dtype)
+    slots = plane_ref.shape[1]
+    depth_hot = jnp.where(
+        lax.broadcasted_iota(jnp.int32, (slots, column), 1) == depth_of_ref[...], 1.0, 0.0
+    ).astype(depth_ref.dtype)
+    for piece in range(3):
+        depth_ref[pl.ds(piece * slots, slots), :] = depth_hot
 
     for copy in starts:
         copy.wait()
@@ -160,7 +170,7 @@
         copy.wait()
 
 
-def whole_window(now, before, courant, imaging, at_plane, pieces, at_depth, snaps):
+def whole_window(now, before, courant, imaging, plane_of, pieces, depth_of, snaps):
     grid_x, grid_y = lax.axis_size("gx"), lax.axis_size("gy")
     width_x, width_y, column = now.shape
     field = jax.ShapeDtypeStruct(now.shape, jnp.float32)
@@ -175,8 +185,10 @@
             pltpu.VMEM((3, width_x + 2 * HALO, width_y, column), jnp.float32),
             pltpu.VMEM((3, width_x, width_y + 4 * HALO, column), jnp.float32),
             pltpu.VMEM((width_x * width_y, column), jnp.float32),
-            pltpu.VMEM((width_x * width_y, 3 * at_plane.shape[1]), jnp.bfloat16),
+            pltpu.VMEM((width_x * width_y, 3 * plane_of.shape[1]), jnp.bfloat16),
             pltpu.VMEM(snaps.shape[1:], snaps.dtype),
+            pltpu.VMEM((width_x * width_y, plane_of.shape[1]), jnp.bfloat16),
+            pltpu.VMEM((3 * plane_of.shape[1], column), jnp.bfloat16),
             pltpu.SemaphoreType.DMA((4,)),
             pltpu.SemaphoreType.DMA((3, 4)),
             pltpu.SemaphoreType.DMA((6,)),
@@ -184,7 +196,7 @@
         compiler_params=pltpu.CompilerParams(
             collective_id=0, has_side_effects=True, vmem_limit_bytes=60 * 1024 * 1024
         ),
-    )(now, before, courant, imaging, at_plane, pieces, at_depth, snaps)
+    )(now, before, courant, imaging, plane_of, pieces, depth_of, snaps)
 
 
 def split_high(value):
@@ -262,16 +274,14 @@
     column = courant.shape[2]
     got_plane = got_cells // column
     got_depth = got_cells % column
-    at_plane = (got_plane[None, :] == jnp.arange(plane, dtype=jnp.int32)[:, None]).astype(jnp.bfloat16)
-    at_depth = got_depth[:, None] == jnp.arange(column, dtype=jnp.int32)[None, :]
     top = split_high(got_values)
     rest = got_values - top
     second = split_high(rest)
     pieces = jnp.stack([top, second, rest - second], axis=1).astype(jnp.bfloat16)
 
-    at_depth = jnp.concatenate([at_depth.astype(jnp.bfloat16)] * 3, axis=0)
     current, before, imaging = whole_window(
-        adjoint_now, adjoint_prev, courant, image_start, at_plane, pieces, at_depth, forward_field
+        adjoint_now, adjoint_prev, courant, image_start, got_plane[None, :], pieces,
+        got_depth[:, None], forward_field,
     )
     return (current, before, imaging)
 

time: 218 us -> 220 us (level)
  local copies, waits for them, and re-layouts: 4.8 us -> 7.32 us
    unnamed x9 -> x5, local copies, waits for them, and re-layouts: 4.41 us -> 6.93 us
where the time goes in v11:
time: 220 us; the launch traced here: 217 us
  Pallas kernels  180 us (82%)
  blocking collectives  18.5 us (8%)
  other arithmetic  8.44 us (4%)
  local copies, waits for them, and re-layouts  7.32 us (3%)
    pallas_call x1, Pallas kernels, whole_window(): pl.pallas_call(functools.partial(window_kernel, grid_x, grid_y), out_shap...  180 us
    all_to_all x1, blocking collectives, per_device(): lax.all_to_all(parcel, ('gx', 'gy'), split_axis=1, concat_axis=1, tiled=T...  18.5 us
    unnamed x5, local copies, waits for them, and re-layouts  6.93 us

profile of v11, /device:TPU:38, one launch (start us, length us, event | category | flops | bytes accessed | tf_op | source)
XLA Modules:
  0.0 216.7 jit_solution(1920975816928713779)
XLA Ops:
  0.6 0.0 copy-start
  0.6 0.7 convert_element_type.32
  1.3 0.9 convert_reduce_fusion
  2.3 0.7 multiply_add_fusion.1
  3.0 0.0 copy-done
  3.0 0.9 convolution_bitcast_fusion
  3.9 1.4 multiply_add_fusion
  5.3 0.7 fusion
  6.0 18.5 %all_to_all.9 = f32[17,128,4]{0,2,1:T(4,128)S(1)} all-to-all(f32[17,128,4]{0,2,1:T(4,128)S(1)} %bitcast.37), channel_id=1, replica_groups=mesh['gx'=16,'gy'=8] {'gx','gy'}, dimensions={1} | all-to-all | bytes 69632 | tf_op jit(solution)/shard_map/all_to_all | solution.py:270
  24.5 0.1 copy.51
  24.6 0.1 rev.3
  24.8 2.4 %fusion.17 = s32[128,4]{1,0:T(8,128)S(1)} fusion(f32[17,128,4]{0,2,1:T(4,128)S(1)} %all_to_all.9), kind=kLoop, calls=%fused_computation.35 | loop fusion | flops 512 | bytes 4096 | tf_op jit(solution)/shard_map/convert_element_type | solution.py:272
  27.2 0.1 convert_element_type.35
  27.3 0.6 and_select_fusion.plane_of_ref
  27.9 0.2 slice_convert_fusion
  28.1 0.8 add_select_fusion.depth_of_ref
  28.9 0.7 pad_maximum_fusion.pieces_ref
  29.7 180.1 %shard_map.130 = (f32[32,32,256]{2,1,0:T(8,128)}, f32[32,32,256]{2,1,0:T(8,128)}, f32[32,32,256]{2,1,0:T(8,128)}) custom-call(f32[32,32,256]{2,1,0:T(8,128)} %now_ref.1, f32[32,32,256]{2,1,0:T(8,128)} %prev_ref.1, f32[32,32,256]{2,1,0:T(8,128)} %courant_ref.1, f32[32,32,256]{2,1,0:T(8,128)} %image_ref.1, s32[1,512]{1,0:T(1,128)} %and_select_fusion.plane_of_ref, ...), custom_call_target="tpu_custom_call" | custom-call | tf_op jit(solution)/shard_map/pallas_call | solution.py:179
  209.8 2.3 %copy.62 = f32[32,32,256]{2,1,0:T(8,128)} copy(f32[32,32,256]{2,1,0:T(8,128)} %get-tuple-element.26) | data formatting | bytes 2097152
  212.1 2.3 %copy.63 = f32[32,32,256]{2,1,0:T(8,128)} copy(f32[32,32,256]{2,1,0:T(8,128)} %get-tuple-element.27) | data formatting | bytes 2097152
  214.4 2.3 %copy.64 = f32[32,32,256]{2,1,0:T(8,128)} copy(f32[32,32,256]{2,1,0:T(8,128)} %get-tuple-element.28) | data formatting | bytes 2097152
  (5 shorter events, 0.1 us)
Async XLA Ops:
  0.6 2.3 %copy-start = (f32[16,17]{1,0:T(8,128)S(1)}, f32[16,17]{1,0:T(8,128)}, u32[]{:S(2)}) copy-start(f32[16,17]{1,0:T(8,128)} %param.13) | copy-start | bytes 3268

commit v12 on v9

--- a/solution.py
+++ b/solution.py
@@ -90,11 +90,16 @@
         return pltpu.make_async_remote_copy(
             src_ref=faces[side],
             dst_ref=zones(slot)[zone],
-            send_sem=send_sem.at[side],
+            send_sem=send_sem.at[slot, side],
             recv_sem=recv_sem.at[slot, zone],
             device_id=peers[side],
             device_id_type=MESH,
         )
+
+    for side in (0, 1):
+        @pl.when(has[side])
+        def _():
+            copy_to(0, side).start()
 
     def step(position, carry):
         now = position % 3
@@ -102,7 +107,7 @@
         last = (position + 2) % 3
         snap_in = pltpu.make_async_copy(snaps_hbm.at[position], snap_buf, local_sem.at[5])
         snap_in.start()
-        for side in range(4):
+        for side in (2, 3):
             @pl.when(has[side])
             def _():
                 copy_to(now, side).start()
@@ -140,7 +145,19 @@
             image_out_ref[x] = image_out_ref[x] + snap_buf[x].astype(jnp.float32) * following
             return inner
 
-        lax.fori_loop(0, width_x, row, 0, unroll=2)
+        def face_row(i, inner):
+            return row(jnp.where(i < HALO, i, i + width_x - 2 * HALO), inner)
+
+        lax.fori_loop(0, 2 * HALO, face_row, 0)
+
+        @pl.when(position + 1 < steps)
+        def _():
+            for side in (0, 1):
+                @pl.when(has[side])
+                def _():
+                    copy_to(after, side).start()
+
+        lax.fori_loop(HALO, width_x - HALO, row, 0, unroll=2)
 
         for side in range(4):
             @pl.when(has[side])
@@ -177,7 +194,7 @@
             pltpu.VMEM((width_x * width_y, column), jnp.float32),
             pltpu.VMEM((width_x * width_y, 3 * at_plane.shape[1]), jnp.bfloat16),
             pltpu.VMEM(snaps.shape[1:], snaps.dtype),
-            pltpu.SemaphoreType.DMA((4,)),
+            pltpu.SemaphoreType.DMA((3, 4)),
             pltpu.SemaphoreType.DMA((3, 4)),
             pltpu.SemaphoreType.DMA((6,)),
         ],

time: 218 us -> 216 us (level); the launches traced: 215 us -> 216 us
  no operation moved by 1% of the time
where the time goes in v12:
time: 216 us
  Pallas kernels  181 us (84%)
  blocking collectives  18.5 us (9%)
  other arithmetic  9.35 us (4%)
  local copies, waits for them, and re-layouts  4.8 us (2%)
    pallas_call x1, Pallas kernels, whole_window(): pl.pallas_call(functools.partial(window_kernel, grid_x, grid_y), out_shap...  181 us
    all_to_all x1, blocking collectives, per_device(): lax.all_to_all(parcel, ('gx', 'gy'), split_axis=1, concat_axis=1, tiled=T...  18.5 us
    unnamed x9, local copies, waits for them, and re-layouts  4.41 us

profile of v12, /device:TPU:38, one launch (start us, length us, event | category | flops | bytes accessed | tf_op | source)
XLA Modules:
  0.0 216.1 jit_solution(2170346435335112102)
XLA Ops:
  0.6 0.0 copy-start
  0.6 0.7 convert_element_type.27
  1.3 0.9 convert_reduce_fusion
  2.3 0.7 multiply_add_fusion.1
  3.0 0.0 copy-done
  3.0 0.9 convolution_bitcast_fusion
  3.9 1.4 multiply_add_fusion
  5.3 0.7 fusion.1
  6.0 18.5 %all_to_all.9 = f32[17,128,4]{0,2,1:T(4,128)S(1)} all-to-all(f32[17,128,4]{0,2,1:T(4,128)S(1)} %bitcast.34), channel_id=1, replica_groups=mesh['gx'=16,'gy'=8] {'gx','gy'}, dimensions={1} | all-to-all | bytes 69632 | tf_op jit(solution)/shard_map/all_to_all | solution.py:275
  24.5 0.1 copy.39
  24.6 0.1 rev.3
  24.8 2.4 %fusion.2 = s32[128,4]{1,0:T(8,128)S(1)} fusion(f32[17,128,4]{0,2,1:T(4,128)S(1)} %all_to_all.9), kind=kLoop, calls=%fused_computation.8 | loop fusion | flops 512 | bytes 4096 | tf_op jit(solution)/shard_map/convert_element_type | solution.py:277
  27.2 0.1 convert_element_type.30
  27.4 0.1 iota_compare_fusion.1
  27.5 1.0 add_convert_fusion.depth_ref
  28.5 1.4 fusion.plane_ref
  29.9 0.7 pad_maximum_fusion.pieces_ref
  30.6 181.0 %shard_map.130 = (f32[32,32,256]{2,1,0:T(8,128)}, f32[32,32,256]{2,1,0:T(8,128)}, f32[32,32,256]{2,1,0:T(8,128)}) custom-call(f32[32,32,256]{2,1,0:T(8,128)} %now_ref.1, f32[32,32,256]{2,1,0:T(8,128)} %prev_ref.1, f32[32,32,256]{2,1,0:T(8,128)} %courant_ref.1, f32[32,32,256]{2,1,0:T(8,128)} %image_ref.1, bf16[1024,512]{1,0:T(8,128)(2,1)} %fusion.plane_ref, ...), custom_call_target="tpu_custom_call" | custom-call | tf_op jit(solution)/shard_map/pallas_call | solution.py:186
  211.7 0.0 copy-start.2
  211.7 0.0 copy-start.1
  211.7 2.5 %copy.47 = f32[32,32,256]{2,1,0:T(8,128)} copy(f32[32,32,256]{2,1,0:T(8,128)} %get-tuple-element.28) | data formatting | bytes 2097152
  214.1 0.0 copy-done.2
  214.1 1.0 copy.48
  215.1 0.0 copy-done.1
  215.1 1.0 copy.49
  (6 shorter events, 0.1 us)
Async XLA Ops:
  0.6 2.3 %copy-start = (f32[16,17]{1,0:T(8,128)S(1)}, f32[16,17]{1,0:T(8,128)}, u32[]{:S(2)}) copy-start(f32[16,17]{1,0:T(8,128)} %param.13) | copy-start | bytes 3268
  211.7 2.5 %copy-start.2 = (f32[32,32,256]{2,1,0:T(8,128)S(1)}, f32[32,32,256]{2,1,0:T(8,128)}, u32[]{:S(2)}) copy-start(f32[32,32,256]{2,1,0:T(8,128)} %get-tuple-element.29) | copy-start | bytes 3145732
  211.7 3.4 %copy-start.1 = (f32[32,32,256]{2,1,0:T(8,128)S(1)}, f32[32,32,256]{2,1,0:T(8,128)}, u32[]{:S(2)}) copy-start(f32[32,32,256]{2,1,0:T(8,128)} %get-tuple-element.30) | copy-start | bytes 3145732

commit v13 on v12

--- a/solution.py
+++ b/solution.py
@@ -96,7 +96,7 @@
             device_id_type=MESH,
         )
 
-    for side in (0, 1):
+    for side in range(4):
         @pl.when(has[side])
         def _():
             copy_to(0, side).start()
@@ -107,10 +107,6 @@
         last = (position + 2) % 3
         snap_in = pltpu.make_async_copy(snaps_hbm.at[position], snap_buf, local_sem.at[5])
         snap_in.start()
-        for side in (2, 3):
-            @pl.when(has[side])
-            def _():
-                copy_to(now, side).start()
 
         slots = plane_ref.shape[1]
         for piece in range(3):
@@ -158,6 +154,13 @@
                     copy_to(after, side).start()
 
         lax.fori_loop(HALO, width_x - HALO, row, 0, unroll=2)
+
+        @pl.when(position + 1 < steps)
+        def _():
+            for side in (2, 3):
+                @pl.when(has[side])
+                def _():
+                    copy_to(after, side).start()
 
         for side in range(4):
             @pl.when(has[side])

time: 216 us -> 216 us (level)
  no operation moved by 1% of the time
where the time goes in v13:
time: 216 us
  Pallas kernels  181 us (84%)
  blocking collectives  18.5 us (9%)
  other arithmetic  9.35 us (4%)
  local copies, waits for them, and re-layouts  4.8 us (2%)
    pallas_call x1, Pallas kernels, whole_window(): pl.pallas_call(functools.partial(window_kernel, grid_x, grid_y), out_shap...  181 us
    all_to_all x1, blocking collectives, per_device(): lax.all_to_all(parcel, ('gx', 'gy'), split_axis=1, concat_axis=1, tiled=T...  18.5 us
    unnamed x9, local copies, waits for them, and re-layouts  4.41 us

profile of v13, /device:TPU:38, one launch (start us, length us, event | category | flops | bytes accessed | tf_op | source)
XLA Modules:
  0.0 215.8 jit_solution(9741160233771326088)
XLA Ops:
  0.6 0.0 copy-start
  0.6 0.7 convert_element_type.27
  1.3 0.9 convert_reduce_fusion
  2.3 0.7 multiply_add_fusion.1
  3.0 0.0 copy-done
  3.0 0.9 convolution_bitcast_fusion
  3.9 1.4 multiply_add_fusion
  5.3 0.7 fusion.1
  6.0 18.5 %all_to_all.9 = f32[17,128,4]{0,2,1:T(4,128)S(1)} all-to-all(f32[17,128,4]{0,2,1:T(4,128)S(1)} %bitcast.34), channel_id=1, replica_groups=mesh['gx'=16,'gy'=8] {'gx','gy'}, dimensions={1} | all-to-all | bytes 69632 | tf_op jit(solution)/shard_map/all_to_all | solution.py:278
  24.5 0.1 copy.39
  24.6 0.1 rev.3
  24.8 2.4 %fusion.2 = s32[128,4]{1,0:T(8,128)S(1)} fusion(f32[17,128,4]{0,2,1:T(4,128)S(1)} %all_to_all.9), kind=kLoop, calls=%fused_computation.8 | loop fusion | flops 512 | bytes 4096 | tf_op jit(solution)/shard_map/convert_element_type | solution.py:280
  27.2 0.1 convert_element_type.30
  27.4 0.1 iota_compare_fusion.1
  27.5 1.0 add_convert_fusion.depth_ref
  28.5 1.4 fusion.plane_ref
  29.9 0.7 pad_maximum_fusion.pieces_ref
  30.6 180.7 %shard_map.130 = (f32[32,32,256]{2,1,0:T(8,128)}, f32[32,32,256]{2,1,0:T(8,128)}, f32[32,32,256]{2,1,0:T(8,128)}) custom-call(f32[32,32,256]{2,1,0:T(8,128)} %now_ref.1, f32[32,32,256]{2,1,0:T(8,128)} %prev_ref.1, f32[32,32,256]{2,1,0:T(8,128)} %courant_ref.1, f32[32,32,256]{2,1,0:T(8,128)} %image_ref.1, bf16[1024,512]{1,0:T(8,128)(2,1)} %fusion.plane_ref, ...), custom_call_target="tpu_custom_call" | custom-call | tf_op jit(solution)/shard_map/pallas_call | solution.py:189
  211.3 0.0 copy-start.2
  211.4 0.0 copy-start.1
  211.4 2.5 %copy.47 = f32[32,32,256]{2,1,0:T(8,128)} copy(f32[32,32,256]{2,1,0:T(8,128)} %get-tuple-element.28) | data formatting | bytes 2097152
  213.8 0.0 copy-done.2
  213.8 1.0 copy.48
  214.8 0.0 copy-done.1
  214.8 1.0 copy.49
  (6 shorter events, 0.1 us)
Async XLA Ops:
  0.6 2.3 %copy-start = (f32[16,17]{1,0:T(8,128)S(1)}, f32[16,17]{1,0:T(8,128)}, u32[]{:S(2)}) copy-start(f32[16,17]{1,0:T(8,128)} %param.13) | copy-start | bytes 3268
  211.3 2.5 %copy-start.2 = (f32[32,32,256]{2,1,0:T(8,128)S(1)}, f32[32,32,256]{2,1,0:T(8,128)}, u32[]{:S(2)}) copy-start(f32[32,32,256]{2,1,0:T(8,128)} %get-tuple-element.29) | copy-start | bytes 3145732
  211.4 3.4 %copy-start.1 = (f32[32,32,256]{2,1,0:T(8,128)S(1)}, f32[32,32,256]{2,1,0:T(8,128)}, u32[]{:S(2)}) copy-start(f32[32,32,256]{2,1,0:T(8,128)} %get-tuple-element.30) | copy-start | bytes 3145732
